TPU v7x, 32 devices: a whole 2x2x4 slice. The times are simulated.
32 devices in a mesh: grp: 2 (over x), pix: 8 (over z, y), disp: 2 (over core).
Axes of the slice: x: 2, y: 2, z: 4, core: 2. Of those that a mesh axis runs over, the one named last changes fastest.
Arguments:
- left_image: int32 [128, 1024], P(('grp', 'pix')), parts along dimension 0, may hold values from 0 to 255
- right_image: int32 [128, 1024], P(('grp', 'pix')), parts along dimension 0, may hold values from 0 to 255
- feat_weight: float32 [16, 16], replicated, may hold values from -1.5 to 1.5
- first_weight: bfloat16 [3, 3, 3, 16, 16], replicated, may hold values from -0.3125 to 0.3125
- first_bias: float32 [16], replicated, may hold values from -3 to 3
- second_weight: bfloat16 [3, 3, 3, 16, 16], replicated, may hold values from -0.3125 to 0.3125
- second_bias: float32 [16], replicated, may hold values from -3 to 3
- head_weight: float32 [16], replicated, may hold values from -1.5 to 1.5
- mask_weight: float32 [16, 144], replicated, may hold values from -1.5 to 1.5
- confidence: float32 [128, 1024], P(('grp', 'pix')), parts along dimension 0, may hold values from 0.1 to 1
Outputs:
- coarse_disparity: float32 [32, 256], P(('grp', 'pix')), parts along dimension 0
- disparity_map: float32 [128, 1024], P(('grp', 'pix')), parts along dimension 0
There are 2 independent parts, one for each index of `grp`. A program takes and returns all parts, laid end to end along the dimension named above; an argument that names none is the same for every part. Nothing has to cross between parts.
All inputs are finite; a program needn't handle non-finite values.
Results may differ from a plain program's by a relative error of at most 0.0065.
Values may be sent and summed in bfloat16 or wider, within the bound.
No kernel may reach another device: no remote copies, remote signals or barrier semaphores. Data moves between devices by JAX's collectives and lax.ppermute only.
A program may use at most 64 MiB of HBM per device.

v0:
```python
import jax
import jax.numpy as jnp
from jax import lax
from jax.sharding import PartitionSpec as P

DSP = 128
UP = 4
TV_ITERS = 8


dual_step = 0.175
primal_step = 0.7
tv_bound = 0.3
cost_scale = 8.0
mask_scale = 3.0
highest_prec = lax.Precision.HIGHEST


def with_halo(value, sides, width):
    for axis, dim in sides:
        size, length = (lax.axis_size(axis), value.shape[dim])
        up = [(i, (i + 1) % size) for i in range(size - 1)]
        down = [(j, i) for i, j in up]
        last = lax.slice_in_dim(value, length - width, length, axis=dim)
        leading = lax.slice_in_dim(value, 0, width, axis=dim)
        before = lax.ppermute(last, axis, up)
        after = lax.ppermute(leading, axis, down)
        value = jnp.concatenate([before, value, after], axis=dim)
    return value


def features(image, feat_weight):
    pixels = image.astype(jnp.float32) / 64.0 - 2.0
    row_count = image.shape[0] // UP
    col_count = image.shape[1] // UP
    patches = (
        pixels.reshape(row_count, UP, col_count, UP)
        .transpose(1, 3, 0, 2)
        .reshape(UP * UP, row_count, col_count)
    )
    return jnp.einsum("pc,prw->crw", feat_weight, patches, precision=highest_prec).astype(
        jnp.bfloat16
    )


def cost_volume(left_feat, right_feat, planes):
    col_count = right_feat.shape[2]
    padded = jnp.pad(right_feat, ((0, 0), (0, 0), (DSP, 0)))

    def take_plane(plane):
        return lax.dynamic_slice_in_dim(padded, DSP - plane, col_count, 2)

    shifted = jax.vmap(take_plane)(planes)
    return (left_feat.astype(jnp.float32)[None] * shifted.astype(jnp.float32)).astype(jnp.bfloat16)


def conv_valid(padded, weights):
    plane_total = padded.shape[0] - 2
    channels = padded.shape[1]
    row_count = padded.shape[2] - 2
    col_count = padded.shape[3]
    widened = jnp.pad(padded, ((0, 0), (0, 0), (0, 0), (1, 1)))
    columns = jnp.concatenate(
        [
            widened[:, :, shift_y : shift_y + row_count, shift_x : shift_x + col_count]
            for shift_y in range(3)
            for shift_x in range(3)
        ],
        axis=1,
    )
    folded = weights.reshape(3, 9 * channels, weights.shape[4])
    summed = jnp.einsum(
        "dkrw,ko->dorw", columns[0:plane_total], folded[0], preferred_element_type=jnp.float32
    )
    for shift_d in range(1, 3):
        summed = summed + jnp.einsum(
            "dkrw,ko->dorw",
            columns[shift_d : shift_d + plane_total],
            folded[shift_d],
            preferred_element_type=jnp.float32,
        )
    return summed


def upsample(rimmed, left_feat, mask_weight):
    row_count = rimmed.shape[0] - 2
    col_count = rimmed.shape[1]
    logits = mask_scale * jnp.tanh(
        jnp.einsum(
            "ck,crw->krw", mask_weight, left_feat.astype(jnp.float32), precision=highest_prec
        )
    )
    expo = jnp.exp(logits).reshape(9, UP * UP, row_count, col_count)
    mixing = expo / jnp.sum(expo, 0)
    widened = jnp.pad(rimmed, ((0, 0), (1, 1)))
    neighbours = jnp.stack(
        [
            widened[shift_y : shift_y + row_count, shift_x : shift_x + col_count]
            for shift_y in range(3)
            for shift_x in range(3)
        ]
    )
    subpixel = jnp.sum(mixing * neighbours[:, None], 0)
    return (
        subpixel.reshape(UP, UP, row_count, col_count)
        .transpose(2, 0, 3, 1)
        .reshape(row_count * UP, col_count * UP)
    )


def zero_row(values):
    return jnp.zeros_like(values[:1])


def tv_iter(current, target, fidelity, global_fine, row_total, fetch_below, fetch_above):
    primal, extrap, dual_x, dual_y = current
    below_row = fetch_below(extrap)
    downward = jnp.concatenate([extrap[1:], below_row], 0)
    inside = ((global_fine >= 0) & (global_fine < row_total - 1))[:, None]
    grad_y = jnp.where(inside, downward - extrap, 0.0)
    grad_x = jnp.concatenate([extrap[:, 1:] - extrap[:, :-1], jnp.zeros_like(extrap[:, :1])], 1)
    trial_x = dual_x + dual_step * grad_x
    trial_y = dual_y + dual_step * grad_y
    shrink = jnp.maximum(1.0, jnp.sqrt(trial_x * trial_x + trial_y * trial_y) / tv_bound)
    dual_x = trial_x / shrink
    dual_y = trial_y / shrink
    above_row = fetch_above(dual_y)
    upper = jnp.concatenate([above_row, dual_y[:-1]], 0)
    left_col = jnp.concatenate([jnp.zeros_like(dual_x[:, :1]), dual_x[:, :-1]], 1)
    divergence = dual_x - left_col + dual_y - upper
    updated = (primal + primal_step * divergence + primal_step * fidelity * target) / (
        1.0 + primal_step * fidelity
    )
    return (updated, 2.0 * updated - primal, dual_x, dual_y)


def local(
    left_image,
    right_image,
    feat_weight,
    first_weight,
    first_bias,
    second_weight,
    second_bias,
    head_weight,
    mask_weight,
    confidence,
):
    left_feat = features(left_image, feat_weight)
    right_feat = features(right_image, feat_weight)
    plane_count = DSP // lax.axis_size("disp")
    plane_start = lax.axis_index("disp") * plane_count
    planes = plane_start + jnp.arange(plane_count, dtype=jnp.int32)
    first_shift = first_bias[None, :, None, None]
    volume = cost_volume(left_feat, right_feat, planes)
    padded = with_halo(volume, (("pix", 2), ("disp", 0)), 1)
    hidden = jax.nn.relu(conv_valid(padded, first_weight) + first_shift).astype(jnp.bfloat16)
    padded = with_halo(hidden, (("pix", 2), ("disp", 0)), 1)
    second = jax.nn.relu(conv_valid(padded, second_weight) + second_bias[None, :, None, None])
    raw_score = jnp.einsum("dorw,o->drw", second, head_weight, precision=highest_prec)
    match_cost = cost_scale * jnp.tanh(raw_score)
    expo = jnp.exp(-match_cost)
    plane_frac = planes.astype(jnp.float32) / DSP
    total_weight, total_plane = lax.psum(
        (jnp.sum(expo, 0), jnp.sum(expo * plane_frac[:, None, None], 0)), "disp"
    )
    coarse = total_plane / total_weight
    rimmed = with_halo(coarse, (("pix", 0),), 1)
    initial = upsample(rimmed, left_feat, mask_weight)
    fine_rows = initial.shape[0]
    row_total = fine_rows * lax.axis_size("pix")
    stacked = jnp.stack([initial, confidence])
    extended_fine = with_halo(stacked.astype(jnp.bfloat16), (("pix", 1),), TV_ITERS).astype(
        stacked.dtype
    )
    target = extended_fine[0]
    fidelity = extended_fine[1]
    global_fine = (
        lax.axis_index("pix") * fine_rows
        - TV_ITERS
        + jnp.arange(fine_rows + 2 * TV_ITERS, dtype=jnp.int32)
    )
    margin = TV_ITERS
    current = (target, target, jnp.zeros_like(target), jnp.zeros_like(target))
    for step_index in range(TV_ITERS):
        current = tv_iter(current, target, fidelity, global_fine, row_total, zero_row, zero_row)
    result = current[0][margin : margin + fine_rows]
    return (coarse, result)


def solution(mesh):
    placed = (
        P(("grp", "pix"), None),
        P(("grp", "pix"), None),
        P(),
        P(),
        P(),
        P(),
        P(),
        P(),
        P(),
        P(("grp", "pix"), None),
    )
    return jax.shard_map(
        local,
        mesh=mesh,
        in_specs=placed,
        out_specs=(P(("grp", "pix"), None), P(("grp", "pix"), None)),
        check_vma=False,
    )
```

profile of v0, /device:TPU:0, one launch (start us, length us, event | category | flops | bytes accessed | tf_op | source)
XLA Modules:
  0.0 152.6 jit_solution(6051076933376511878)
XLA Ops:
  1.4 1.1 reshape.79
  2.8 0.9 fusion.26
  4.1 19.3 %gather_fusion = bf16[64,16,2,256]{1,2,3,0:T(2,128)(2,1)} fusion(bf16[16,2,384]{0,1,2:T(2,128)(2,1)S(1)} %pad.48.clone, s32[64]{0:T(128)S(1)} %shift-left_bitcast_fusion), kind=kCustom, calls=%fused_computation | custom fusion | bytes 2097920 | tf_op jit(solution)/shard_map/vmap()/gather | solution.py:51
  23.3 15.6 %copy.87 = bf16[64,16,2,256]{3,1,2,0:T(8,128)(2,1)S(1)} copy(bf16[64,16,2,256]{1,2,3,0:T(2,128)(2,1)} %gather_fusion) | data formatting | bytes 2097152 | tf_op jit(solution)/shard_map/vmap()/gather | solution.py:51
  39.0 1.1 reshape.77
  41.0 4.9 %collective-permute-start = (bf16[64,16,1,256]{3,1,2,0:T(8,128)(2,1)S(1)}, bf16[64,16,1,256]{3,1,2,0:T(8,128)(2,1)S(1)}, u32[]{:S(2)}, u32[]{:S(2)}) collective-permute-start(bf16[64,16,1,256]{3,1,2,0:T(8,128)(2,1)S(1)} %get-tuple-element.41), channel_id=1, source_target_pairs={{0,2},{2,4},{4,6},{6,8},{8,10},{10,12},{12,14},{1,3},{3,5},{5,7},{... | collective-permute-start | bytes 1572872 | tf_op jit(solution)/shard_map/ppermute | solution.py:26
  45.9 1.3 collective-permute-start.1
  47.2 21.1 %collective-permute-done = bf16[64,16,1,256]{3,1,2,0:T(8,128)(2,1)S(1)} collective-permute-done((bf16[64,16,1,256]{3,1,2,0:T(8,128)(2,1)S(1)}, bf16[64,16,1,256]{3,1,2,0:T(8,128)(2,1)S(1)}, u32[]{:S(2)}, u32[]{:S(2)}) %collective-permute-start) | collective-permute-done | bytes 524320 | tf_op jit(solution)/shard_map/ppermute | solution.py:26
  68.3 1.3 collective-permute-start.2
  69.6 1.5 collective-permute-start.3
  71.1 1.6 %collective-permute-done.3 = bf16[1,16,4,256]{3,1,2,0:T(8,128)(2,1)S(1)} collective-permute-done((bf16[1,16,4,256]{3,1,2,0:T(8,128)(2,1)S(1)}, bf16[1,16,4,256]{3,1,2,0:T(8,128)(2,1)S(1)}, u32[]{:S(2)}, u32[]{:S(2)}) %collective-permute-start.3) | collective-permute-done | bytes 32800 | tf_op jit(solution)/shard_map/ppermute | solution.py:27
  76.2 1.4 fusion.8
  77.6 1.4 fusion.10
  79.0 1.4 fusion.20
  80.5 4.4 %collective-permute-start.4 = (bf16[64,16,1,256]{3,1,2,0:T(8,128)(2,1)S(1)}, bf16[64,16,1,256]{3,1,2,0:T(8,128)(2,1)S(1)}, u32[]{:S(2)}, u32[]{:S(2)}) collective-permute-start(bf16[64,16,1,256]{3,1,2,0:T(8,128)(2,1)S(1)} %get-tuple-element.39), channel_id=1, source_target_pairs={{0,2},{2,4},{4,6},{6,8},{8,10},{10,12},{12,14},{1,3},{3,5},{5,7},{... | collective-permute-start | bytes 1572872 | tf_op jit(solution)/shard_map/ppermute | solution.py:26
  84.9 1.3 collective-permute-start.5
  86.6 21.0 %collective-permute-done.4 = bf16[64,16,1,256]{3,1,2,0:T(8,128)(2,1)S(1)} collective-permute-done((bf16[64,16,1,256]{3,1,2,0:T(8,128)(2,1)S(1)}, bf16[64,16,1,256]{3,1,2,0:T(8,128)(2,1)S(1)}, u32[]{:S(2)}, u32[]{:S(2)}) %collective-permute-start.4) | collective-permute-done | bytes 524320 | tf_op jit(solution)/shard_map/ppermute | solution.py:26
  107.6 1.3 collective-permute-start.6
  108.9 1.5 collective-permute-start.7
  110.5 1.6 %collective-permute-done.7 = bf16[1,16,4,256]{3,1,2,0:T(8,128)(2,1)S(1)} collective-permute-done((bf16[1,16,4,256]{3,1,2,0:T(8,128)(2,1)S(1)}, bf16[1,16,4,256]{3,1,2,0:T(8,128)(2,1)S(1)}, u32[]{:S(2)}, u32[]{:S(2)}) %collective-permute-start.7) | collective-permute-done | bytes 32800 | tf_op jit(solution)/shard_map/ppermute | solution.py:27
  115.5 1.4 fusion.2
  116.9 1.4 fusion.4
  118.3 1.4 fusion
  119.7 1.5 %fusion.12 = f32[1,64,2,256]{3,0,2,1:T(1,128)S(1)} fusion(f32[64,2,256,16]{2,3,1,0:T(8,128)S(1)} %fusion, f32[64,2,256,16]{2,3,1,0:T(8,128)S(1)} %fusion.4, f32[64,2,256,16]{2,3,1,0:T(8,128)S(1)} %fusion.2, f32[16]{0:T(128)S(1)} %copy-done.8, f32[16]{0:T(128)S(1)} %copy-done.9), kind=kOutput, calls=%fused_computation.27 | convolution fusion | flops 8388608 | bytes 6422656 | tf_op jit(solution)/shard_map/dorw,o->drw/dot_general | solution.py:160
  121.3 2.5 %all-reduce.37 = (f32[2,256]{1,0:T(2,128)S(1)}, f32[2,256]{1,0:T(2,128)S(1)}) all-reduce(f32[2,256]{1,0:T(2,128)S(1)} %get-tuple-element.3, f32[2,256]{1,0:T(2,128)S(1)} %get-tuple-element.2), channel_id=1, replica_groups=mesh['grp'=2,'pix'=8,'disp'=2] {'disp'}, use_global_device_ids=true, to_apply=%region_1.2 | all-reduce | flops 1024 | bytes 8192 | tf_op jit(solution)/shard_map/psum | solution.py:164
  123.8 4.4 %collective-permute-start.8 = (f32[1,256]{1,0:T(1,128)S(1)}, f32[1,256]{1,0:T(1,128)S(1)}, u32[]{:S(2)}, u32[]{:S(2)}) collective-permute-start(f32[1,256]{1,0:T(1,128)S(1)} %get-tuple-element.52), channel_id=1, source_target_pairs={{0,2},{2,4},{4,6},{6,8},{8,10},{10,12},{12,14},{1,3},{3,5},{5,7},{... | collective-permute-start | bytes 3080 | tf_op jit(solution)/shard_map/ppermute | solution.py:26
  128.2 1.3 collective-permute-start.9
  129.6 6.7 %collective-permute-done.9 = f32[1,256]{1,0:T(1,128)S(1)} collective-permute-done((f32[1,256]{1,0:T(1,128)S(1)}, f32[1,256]{1,0:T(1,128)S(1)}, u32[]{:S(2)}, u32[]{:S(2)}) %collective-permute-start.9) | collective-permute-done | bytes 1056 | tf_op jit(solution)/shard_map/ppermute | solution.py:27
  137.1 0.8 stack_reshape.4
  137.9 4.8 %collective-permute-start.10 = (bf16[2,8,1024]{2,1,0:T(8,128)(2,1)S(1)}, bf16[2,8,1024]{2,1,0:T(8,128)(2,1)S(1)}, u32[]{:S(2)}, u32[]{:S(2)}) collective-permute-start(bf16[2,8,1024]{2,1,0:T(8,128)(2,1)S(1)} %pad_maximum_fusion.8), channel_id=1, source_target_pairs={{0,2},{2,4},{4,6},{6,8},{8,10},{10,12},{12,14},{1,3},{3,5},{5,7},{... | collective-permute-start | bytes 98312 | tf_op jit(solution)/shard_map/ppermute | solution.py:26
  142.7 1.3 collective-permute-start.11
  144.3 4.2 %collective-permute-done.11 = bf16[2,8,1024]{2,1,0:T(8,128)(2,1)S(1)} collective-permute-done((bf16[2,8,1024]{2,1,0:T(8,128)(2,1)S(1)}, bf16[2,8,1024]{2,1,0:T(8,128)(2,1)S(1)}, u32[]{:S(2)}, u32[]{:S(2)}) %collective-permute-start.11) | collective-permute-done | bytes 32800 | tf_op jit(solution)/shard_map/ppermute | solution.py:27
  (125 shorter events, 14.8 us)
Async XLA Ops:
  0.6 85.6 %copy-start = (f32[16,144]{1,0:T(8,128)S(1)}, f32[16,144]{1,0:T(8,128)}, u32[]{:S(2)}) copy-start(f32[16,144]{1,0:T(8,128)} %param.18) | copy-start | bytes 27652
  23.3 15.6 %copy-start.5 = (s32[8,1024]{1,0:T(8,128)S(1)}, s32[8,1024]{1,0:T(8,128)}, u32[]{:S(2)}) copy-start(s32[8,1024]{1,0:T(8,128)} %param.10) | copy-start | bytes 98308
  23.3 17.0 %copy-start.6 = (f32[16,16]{1,0:T(8,128)S(1)}, f32[16,16]{1,0:T(8,128)}, u32[]{:S(2)}) copy-start(f32[16,16]{1,0:T(8,128)} %param.12) | copy-start | bytes 3076
  40.4 30.7 %copy-start.1 = (bf16[3,3,3,16,16]{4,3,2,1,0:T(8,128)(2,1)S(1)}, bf16[3,3,3,16,16]{4,3,2,1,0:T(8,128)(2,1)}, u32[]{:S(2)}) copy-start(bf16[3,3,3,16,16]{4,3,2,1,0:T(8,128)(2,1)} %param.13) | copy-start | bytes 41476
  41.0 27.3 %collective-permute-start = (bf16[64,16,1,256]{3,1,2,0:T(8,128)(2,1)S(1)}, bf16[64,16,1,256]{3,1,2,0:T(8,128)(2,1)S(1)}, u32[]{:S(2)}, u32[]{:S(2)}) collective-permute-start(bf16[64,16,1,256]{3,1,2,0:T(8,128)(2,1)S(1)} %get-tuple-element.41), channel_id=1, source_target_pairs={{0,2},{2,4},{4,6},{6,8},{8,10},{10,12},{12,14},{1,3},{3,5},{5,7},{... | collective-permute-start | bytes 1572872 | tf_op jit(solution)/shard_map/ppermute | solution.py:26
  45.9 22.4 %collective-permute-start.1 = (bf16[64,16,1,256]{3,1,2,0:T(8,128)(2,1)S(1)}, bf16[64,16,1,256]{3,1,2,0:T(8,128)(2,1)S(1)}, u32[]{:S(2)}, u32[]{:S(2)}) collective-permute-start(bf16[64,16,1,256]{3,1,2,0:T(8,128)(2,1)S(1)} %get-tuple-element.42), channel_id=1, source_target_pairs={{2,0},{4,2},{6,4},{8,6},{10,8},{12,10},{14,12},{3,1},{5,3},{7,5},{... | collective-permute-start | bytes 1572872 | tf_op jit(solution)/shard_map/ppermute | solution.py:27
  68.3 2.8 %collective-permute-start.2 = (bf16[1,16,4,256]{3,1,2,0:T(8,128)(2,1)S(1)}, bf16[1,16,4,256]{3,1,2,0:T(8,128)(2,1)S(1)}, u32[]{:S(2)}, u32[]{:S(2)}) collective-permute-start(bf16[1,16,4,256]{3,1,2,0:T(8,128)(2,1)S(1)} %get-tuple-element.37), channel_id=1, source_target_pairs={{0,1},{2,3},{4,5},{6,7},{8,9},{10,11},{12,13},{14,15},{16,17},{18,... | collective-permute-start | bytes 98312 | tf_op jit(solution)/shard_map/ppermute | solution.py:26
  69.6 3.1 %collective-permute-start.3 = (bf16[1,16,4,256]{3,1,2,0:T(8,128)(2,1)S(1)}, bf16[1,16,4,256]{3,1,2,0:T(8,128)(2,1)S(1)}, u32[]{:S(2)}, u32[]{:S(2)}) collective-permute-start(bf16[1,16,4,256]{3,1,2,0:T(8,128)(2,1)S(1)} %get-tuple-element.38), channel_id=1, source_target_pairs={{1,0},{3,2},{5,4},{7,6},{9,8},{11,10},{13,12},{15,14},{17,16},{19,... | collective-permute-start | bytes 98312 | tf_op jit(solution)/shard_map/ppermute | solution.py:27
  77.6 1.4 copy-start.7
  79.0 7.2 %copy-start.2 = (bf16[3,3,3,16,16]{4,3,2,1,0:T(8,128)(2,1)S(1)}, bf16[3,3,3,16,16]{4,3,2,1,0:T(8,128)(2,1)}, u32[]{:S(2)}) copy-start(bf16[3,3,3,16,16]{4,3,2,1,0:T(8,128)(2,1)} %param.15) | copy-start | bytes 41476
  80.5 27.1 %collective-permute-start.4 = (bf16[64,16,1,256]{3,1,2,0:T(8,128)(2,1)S(1)}, bf16[64,16,1,256]{3,1,2,0:T(8,128)(2,1)S(1)}, u32[]{:S(2)}, u32[]{:S(2)}) collective-permute-start(bf16[64,16,1,256]{3,1,2,0:T(8,128)(2,1)S(1)} %get-tuple-element.39), channel_id=1, source_target_pairs={{0,2},{2,4},{4,6},{6,8},{8,10},{10,12},{12,14},{1,3},{3,5},{5,7},{... | collective-permute-start | bytes 1572872 | tf_op jit(solution)/shard_map/ppermute | solution.py:26
  84.9 22.7 %collective-permute-start.5 = (bf16[64,16,1,256]{3,1,2,0:T(8,128)(2,1)S(1)}, bf16[64,16,1,256]{3,1,2,0:T(8,128)(2,1)S(1)}, u32[]{:S(2)}, u32[]{:S(2)}) collective-permute-start(bf16[64,16,1,256]{3,1,2,0:T(8,128)(2,1)S(1)} %get-tuple-element.40), channel_id=1, source_target_pairs={{2,0},{4,2},{6,4},{8,6},{10,8},{12,10},{14,12},{3,1},{5,3},{7,5},{... | collective-permute-start | bytes 1572872 | tf_op jit(solution)/shard_map/ppermute | solution.py:27
  107.6 2.8 %collective-permute-start.6 = (bf16[1,16,4,256]{3,1,2,0:T(8,128)(2,1)S(1)}, bf16[1,16,4,256]{3,1,2,0:T(8,128)(2,1)S(1)}, u32[]{:S(2)}, u32[]{:S(2)}) collective-permute-start(bf16[1,16,4,256]{3,1,2,0:T(8,128)(2,1)S(1)} %get-tuple-element.35), channel_id=1, source_target_pairs={{0,1},{2,3},{4,5},{6,7},{8,9},{10,11},{12,13},{14,15},{16,17},{18,... | collective-permute-start | bytes 98312 | tf_op jit(solution)/shard_map/ppermute | solution.py:26
  108.9 3.1 %collective-permute-start.7 = (bf16[1,16,4,256]{3,1,2,0:T(8,128)(2,1)S(1)}, bf16[1,16,4,256]{3,1,2,0:T(8,128)(2,1)S(1)}, u32[]{:S(2)}, u32[]{:S(2)}) collective-permute-start(bf16[1,16,4,256]{3,1,2,0:T(8,128)(2,1)S(1)} %get-tuple-element.36), channel_id=1, source_target_pairs={{1,0},{3,2},{5,4},{7,6},{9,8},{11,10},{13,12},{15,14},{17,16},{19,... | collective-permute-start | bytes 98312 | tf_op jit(solution)/shard_map/ppermute | solution.py:27
  118.3 1.4 copy-start.8
  118.3 1.4 copy-start.9
  119.7 9.8 %copy-start.4 = (f32[8,1024]{1,0:T(8,128)S(1)}, f32[8,1024]{1,0:T(8,128)}, u32[]{:S(2)}) copy-start(f32[8,1024]{1,0:T(8,128)} %param.19) | copy-start | bytes 98308
  123.8 25.6 %copy-start.3 = (f32[2,256]{1,0:T(2,128)}, f32[2,256]{1,0:T(2,128)S(1)}, u32[]{:S(2)}) copy-start(f32[2,256]{1,0:T(2,128)S(1)} %div.123) | copy-start | bytes 6148
  123.8 5.8 %collective-permute-start.8 = (f32[1,256]{1,0:T(1,128)S(1)}, f32[1,256]{1,0:T(1,128)S(1)}, u32[]{:S(2)}, u32[]{:S(2)}) collective-permute-start(f32[1,256]{1,0:T(1,128)S(1)} %get-tuple-element.52), channel_id=1, source_target_pairs={{0,2},{2,4},{4,6},{6,8},{8,10},{10,12},{12,14},{1,3},{3,5},{5,7},{... | collective-permute-start | bytes 3080 | tf_op jit(solution)/shard_map/ppermute | solution.py:26
  128.2 8.1 %collective-permute-start.9 = (f32[1,256]{1,0:T(1,128)S(1)}, f32[1,256]{1,0:T(1,128)S(1)}, u32[]{:S(2)}, u32[]{:S(2)}) collective-permute-start(f32[1,256]{1,0:T(1,128)S(1)} %get-tuple-element.53), channel_id=1, source_target_pairs={{2,0},{4,2},{6,4},{8,6},{10,8},{12,10},{14,12},{3,1},{5,3},{7,5},{... | collective-permute-start | bytes 3080 | tf_op jit(solution)/shard_map/ppermute | solution.py:27
  137.9 6.4 %collective-permute-start.10 = (bf16[2,8,1024]{2,1,0:T(8,128)(2,1)S(1)}, bf16[2,8,1024]{2,1,0:T(8,128)(2,1)S(1)}, u32[]{:S(2)}, u32[]{:S(2)}) collective-permute-start(bf16[2,8,1024]{2,1,0:T(8,128)(2,1)S(1)} %pad_maximum_fusion.8), channel_id=1, source_target_pairs={{0,2},{2,4},{4,6},{6,8},{8,10},{10,12},{12,14},{1,3},{3,5},{5,7},{... | collective-permute-start | bytes 98312 | tf_op jit(solution)/shard_map/ppermute | solution.py:26
  142.7 5.8 %collective-permute-start.11 = (bf16[2,8,1024]{2,1,0:T(8,128)(2,1)S(1)}, bf16[2,8,1024]{2,1,0:T(8,128)(2,1)S(1)}, u32[]{:S(2)}, u32[]{:S(2)}) collective-permute-start(bf16[2,8,1024]{2,1,0:T(8,128)(2,1)S(1)} %pad_maximum_fusion.8), channel_id=1, source_target_pairs={{2,0},{4,2},{6,4},{8,6},{10,8},{12,10},{14,12},{3,1},{5,3},{7,5},{... | collective-permute-start | bytes 98312 | tf_op jit(solution)/shard_map/ppermute | solution.py:27
where the time goes:
time: 153 us
  waiting for transfers between devices  56.4 us (37%)
  local copies, waits for them, and re-layouts  45.8 us (30%)
  starting transfers between devices  29.3 us (19%)
  matrix products  11.4 us (7%)
  other arithmetic  5.9 us (4%)
  blocking collectives  2.46 us (2%)
    ppermute x6, waiting for transfers between devices, with_halo(): before = lax.ppermute(last, axis, up)  42.3 us
    gather x2, local copies, waits for them, and re-layouts, take_plane(): return lax.dynamic_slice_in_dim(padded, DSP - plane, col_count, 2)  34.9 us
    ppermute x6, starting transfers between devices, with_halo(): before = lax.ppermute(last, axis, up)  21.1 us
    ppermute x6, waiting for transfers between devices, with_halo(): after = lax.ppermute(leading, axis, down)  14.1 us
    ppermute x6, starting transfers between devices, with_halo(): after = lax.ppermute(leading, axis, down)  8.15 us
    unnamed x43, local copies, waits for them, and re-layouts  5.54 us
    dot_general x4, matrix products, conv_valid(): jnp.einsum('dkrw,ko->dorw', columns[shift_d:shift_d + plane_total], folde...  5.53 us
  transfers between devices with their start and end apart: 12, of which 7 were waited for; matrix products, arithmetic and copies ran while one was open for 0% of the time, Pallas kernels for 0%

commit v1 on v0

v1 whole, which is shorter than its diff:
```python
import functools

import jax
import jax.numpy as jnp
from jax import lax
from jax.experimental import pallas as pl
from jax.experimental.pallas import tpu as pltpu
from jax.sharding import PartitionSpec as P

DSP = 128
UP = 4
TV_ITERS = 8
CH = 16

dual_step = 0.175
primal_step = 0.7
tv_bound = 0.3
cost_scale = 8.0
mask_scale = 3.0
f32 = jnp.float32
bf16 = jnp.bfloat16


def involution(pairs, pix_size, disp_size):
    perm = []
    used = set()
    for i, j in pairs:
        used |= {i, j}
        for d in range(disp_size):
            perm += [(i * disp_size + d, j * disp_size + d), (j * disp_size + d, i * disp_size + d)]
    for i in range(pix_size):
        if i not in used:
            perm += [(i * disp_size + d, i * disp_size + (d ^ 1)) for d in range(disp_size)]
    return sorted(perm)


def split3(values):
    high = values.astype(bf16)
    rest = values - high.astype(f32)
    middle = rest.astype(bf16)
    low = (rest - middle.astype(f32)).astype(bf16)
    return high, middle, low


def split3_outside(values):
    high = lax.reduce_precision(values, 8, 7)
    middle = lax.reduce_precision(values - high, 8, 7)
    low = values - high - middle
    return high.astype(bf16), middle.astype(bf16), low.astype(bf16)


def phase_matrix(transposed):
    rows = lax.broadcasted_iota(jnp.int32, (256, 256), 0)
    cols = lax.broadcasted_iota(jnp.int32, (256, 256), 1)
    if transposed:
        rows, cols = cols, rows
    return jnp.where(rows == UP * (cols % 64) + cols // 64, 1.0, 0.0).astype(bf16)


def deinterleave(values):
    perm = phase_matrix(False)
    chunks = values.shape[1] // 256
    pieces = [
        jnp.dot(values[:, 256 * j : 256 * j + 256], perm, preferred_element_type=f32)
        for j in range(chunks)
    ]
    lane = lax.broadcasted_iota(jnp.int32, (values.shape[0], 128), 1)
    phases = []
    for b in range(UP):
        tiles = []
        for t in range(chunks // 2):
            first = pieces[2 * t][:, 128 * (b // 2) : 128 * (b // 2) + 128]
            second = pieces[2 * t + 1][:, 128 * (b // 2) : 128 * (b // 2) + 128]
            if b % 2 == 0:
                second = pltpu.roll(second, 64, 1)
            else:
                first = pltpu.roll(first, 64, 1)
            tiles.append(jnp.where(lane < 64, first, second))
        phases.append(jnp.concatenate(tiles, 1))
    return phases


def interleave(phases):
    perm = phase_matrix(True)
    rows = phases[0].shape[0]
    lane = lax.broadcasted_iota(jnp.int32, (rows, 128), 1)
    outs = []
    for t in range(phases[0].shape[1] // 128):
        tiles = [phase[:, 128 * t : 128 * t + 128] for phase in phases]
        rolled = [pltpu.roll(tile, 64, 1) for tile in tiles]
        for half in range(2):
            if half == 0:
                packed = [jnp.where(lane < 64, tiles[b], rolled[b + 1]) for b in (0, 2)]
            else:
                packed = [jnp.where(lane < 64, rolled[b], tiles[b + 1]) for b in (0, 2)]
            packed = jnp.concatenate(packed, 1)
            total = None
            for part in split3(packed)[::-1]:
                moved = jnp.dot(part, perm, preferred_element_type=f32)
                total = moved if total is None else total + moved
            outs.append(total)
    return jnp.concatenate(outs, 1)


def shift_right(values):
    lane = lax.broadcasted_iota(jnp.int32, (values.shape[0], 128), 1)
    rolled = [pltpu.roll(values[:, t : t + 128], 1, 1) for t in range(0, values.shape[1], 128)]
    zero = jnp.zeros_like(rolled[0])
    return jnp.concatenate(
        [jnp.where(lane == 0, prev, now) for prev, now in zip([zero] + rolled[:-1], rolled)], 1
    )


def shift_left(values):
    lane = lax.broadcasted_iota(jnp.int32, (values.shape[0], 128), 1)
    rolled = [pltpu.roll(values[:, t : t + 128], 127, 1) for t in range(0, values.shape[1], 128)]
    zero = jnp.zeros_like(rolled[0])
    return jnp.concatenate(
        [jnp.where(lane == 127, after, now) for now, after in zip(rolled, rolled[1:] + [zero])], 1
    )


def join_taps(taps):
    size = taps.shape[0] // 3
    return (
        taps[size : 2 * size] + shift_right(taps[:size]) + shift_left(taps[2 * size :])
    )


def score_kernel(
    place_ref,
    own_ref,
    pair_ref,
    other_ref,
    project_ref,
    first_ref,
    second_ref,
    const_ref,
    total_ref,
    left_ref,
    conf_ref,
    volume,
    hidden,
    folded,
    *,
    pix_size,
    disp_size,
):
    pix = place_ref[0]
    disp = place_ref[1]
    plane_count = DSP // disp_size
    even = pix % 2 == 0
    pair = pair_ref[...].astype(f32)
    other = other_ref[...].astype(f32)
    above = jnp.where(even, other, pair)
    below = jnp.where(even, pair, other)
    gathered = jnp.concatenate([above, own_ref[...].astype(f32), below], 0).astype(bf16)
    phases = deinterleave(gathered)
    fine = own_ref.shape[0] // 3
    conf_ref[...] = jnp.concatenate(
        [
            jnp.concatenate([phase[s * 3 * fine + 2 * fine : s * 3 * fine + 3 * fine] for s in range(3)], 0)
            for phase in phases
        ],
        1,
    )
    stacked = jnp.concatenate(
        [
            phase[s * 3 * fine + img * fine : s * 3 * fine + (img + 1) * fine]
            for phase in phases
            for img in range(2)
            for s in range(3)
        ],
        0,
    )
    patches = (stacked / 64.0 - 2.0).astype(bf16)
    feats3 = jnp.dot(project_ref[...], patches, preferred_element_type=f32)
    size = feats3.shape[0] // 3
    feats = (feats3[2 * size :] + feats3[size : 2 * size]) + feats3[:size]
    half = size // 2
    rows = half // CH
    local_rows = rows // 3
    row_id = lax.broadcasted_iota(jnp.int32, (half, 1), 0) // CH + (pix - 1) * local_rows
    inside = (row_id >= 0) & (row_id < pix_size * local_rows)
    left = jnp.where(inside, feats[:half], 0.0).astype(bf16)
    right = feats[half:].astype(bf16).astype(f32)
    left_ref[...] = left
    left_wide = left.astype(f32)
    lane = lax.broadcasted_iota(jnp.int32, right.shape, 1)
    start = disp * plane_count

    def shifted_by(amount):
        return jnp.where(lane >= amount, pltpu.roll(right, amount, 1), 0.0)

    @pl.when(disp == 0)
    def _():
        volume[0:2] = jnp.zeros(volume[0:2].shape, bf16)

    @pl.when(disp > 0)
    def _():
        volume[0] = (left_wide * shifted_by(start - 2)).astype(bf16)
        volume[1] = (left_wide * shifted_by(start - 1)).astype(bf16)

    def fill(plane, moved):
        volume[plane] = (left_wide * moved).astype(bf16)
        return shift_right(moved)

    lax.fori_loop(2, plane_count + 4, fill, shifted_by(start), unroll=2)

    @pl.when(disp == disp_size - 1)
    def _():
        volume[plane_count + 2 :] = jnp.zeros((2,) + volume.shape[1:], bf16)

    hid_rows = hidden.shape[1]
    first = first_ref[...]
    first_bias = const_ref[0]

    def conv_first(t, carry):
        for window in range(hid_rows // 32):
            block = volume[pl.ds(2 * t, 4), 32 * window : 32 * window + 64, :]
            block = block.reshape(256, block.shape[2])
            taps = jnp.dot(first, block, preferred_element_type=f32)
            made = jnp.maximum(join_taps(taps) + first_bias, 0.0).astype(bf16)
            hidden[pl.ds(2 * t, 2), 32 * window : 32 * window + 32, :] = made.reshape(
                2, 32, made.shape[1]
            )
        return carry

    lax.fori_loop(0, plane_count // 2 + 1, conv_first, 0)

    @pl.when(disp == 0)
    def _():
        hidden[0] = jnp.zeros(hidden.shape[1:], bf16)

    @pl.when(disp == disp_size - 1)
    def _():
        hidden[plane_count + 1] = jnp.zeros(hidden.shape[1:], bf16)

    @pl.when(pix == 0)
    def _():
        hidden[:, :CH] = jnp.zeros((hidden.shape[0], CH, hidden.shape[2]), bf16)

    @pl.when(pix == pix_size - 1)
    def _():
        hidden[:, hid_rows - CH :] = jnp.zeros((hidden.shape[0], CH, hidden.shape[2]), bf16)

    second = second_ref[...]
    second_bias = const_ref[1]
    head = const_ref[2]

    def conv_second(t, carry):
        block = hidden[pl.ds(2 * t, 4)]
        block = block.reshape(256, block.shape[2])
        taps = jnp.dot(second, block, preferred_element_type=f32)
        made = jnp.maximum(join_taps(taps) + second_bias, 0.0) * head
        folded[t] = jnp.sum(made.reshape(8, 8, made.shape[1]), 0)
        return carry

    lax.fori_loop(0, plane_count // 2, conv_second, 0)

    score = folded[...]
    cols = score.shape[2]
    score = score.reshape(-1, cols)
    row8 = lax.broadcasted_iota(jnp.int32, (8, cols), 0)
    weight = jnp.zeros((8, cols), f32)
    moment = jnp.zeros((8, cols), f32)
    for t in range(plane_count // 2):
        part = score[8 * t : 8 * t + 8]
        raw = part + pltpu.roll(part, 4, 0)
        expo = jnp.exp(-cost_scale * jnp.tanh(raw))
        plane = (start + 2 * t + (row8 // 2) % 2).astype(f32) / DSP
        weight = weight + expo
        moment = moment + expo * plane
    weight = weight + pltpu.roll(weight, 2, 0)
    moment = moment + pltpu.roll(moment, 2, 0)
    total_ref[...] = jnp.where(row8 % 4 < 2, weight, moment)


def mixing_kernel(left_ref, mask_ref, mix_ref):
    cols = left_ref.shape[1]
    kinds = mask_ref.shape[0] // 3
    for r in range(mix_ref.shape[0]):
        logits3 = jnp.dot(
            mask_ref[...], left_ref[CH * r : CH * r + CH, :], preferred_element_type=f32
        )
        logits = (logits3[2 * kinds :] + logits3[kinds : 2 * kinds]) + logits3[:kinds]
        expo = jnp.exp(mask_scale * jnp.tanh(logits)).reshape(9, UP * UP, cols)
        mix_ref[r] = (expo / jnp.sum(expo, 0)).reshape(kinds, cols)


def refine_kernel(
    place_ref,
    own_ref,
    pair_ref,
    other_ref,
    far_ref,
    swapped_ref,
    mix_ref,
    conf_ref,
    out_ref,
    *,
    pix_size,
):
    pix = place_ref[0]
    disp = place_ref[1]
    local = own_ref.shape[0]
    even = pix % 2 == 0
    above = jnp.where(even, other_ref[...], pair_ref[...])
    below = jnp.where(even, pair_ref[...], other_ref[...])
    first_core = disp == 0
    far_below = jnp.where(first_core, far_ref[...], swapped_ref[...])
    far_above = jnp.where(first_core, swapped_ref[...], far_ref[...])
    window = [far_above[local - 1 :], above, own_ref[...], below, far_below[:1]]
    window = jnp.concatenate(window, 0)
    cols = window.shape[1]
    row_id = lax.broadcasted_iota(jnp.int32, window.shape, 0) + pix * local - local - 1
    window = jnp.where((row_id >= 0) & (row_id < pix_size * local), window, 0.0)
    moved = [shift_right(window), window, shift_left(window)]
    phases = [[] for _ in range(UP)]
    for r in range(3 * local):
        mixing = mix_ref[r]
        total = jnp.zeros((UP * UP, cols), f32)
        for k in range(9):
            near = moved[k % 3][r + k // 3 : r + k // 3 + 1]
            total = total + mixing[UP * UP * k : UP * UP * k + UP * UP] * near
        for b in range(UP):
            phases[b].append(total[UP * b : UP * b + UP])
    target = jnp.concatenate([jnp.concatenate(phase, 0) for phase in phases], 1)
    fine = target.shape[0]
    out_rows = fine // 3
    conf = conf_ref[...]
    lanes = target.shape[1]
    global_row = lax.broadcasted_iota(jnp.int32, target.shape, 0) + (pix - 1) * out_rows
    row_inside = (global_row >= 0) & (global_row < pix_size * out_rows - 1)
    local_row = lax.broadcasted_iota(jnp.int32, target.shape, 0)
    lane_id = lax.broadcasted_iota(jnp.int32, target.shape, 1)
    last_col = lane_id == lanes - 1
    anchor = primal_step * conf * target
    scale = 1.0 + primal_step * conf
    primal = target
    extrap = target
    dual_x = jnp.zeros_like(target)
    dual_y = jnp.zeros_like(target)
    for _ in range(TV_ITERS):
        downward = pltpu.roll(extrap, fine - 1, 0)
        grad_y = jnp.where(row_inside, downward - extrap, 0.0)
        ahead = jnp.concatenate([extrap[:, cols:], shift_left(extrap[:, :cols])], 1)
        grad_x = jnp.where(last_col, 0.0, ahead - extrap)
        trial_x = dual_x + dual_step * grad_x
        trial_y = dual_y + dual_step * grad_y
        shrink = jnp.maximum(1.0, jnp.sqrt(trial_x * trial_x + trial_y * trial_y) / tv_bound)
        dual_x = trial_x / shrink
        dual_y = trial_y / shrink
        upper = jnp.where(local_row == 0, 0.0, pltpu.roll(dual_y, 1, 0))
        behind = jnp.concatenate([shift_right(dual_x[:, lanes - cols :]), dual_x[:, : lanes - cols]], 1)
        divergence = dual_x - behind + dual_y - upper
        updated = (primal + primal_step * divergence + anchor) / scale
        extrap = 2.0 * updated - primal
        primal = updated
    kept = primal[out_rows : 2 * out_rows]
    out_ref[...] = interleave([kept[:, b * cols : (b + 1) * cols] for b in range(UP)])


def toeplitz(weights, order):
    moved = weights.transpose(2, 4, 0, 1, 3)
    blocks = jnp.stack(
        [
            jnp.pad(moved, ((0, 0), (0, 0), (do, 1 - do), (ro, 1 - ro), (0, 0)))
            for do in range(2)
            for ro in range(2)
        ],
        1,
    )
    taps, outs = (blocks.shape[0], blocks.shape[2])
    blocks = blocks.reshape(taps, 4, outs, -1)
    if order == "channel_last":
        return blocks.reshape(taps * 4 * outs, -1)
    return blocks.transpose(0, 2, 1, 3).reshape(taps * 4 * outs, -1)


def local(
    left_image,
    right_image,
    feat_weight,
    first_weight,
    first_bias,
    second_weight,
    second_bias,
    head_weight,
    mask_weight,
    confidence,
    *,
    pix_size,
    disp_size,
):
    both = ("pix", "disp")
    fine, width = left_image.shape
    cols = width // UP
    local_rows = fine // UP
    plane_count = DSP // disp_size
    place = jnp.stack([lax.axis_index("pix"), lax.axis_index("disp")]).astype(jnp.int32)
    swap = [(d, d ^ 1) for d in range(disp_size)]
    pairs = involution([(i, i + 1) for i in range(0, pix_size - 1, 2)], pix_size, disp_size)
    others = involution([(i, i + 1) for i in range(1, pix_size - 1, 2)], pix_size, disp_size)
    far = []
    taken = set()
    for i in range(pix_size - 2):
        a, b = (i * disp_size, (i + 2) * disp_size + 1)
        far += [(a, b), (b, a)]
        taken |= {a, b}
    spare = [n for n in range(pix_size * disp_size) if n not in taken]
    for a, b in zip(spare[::2], spare[1::2]):
        far += [(a, b), (b, a)]
    far = sorted(far)

    packed = jnp.concatenate(
        [left_image.astype(bf16), right_image.astype(bf16), confidence.astype(bf16)], 0
    )
    from_pair = lax.ppermute(packed, both, pairs)
    from_other = lax.ppermute(packed, both, others)

    first = toeplitz(first_weight, "channel_last")
    second = toeplitz(second_weight, "channel_first")
    groups = 6 * local_rows
    spread = jnp.einsum(
        "abc,gh->gcbha", feat_weight.reshape(UP, UP, CH), jnp.eye(groups, dtype=f32),
        precision=lax.Precision.HIGHEST,
    ).reshape(groups * CH, UP * groups * UP)
    project = jnp.concatenate(split3_outside(spread), 0)
    by_phase = mask_weight.reshape(CH, 9, UP, UP).transpose(1, 3, 2, 0).reshape(-1, CH)
    mask3 = jnp.concatenate(split3_outside(by_phase), 0)
    consts = jnp.stack(
        [jnp.tile(first_bias, 4), jnp.repeat(second_bias, 4), jnp.repeat(head_weight, 4)]
    )
    consts = jnp.broadcast_to(consts[:, :, None], consts.shape + (cols,))

    vmem = pl.BlockSpec(memory_space=pltpu.VMEM)
    smem = pl.BlockSpec(memory_space=pltpu.SMEM)
    total, left, conf = pl.pallas_call(
        functools.partial(score_kernel, pix_size=pix_size, disp_size=disp_size),
        out_shape=(
            jax.ShapeDtypeStruct((8, cols), f32),
            jax.ShapeDtypeStruct((3 * local_rows * CH, cols), bf16),
            jax.ShapeDtypeStruct((3 * fine, width), f32),
        ),
        in_specs=[smem] + [vmem] * 7,
        out_specs=(vmem, vmem, vmem),
        scratch_shapes=[
            pltpu.VMEM((plane_count + 4, 3 * local_rows * CH, cols), bf16),
            pltpu.VMEM((plane_count + 2, (local_rows + 2) * CH, cols), bf16),
            pltpu.VMEM((plane_count // 2, 8, cols), f32),
        ],
        compiler_params=pltpu.CompilerParams(vmem_limit_bytes=32 * 2**20),
        name="score",
    )(place, packed, from_pair, from_other, project, first, second, consts)

    total = total[:4]
    summed = total + lax.ppermute(total, "disp", swap)
    coarse = summed[local_rows:] / summed[:local_rows]
    far_rows = lax.ppermute(coarse, both, far)
    from_pair = lax.ppermute(coarse, both, pairs)
    from_other = lax.ppermute(coarse, both, others)
    swapped = lax.ppermute(far_rows, "disp", swap)
    mix = pl.pallas_call(
        mixing_kernel,
        out_shape=jax.ShapeDtypeStruct((3 * local_rows, mask_weight.shape[1], cols), f32),
        in_specs=[vmem, vmem],
        out_specs=vmem,
        name="mixing",
    )(left, mask3)
    refined = pl.pallas_call(
        functools.partial(refine_kernel, pix_size=pix_size),
        out_shape=jax.ShapeDtypeStruct((fine, width), f32),
        in_specs=[smem] + [vmem] * 7,
        out_specs=vmem,
        name="refine",
    )(place, coarse, from_pair, from_other, far_rows, swapped, mix, conf)
    return (coarse, refined)


def solution(mesh):
    rows = P(("grp", "pix"), None)
    placed = (rows, rows, P(), P(), P(), P(), P(), P(), P(), rows)
    return jax.shard_map(
        functools.partial(local, pix_size=mesh.shape["pix"], disp_size=mesh.shape["disp"]),
        mesh=mesh,
        in_specs=placed,
        out_specs=(rows, rows),
        check_vma=False,
    )
```

time: 153 us -> 53.7 us (0.35)
  waiting for transfers between devices: 56.4 us -> 0.53 us
  local copies, waits for them, and re-layouts: 45.8 us -> 8.33 us
  Pallas kernels: 0 us -> 31.3 us
  starting transfers between devices: 29.3 us -> 8.36 us
  matrix products: 11.4 us -> 0 us
  blocking collectives: 2.46 us -> 0 us
  other arithmetic: 5.9 us -> 3.6 us
    ppermute x12 -> x7, waiting for transfers between devices: 56.4 us -> 0.53 us  [the longest x1 0.52 us: local(): summed = total + lax.ppermute(total, 'disp', swap)]
    gather x2 -> x0, local copies, waits for them, and re-layouts: 34.9 us -> none  [take_plane(): return lax.dynamic_slice_in_dim(padded, DSP - plane, col_count, 2)]
    pallas_call x0 -> x3, Pallas kernels: none -> 31.3 us  [the longest x1 25.2 us: local(): pl.pallas_call(functools.partial(score_kernel, pix_size=pix_size, disp_si...]
    ppermute x12 -> x7, starting transfers between devices: 29.3 us -> 8.36 us  [the longest x1 3.1 us: local(): from_pair = lax.ppermute(coarse, both, pairs)]
    dot_general x10 -> x0, matrix products: 11.4 us -> none  [the longest x4 5.53 us: conv_valid(): jnp.einsum('dkrw,ko->dorw', columns[shift_d:shift_d + plane_total], folde...]
    another operation x4 -> x11, local copies, waits for them, and re-layouts: 0.93 us -> 3.83 us  [the longest x6 2.86 us: toeplitz(): jnp.stack([jnp.pad(moved, ((0, 0), (0, 0), (do, 1 - do), (ro, 1 - ro), (0...]
    unnamed x43 -> x28, local copies, waits for them, and re-layouts: 5.54 us -> 2.96 us
    psum x1 -> x0, blocking collectives: 2.46 us -> none  [local(): lax.psum((jnp.sum(expo, 0), jnp.sum(expo * plane_frac[:, None, None], 0))...]
  transfers between devices with their start and end apart: 12 -> 7, of which waited for: 7 -> 1; matrix products, arithmetic and copies ran while one was open for 0% -> 14% of each run, Pallas kernels for 0% -> 5%
where the time goes in v1:
time: 53.7 us; the launch traced here: 53.1 us
  Pallas kernels  31.3 us (58%)
  starting transfers between devices  8.36 us (16%)
  local copies, waits for them, and re-layouts  8.33 us (16%)
  other arithmetic  3.6 us (7%)
  between operations  0.93 us (2%)
    pallas_call x1, Pallas kernels, local(): pl.pallas_call(functools.partial(score_kernel, pix_size=pix_size, disp_si...  25.2 us
    pallas_call x1, Pallas kernels, local(): pl.pallas_call(functools.partial(refine_kernel, pix_size=pix_size), out_s...  3.66 us
    ppermute x1, starting transfers between devices, local(): from_pair = lax.ppermute(coarse, both, pairs)  3.1 us
    ppermute x1, starting transfers between devices, local(): from_pair = lax.ppermute(packed, both, pairs)  3 us
    unnamed x28, local copies, waits for them, and re-layouts  2.96 us
    another operation x6, local copies, waits for them, and re-layouts, toeplitz(): jnp.stack([jnp.pad(moved, ((0, 0), (0, 0), (do, 1 - do), (ro, 1 - ro), (0...  2.86 us
    pallas_call x1, Pallas kernels, local(): pl.pallas_call(mixing_kernel, out_shape=jax.ShapeDtypeStruct((3 * local_r...  2.44 us
    ppermute x1, starting transfers between devices, local(): far_rows = lax.ppermute(coarse, both, far)  1.12 us
  transfers between devices with their start and end apart: 7, of which 1 were waited for; matrix products, arithmetic and copies ran while one was open for 14% of the time, Pallas kernels for 5%

profile of v1, /device:TPU:0, one launch (start us, length us, event | category | flops | bytes accessed | tf_op | source)
XLA Modules:
  0.0 53.1 jit_solution(15740127414253006595)
XLA Ops:
  0.6 0.8 %convert_element_type.40 = bf16[8,1024]{1,0:T(8,128)(2,1)S(1)} convert(s32[8,1024]{1,0:T(8,128)} %param.10) | non-fusion elementwise | flops 8192 | bytes 49152 | tf_op jit(solution)/shard_map/convert_element_type | solution.py:417
  1.4 0.8 %convert_element_type.41 = bf16[8,1024]{1,0:T(8,128)(2,1)S(1)} convert(s32[8,1024]{1,0:T(8,128)} %param.11) | non-fusion elementwise | flops 8192 | bytes 49152 | tf_op jit(solution)/shard_map/convert_element_type | solution.py:417
  2.2 0.8 %convert_element_type.42 = bf16[8,1024]{1,0:T(8,128)(2,1)S(1)} convert(f32[8,1024]{1,0:T(8,128)} %param.19) | non-fusion elementwise | flops 8192 | bytes 49152 | tf_op jit(solution)/shard_map/convert_element_type | solution.py:417
  2.9 3.0 %collective-permute-start = (bf16[24,1024]{1,0:T(8,128)(2,1)S(1)}, bf16[24,1024]{1,0:T(8,128)(2,1)S(1)}, u32[]{:S(2)}, u32[]{:S(2)}) collective-permute-start(bf16[24,1024]{1,0:T(8,128)(2,1)S(1)} %pad_maximum_fusion.3.own_ref), channel_id=1, source_target_pairs={{0,2},{1,3},{2,0},{3,1},{4,6},{5,7},{6,4},{7,5},{8,10},{9,11},{10,... | collective-permute-start | bytes 147464 | tf_op jit(solution)/shard_map/ppermute | solution.py:419
  5.9 1.3 %pad_bitcast_fusion.3 = (bf16[3,1,16,4,4,16]{2,5,0,4,3,1:T(8,128)(2,1)S(1)}, bf16[3,1,16,4,4,16]{2,5,0,4,3,1:T(8,128)(2,1)S(1)}, bf16[3,1,16,4,4,16]{2,5,0,4,3,1:T(8,128)(2,1)S(1)}, bf16[3,1,16,4,4,16]{2,5,0,4,3,1:T(8,128)(2,1)S(1)}) fusion(bf16[3,16,3,3,16]{1,4,0,3,2:T(8,128)(2,1)} %bitcast.26), kind=kLoop, calls=%fused_computation.11 | loop fusion | bytes 112128 | tf_op jit(solution)/shard_map/stack | solution.py:366
  7.2 1.0 %copy.77 = bf16[3,16,3,3,16]{4,3,2,1,0:T(4,128)(2,1)S(1)} copy(bf16[3,16,3,3,16]{1,4,0,3,2:T(8,128)(2,1)} %bitcast.27) | data formatting | bytes 27648
  8.3 0.4 fusion.3
  8.7 0.2 stack.50
  8.9 0.2 stack.51
  9.1 0.2 stack.52
  9.3 0.2 stack.53
  9.5 0.2 multiply_bitcast_fusion
  9.7 0.5 %reshape.31 = f32[192,192]{0,1:T(8,128)S(1)} reshape(f32[12,16,4,12,4]{1,0,4,3,2:T(8,128)S(1)} %multiply_bitcast_fusion) | data formatting | bytes 294912 | tf_op jit(solution)/shard_map/reshape | solution.py:428
  10.3 0.1 copy.64
  10.5 0.1 stack_reshape.6
  11.0 0.2 pad_maximum_fusion
  11.3 0.8 %copy.66 = bf16[3,4,16,4,4,16]{5,4,3,2,1,0:T(4,128)(2,1)S(1)} copy(bf16[3,4,16,4,4,16]{2,5,0,4,3,1:T(8,128)(2,1)S(1)} %pad_maximum_fusion) | data formatting | bytes 196608 | tf_op jit(solution)/shard_map/stack | solution.py:366
  12.1 0.7 %reshape_reshape.3.first_ref = bf16[192,256]{1,0:T(8,128)(2,1)S(1)} reshape(bf16[3,4,16,4,4,16]{5,4,3,2,1,0:T(4,128)(2,1)S(1)} %copy.66) | data formatting | bytes 196608 | tf_op jit(solution)/shard_map/reshape;reshape | solution.py:377
  13.0 25.2 %score.1 = (f32[8,256]{1,0:T(8,128)S(1)}, bf16[96,256]{1,0:T(8,128)(2,1)S(1)}, f32[24,1024]{1,0:T(8,128)S(1)}) custom-call(s32[2]{0:T(128)S(1)} %pad_add_fusion.place_ref, bf16[24,1024]{1,0:T(8,128)(2,1)S(1)} %pad_maximum_fusion.3.own_ref, bf16[24,1024]{1,0:T(8,128)(2,1)S(1)} %collective-permute-done.pair_ref, ...), custom_call_target="tpu_custom_call" | custom-call | tf_op jit(solution)/shard_map/score/pallas_call | solution.py:439
  38.2 0.6 %copy-done = f32[24,1024]{1,0:T(8,128)} copy-done((f32[24,1024]{1,0:T(8,128)}, f32[24,1024]{1,0:T(8,128)S(1)}, u32[]{:S(2)}) %copy-start) | copy-done | bytes 98328
  38.8 0.6 %copy-done.1 = bf16[96,256]{1,0:T(8,128)(2,1)} copy-done((bf16[96,256]{1,0:T(8,128)(2,1)}, bf16[96,256]{1,0:T(8,128)(2,1)S(1)}, u32[]{:S(2)}) %copy-start.1) | copy-done | bytes 49176
  39.4 0.6 %collective-permute-start.2 = (f32[4,256]{1,0:T(4,128)S(1)}, f32[4,256]{1,0:T(4,128)S(1)}, u32[]{:S(2)}, u32[]{:S(2)}) collective-permute-start(f32[4,256]{1,0:T(4,128)S(1)} %slice.9), channel_id=1, source_target_pairs={{0,1},{1,0},{2,3},{3,2},{4,5},{5,4},{6,7},{7,6},{8,9},{9,8},{10,11... | collective-permute-start | bytes 12296 | tf_op jit(solution)/shard_map/ppermute | solution.py:458
  40.1 0.1 copy.72
  40.3 0.1 copy.75
  40.4 0.5 collective-permute-done.2
  40.9 1.1 %collective-permute-start.5 = (f32[2,256]{1,0:T(2,128)S(1)}, f32[2,256]{1,0:T(2,128)S(1)}, u32[]{:S(2)}, u32[]{:S(2)}) collective-permute-start(f32[2,256]{1,0:T(2,128)S(1)} %slice_divide_fusion.own_ref), channel_id=1, source_target_pairs={{0,5},{1,3},{2,7},{3,1},{4,9},{5,0},{6,11},{7,2},{8,13},{9,4},{10,... | collective-permute-start | bytes 6152 | tf_op jit(solution)/shard_map/ppermute | solution.py:460
  42.1 3.1 %collective-permute-start.3 = (f32[2,256]{1,0:T(2,128)S(1)}, f32[2,256]{1,0:T(2,128)S(1)}, u32[]{:S(2)}, u32[]{:S(2)}) collective-permute-start(f32[2,256]{1,0:T(2,128)S(1)} %slice_divide_fusion.own_ref), channel_id=1, source_target_pairs={{0,2},{1,3},{2,0},{3,1},{4,6},{5,7},{6,4},{7,5},{8,10},{9,11},{10,... | collective-permute-start | bytes 6152 | tf_op jit(solution)/shard_map/ppermute | solution.py:461
  45.2 0.5 collective-permute-start.6
  45.7 0.7 %pad_maximum_fusion.2.mask_ref = bf16[432,16]{1,0:T(8,128)(2,1)} fusion(bf16[144,16]{1,0:T(8,128)(2,1)S(1)} %get-tuple-element.12, bf16[144,16]{1,0:T(8,128)(2,1)S(1)} %get-tuple-element.11, bf16[144,16]{1,0:T(8,128)(2,1)S(1)} %get-tuple-element.21), kind=kLoop, calls=%fused_computation.12 | loop fusion | flops 41472 | bytes 27648 | tf_op jit(solution)/shard_map/concatenate | solution.py:431
  46.3 2.4 %mixing.1.mix_ref = f32[6,144,256]{2,1,0:T(8,128)} custom-call(bf16[96,256]{1,0:T(8,128)(2,1)} %copy-done.1, bf16[432,16]{1,0:T(8,128)(2,1)} %pad_maximum_fusion.2.mask_ref), custom_call_target="tpu_custom_call" | custom-call | tf_op jit(solution)/shard_map/mixing/pallas_call | solution.py:464
  48.8 0.5 copy-done.7
  49.4 3.7 %refine.1 = f32[8,1024]{1,0:T(8,128)} custom-call(s32[2]{0:T(128)} %copy-done.2, f32[2,256]{1,0:T(2,128)} %copy-done.4, f32[2,256]{1,0:T(2,128)} %copy-done.7, f32[2,256]{1,0:T(2,128)} %copy-done.8, f32[2,256]{1,0:T(2,128)} %copy-done.6, f32[2,256]{1,0:T(2,128)} %copy-done.9, f32[6,144,256]{2,1,0:T(8,128)} %mixing.1.mix_ref, f32[24,1024]{1,0:T(8,128)} %copy-done), custom_call_target="tpu_custom_call" | custom-call | tf_op jit(solution)/shard_map/refine/pallas_call | solution.py:471
  (54 shorter events, 0.9 us)
Async XLA Ops:
  2.2 7.3 %copy-start.5 = (f32[16,16]{1,0:T(8,128)S(1)}, f32[16,16]{1,0:T(8,128)}, u32[]{:S(2)}) copy-start(f32[16,16]{1,0:T(8,128)} %param.12) | copy-start | bytes 3076
  2.9 9.9 %collective-permute-start = (bf16[24,1024]{1,0:T(8,128)(2,1)S(1)}, bf16[24,1024]{1,0:T(8,128)(2,1)S(1)}, u32[]{:S(2)}, u32[]{:S(2)}) collective-permute-start(bf16[24,1024]{1,0:T(8,128)(2,1)S(1)} %pad_maximum_fusion.3.own_ref), channel_id=1, source_target_pairs={{0,2},{1,3},{2,0},{3,1},{4,6},{5,7},{6,4},{7,5},{8,10},{9,11},{10,... | collective-permute-start | bytes 147464 | tf_op jit(solution)/shard_map/ppermute | solution.py:419
  5.9 6.9 %collective-permute-start.1 = (bf16[24,1024]{1,0:T(8,128)(2,1)S(1)}, bf16[24,1024]{1,0:T(8,128)(2,1)S(1)}, u32[]{:S(2)}, u32[]{:S(2)}) collective-permute-start(bf16[24,1024]{1,0:T(8,128)(2,1)S(1)} %pad_maximum_fusion.3.own_ref), channel_id=1, source_target_pairs={{0,1},{1,0},{2,4},{3,5},{4,2},{5,3},{6,8},{7,9},{8,6},{9,7},{10,12... | collective-permute-start | bytes 147464 | tf_op jit(solution)/shard_map/ppermute | solution.py:420
  9.7 0.8 %copy-start.10 = (f32[16]{0:T(128)S(1)}, f32[16]{0:T(128)}, u32[]{:S(2)}) copy-start(f32[16]{0:T(128)} %param.16) | copy-start | bytes 196
  9.7 0.9 %copy-start.11 = (f32[16]{0:T(128)S(1)}, f32[16]{0:T(128)}, u32[]{:S(2)}) copy-start(f32[16]{0:T(128)} %param.17) | copy-start | bytes 196
  9.7 1.1 %copy-start.12 = (f32[16]{0:T(128)S(1)}, f32[16]{0:T(128)}, u32[]{:S(2)}) copy-start(f32[16]{0:T(128)} %param.14) | copy-start | bytes 196
  11.3 26.9 %copy-start.2 = (s32[2]{0:T(128)}, s32[2]{0:T(128)S(1)}, u32[]{:S(2)}) copy-start(s32[2]{0:T(128)S(1)} %pad_add_fusion.place_ref) | copy-start | bytes 28
  11.3 28.8 %copy-start.3 = (f32[16,144]{1,0:T(8,128)S(1)}, f32[16,144]{1,0:T(8,128)}, u32[]{:S(2)}) copy-start(f32[16,144]{1,0:T(8,128)} %param.18) | copy-start | bytes 27652
  38.2 0.6 %copy-start = (f32[24,1024]{1,0:T(8,128)}, f32[24,1024]{1,0:T(8,128)S(1)}, u32[]{:S(2)}) copy-start(f32[24,1024]{1,0:T(8,128)S(1)} %get-tuple-element.7.conf_ref) | copy-start | bytes 294916
  38.8 0.6 %copy-start.1 = (bf16[96,256]{1,0:T(8,128)(2,1)}, bf16[96,256]{1,0:T(8,128)(2,1)S(1)}, u32[]{:S(2)}) copy-start(bf16[96,256]{1,0:T(8,128)(2,1)S(1)} %get-tuple-element.6.left_ref) | copy-start | bytes 147460
  39.4 1.4 %collective-permute-start.2 = (f32[4,256]{1,0:T(4,128)S(1)}, f32[4,256]{1,0:T(4,128)S(1)}, u32[]{:S(2)}, u32[]{:S(2)}) collective-permute-start(f32[4,256]{1,0:T(4,128)S(1)} %slice.9), channel_id=1, source_target_pairs={{0,1},{1,0},{2,3},{3,2},{4,5},{5,4},{6,7},{7,6},{8,9},{9,8},{10,11... | collective-permute-start | bytes 12296 | tf_op jit(solution)/shard_map/ppermute | solution.py:458
  40.9 7.9 %copy-start.4 = (f32[2,256]{1,0:T(2,128)}, f32[2,256]{1,0:T(2,128)S(1)}, u32[]{:S(2)}) copy-start(f32[2,256]{1,0:T(2,128)S(1)} %slice_divide_fusion.own_ref) | copy-start | bytes 6148
  40.9 4.3 %collective-permute-start.5 = (f32[2,256]{1,0:T(2,128)S(1)}, f32[2,256]{1,0:T(2,128)S(1)}, u32[]{:S(2)}, u32[]{:S(2)}) collective-permute-start(f32[2,256]{1,0:T(2,128)S(1)} %slice_divide_fusion.own_ref), channel_id=1, source_target_pairs={{0,5},{1,3},{2,7},{3,1},{4,9},{5,0},{6,11},{7,2},{8,13},{9,4},{10,... | collective-permute-start | bytes 6152 | tf_op jit(solution)/shard_map/ppermute | solution.py:460
  42.1 6.7 %collective-permute-start.3 = (f32[2,256]{1,0:T(2,128)S(1)}, f32[2,256]{1,0:T(2,128)S(1)}, u32[]{:S(2)}, u32[]{:S(2)}) collective-permute-start(f32[2,256]{1,0:T(2,128)S(1)} %slice_divide_fusion.own_ref), channel_id=1, source_target_pairs={{0,2},{1,3},{2,0},{3,1},{4,6},{5,7},{6,4},{7,5},{8,10},{9,11},{10,... | collective-permute-start | bytes 6152 | tf_op jit(solution)/shard_map/ppermute | solution.py:461
  45.2 3.6 %collective-permute-start.4 = (f32[2,256]{1,0:T(2,128)S(1)}, f32[2,256]{1,0:T(2,128)S(1)}, u32[]{:S(2)}, u32[]{:S(2)}) collective-permute-start(f32[2,256]{1,0:T(2,128)S(1)} %slice_divide_fusion.own_ref), channel_id=1, source_target_pairs={{0,1},{1,0},{2,4},{3,5},{4,2},{5,3},{6,8},{7,9},{8,6},{9,7},{10,12... | collective-permute-start | bytes 6152 | tf_op jit(solution)/shard_map/ppermute | solution.py:462
  45.2 3.7 %copy-start.6 = (f32[2,256]{1,0:T(2,128)}, f32[2,256]{1,0:T(2,128)S(1)}, u32[]{:S(2)}) copy-start(f32[2,256]{1,0:T(2,128)S(1)} %collective-permute-done.5.far_ref) | copy-start | bytes 6148
  45.2 3.6 %collective-permute-start.6 = (f32[2,256]{1,0:T(2,128)S(1)}, f32[2,256]{1,0:T(2,128)S(1)}, u32[]{:S(2)}, u32[]{:S(2)}) collective-permute-start(f32[2,256]{1,0:T(2,128)S(1)} %collective-permute-done.5.far_ref), channel_id=1, source_target_pairs={{0,1},{1,0},{2,3},{3,2},{4,5},{5,4},{6,7},{7,6},{8,9},{9,8},{10,11... | collective-permute-start | bytes 6152 | tf_op jit(solution)/shard_map/ppermute | solution.py:463
  48.8 0.6 %copy-start.7 = (f32[2,256]{1,0:T(2,128)}, f32[2,256]{1,0:T(2,128)S(1)}, u32[]{:S(2)}) copy-start(f32[2,256]{1,0:T(2,128)S(1)} %collective-permute-done.3.pair_ref) | copy-start | bytes 6148
  48.8 0.6 %copy-start.8 = (f32[2,256]{1,0:T(2,128)}, f32[2,256]{1,0:T(2,128)S(1)}, u32[]{:S(2)}) copy-start(f32[2,256]{1,0:T(2,128)S(1)} %collective-permute-done.4.other_ref) | copy-start | bytes 6148
  48.8 0.6 %copy-start.9 = (f32[2,256]{1,0:T(2,128)}, f32[2,256]{1,0:T(2,128)S(1)}, u32[]{:S(2)}) copy-start(f32[2,256]{1,0:T(2,128)S(1)} %collective-permute-done.6.swapped_ref) | copy-start | bytes 6148

commit v2 on v1

--- a/solution.py
+++ b/solution.py
@@ -40,13 +40,6 @@
     middle = rest.astype(bf16)
     low = (rest - middle.astype(f32)).astype(bf16)
     return high, middle, low
-
-
-def split3_outside(values):
-    high = lax.reduce_precision(values, 8, 7)
-    middle = lax.reduce_precision(values - high, 8, 7)
-    low = values - high - middle
-    return high.astype(bf16), middle.astype(bf16), low.astype(bf16)
 
 
 def phase_matrix(transposed):
@@ -102,12 +95,12 @@
     return jnp.concatenate(outs, 1)
 
 
-def shift_right(values):
+def shift_right(values, amount=1):
     lane = lax.broadcasted_iota(jnp.int32, (values.shape[0], 128), 1)
-    rolled = [pltpu.roll(values[:, t : t + 128], 1, 1) for t in range(0, values.shape[1], 128)]
+    rolled = [pltpu.roll(values[:, t : t + 128], amount, 1) for t in range(0, values.shape[1], 128)]
     zero = jnp.zeros_like(rolled[0])
     return jnp.concatenate(
-        [jnp.where(lane == 0, prev, now) for prev, now in zip([zero] + rolled[:-1], rolled)], 1
+        [jnp.where(lane < amount, prev, now) for prev, now in zip([zero] + rolled[:-1], rolled)], 1
     )
 
 
@@ -128,7 +121,6 @@
 
 
 def score_kernel(
-    place_ref,
     own_ref,
     pair_ref,
     other_ref,
@@ -146,8 +138,8 @@
     pix_size,
     disp_size,
 ):
-    pix = place_ref[0]
-    disp = place_ref[1]
+    pix = lax.axis_index("pix")
+    disp = lax.axis_index("disp")
     plane_count = DSP // disp_size
     even = pix % 2 == 0
     pair = pair_ref[...].astype(f32)
@@ -201,11 +193,13 @@
         volume[0] = (left_wide * shifted_by(start - 2)).astype(bf16)
         volume[1] = (left_wide * shifted_by(start - 1)).astype(bf16)
 
-    def fill(plane, moved):
-        volume[plane] = (left_wide * moved).astype(bf16)
-        return shift_right(moved)
-
-    lax.fori_loop(2, plane_count + 4, fill, shifted_by(start), unroll=2)
+    def fill(t, moved):
+        for k in range(6):
+            plane = moved if k == 0 else shift_right(moved, k)
+            volume[2 + 6 * t + k] = (left_wide * plane).astype(bf16)
+        return shift_right(moved, 6)
+
+    lax.fori_loop(0, (plane_count + 2) // 6, fill, shifted_by(start))
 
     @pl.when(disp == disp_size - 1)
     def _():
@@ -226,7 +220,7 @@
             )
         return carry
 
-    lax.fori_loop(0, plane_count // 2 + 1, conv_first, 0)
+    lax.fori_loop(0, plane_count // 2 + 1, conv_first, 0, unroll=3)
 
     @pl.when(disp == 0)
     def _():
@@ -256,7 +250,7 @@
         folded[t] = jnp.sum(made.reshape(8, 8, made.shape[1]), 0)
         return carry
 
-    lax.fori_loop(0, plane_count // 2, conv_second, 0)
+    lax.fori_loop(0, plane_count // 2, conv_second, 0, unroll=4)
 
     score = folded[...]
     cols = score.shape[2]
@@ -289,7 +283,6 @@
 
 
 def refine_kernel(
-    place_ref,
     own_ref,
     pair_ref,
     other_ref,
@@ -301,8 +294,8 @@
     *,
     pix_size,
 ):
-    pix = place_ref[0]
-    disp = place_ref[1]
+    pix = lax.axis_index("pix")
+    disp = lax.axis_index("disp")
     local = own_ref.shape[0]
     even = pix % 2 == 0
     above = jnp.where(even, other_ref[...], pair_ref[...])
@@ -332,50 +325,122 @@
     lanes = target.shape[1]
     global_row = lax.broadcasted_iota(jnp.int32, target.shape, 0) + (pix - 1) * out_rows
     row_inside = (global_row >= 0) & (global_row < pix_size * out_rows - 1)
-    local_row = lax.broadcasted_iota(jnp.int32, target.shape, 0)
     lane_id = lax.broadcasted_iota(jnp.int32, target.shape, 1)
     last_col = lane_id == lanes - 1
     anchor = primal_step * conf * target
-    scale = 1.0 + primal_step * conf
+    scale = 1.0 / (1.0 + primal_step * conf)
+    both_steps = primal_step * dual_step
+    gain_y = jnp.where(row_inside, both_steps, 0.0)
+    gain_x = jnp.where(last_col, 0.0, both_steps)
+    bound = primal_step * tv_bound
     primal = target
     extrap = target
     dual_x = jnp.zeros_like(target)
     dual_y = jnp.zeros_like(target)
     for _ in range(TV_ITERS):
         downward = pltpu.roll(extrap, fine - 1, 0)
-        grad_y = jnp.where(row_inside, downward - extrap, 0.0)
         ahead = jnp.concatenate([extrap[:, cols:], shift_left(extrap[:, :cols])], 1)
-        grad_x = jnp.where(last_col, 0.0, ahead - extrap)
-        trial_x = dual_x + dual_step * grad_x
-        trial_y = dual_y + dual_step * grad_y
-        shrink = jnp.maximum(1.0, jnp.sqrt(trial_x * trial_x + trial_y * trial_y) / tv_bound)
-        dual_x = trial_x / shrink
-        dual_y = trial_y / shrink
-        upper = jnp.where(local_row == 0, 0.0, pltpu.roll(dual_y, 1, 0))
+        trial_x = dual_x + gain_x * (ahead - extrap)
+        trial_y = dual_y + gain_y * (downward - extrap)
+        shrink = jnp.minimum(1.0, bound * lax.rsqrt(trial_x * trial_x + trial_y * trial_y))
+        dual_x = trial_x * shrink
+        dual_y = trial_y * shrink
+        upper = pltpu.roll(dual_y, 1, 0)
         behind = jnp.concatenate([shift_right(dual_x[:, lanes - cols :]), dual_x[:, : lanes - cols]], 1)
-        divergence = dual_x - behind + dual_y - upper
-        updated = (primal + primal_step * divergence + anchor) / scale
+        updated = (primal + (dual_x - behind + dual_y - upper) + anchor) * scale
         extrap = 2.0 * updated - primal
         primal = updated
     kept = primal[out_rows : 2 * out_rows]
     out_ref[...] = interleave([kept[:, b * cols : (b + 1) * cols] for b in range(UP)])
 
 
-def toeplitz(weights, order):
-    moved = weights.transpose(2, 4, 0, 1, 3)
-    blocks = jnp.stack(
-        [
-            jnp.pad(moved, ((0, 0), (0, 0), (do, 1 - do), (ro, 1 - ro), (0, 0)))
-            for do in range(2)
-            for ro in range(2)
-        ],
-        1,
-    )
-    taps, outs = (blocks.shape[0], blocks.shape[2])
-    blocks = blocks.reshape(taps, 4, outs, -1)
-    if order == "channel_last":
-        return blocks.reshape(taps * 4 * outs, -1)
-    return blocks.transpose(0, 2, 1, 3).reshape(taps * 4 * outs, -1)
+def pack_kernel(left_ref, right_ref, conf_ref, out_ref):
+    parts = [left_ref[...].astype(f32), right_ref[...].astype(f32), conf_ref[...]]
+    out_ref[...] = jnp.concatenate(parts, 0).astype(bf16)
+
+
+def transposed(values):
+    size = values.shape[1]
+    eye = lax.broadcasted_iota(jnp.int32, (size, size), 0) == lax.broadcasted_iota(
+        jnp.int32, (size, size), 1
+    )
+    eye = jnp.where(eye, 1.0, 0.0).astype(bf16)
+    flipped = lax.dot_general(
+        eye, values, (((1,), (1,)), ((), ())), preferred_element_type=f32
+    )
+    return flipped.astype(bf16)
+
+
+def column(values, index):
+    count = values.shape[0]
+    lane = lax.broadcasted_iota(jnp.int32, (index.shape[0], count), 1)
+    wide = jnp.broadcast_to(values.reshape(1, count), (index.shape[0], count))
+    return jnp.sum(jnp.where(lane == index, wide, 0.0), 1, keepdims=True)
+
+
+def prepare_kernel(
+    feat_ref,
+    first_weight_ref,
+    first_bias_ref,
+    second_weight_ref,
+    second_bias_ref,
+    head_ref,
+    mask_weight_ref,
+    project_ref,
+    first_ref,
+    second_ref,
+    const_ref,
+    mask_ref,
+):
+    taps = first_weight_ref.shape[0] ** 3 * CH
+    flat = [
+        transposed(ref[...].reshape(taps, CH)) for ref in (first_weight_ref, second_weight_ref)
+    ]
+    flat = jnp.concatenate(flat, 0)
+    source = lax.broadcasted_iota(jnp.int32, (taps, 256), 0)
+    lane = lax.broadcasted_iota(jnp.int32, (1, 256), 1)
+    plane, row, chan = (lane // 64, (lane // CH) % 4, lane % CH)
+    out_row = lax.broadcasted_iota(jnp.int32, (64, 64), 0)
+    out_col = lax.broadcasted_iota(jnp.int32, (64, 64), 1)
+    regroup = jnp.where(out_col == (out_row % 4) * CH + out_row // 4, 1.0, 0.0).astype(bf16)
+    for tap in range(3):
+        wanted = jnp.where((plane < 3) & (row < 3), ((plane * 3 + row) * 3 + tap) * CH + chan, -1)
+        select = jnp.where(source == wanted, 1.0, 0.0).astype(bf16)
+        base = jnp.dot(flat, select, preferred_element_type=f32)
+        placed = [base] + [pltpu.roll(base, 64 * (j // 2) + CH * (j % 2), 1) for j in range(1, 4)]
+        blocks = [jnp.concatenate([p[n * CH : n * CH + CH] for p in placed], 0) for n in range(2)]
+        first_ref[64 * tap : 64 * tap + 64, :] = blocks[0].astype(bf16)
+        mixed = jnp.dot(regroup, blocks[1].astype(bf16), preferred_element_type=f32)
+        second_ref[64 * tap : 64 * tap + 64, :] = mixed.astype(bf16)
+
+    size = project_ref.shape[1]
+    groups = size // (UP * UP)
+    pixel = lax.broadcasted_iota(jnp.int32, (UP * UP, size), 0)
+    spot = lax.broadcasted_iota(jnp.int32, (UP * UP, size), 1)
+    expand = jnp.where(pixel == UP * (spot % UP) + spot // (UP * groups), 1.0, 0.0).astype(bf16)
+    own_group = lax.broadcasted_iota(jnp.int32, (size, size), 0) // CH
+    keep = own_group == (lax.broadcasted_iota(jnp.int32, (size, size), 1) // UP) % groups
+    for n, part in enumerate(split3(feat_ref[...])):
+        wide = jnp.dot(transposed(part), expand, preferred_element_type=f32)
+        wide = jnp.concatenate([wide] * groups, 0)
+        project_ref[size * n : size * n + size, :] = jnp.where(keep, wide, 0.0).astype(bf16)
+
+    kinds = mask_weight_ref.shape[1]
+    new = lax.broadcasted_iota(jnp.int32, (kinds, kinds), 0)
+    old = lax.broadcasted_iota(jnp.int32, (kinds, kinds), 1)
+    swapped = (new // (UP * UP)) * (UP * UP) + (new % UP) * UP + (new // UP) % UP
+    swapped = jnp.where(old == swapped, 1.0, 0.0).astype(bf16)
+    for n, part in enumerate(split3(mask_weight_ref[...])):
+        moved = lax.dot_general(
+            swapped, part, (((1,), (1,)), ((), ())), preferred_element_type=f32
+        )
+        mask_ref[kinds * n : kinds * n + kinds, :] = moved.astype(bf16)
+
+    index = lax.broadcasted_iota(jnp.int32, (64, 1), 0)
+    shape = const_ref.shape[1:]
+    const_ref[0] = jnp.broadcast_to(column(first_bias_ref[...], index % CH), shape)
+    const_ref[1] = jnp.broadcast_to(column(second_bias_ref[...], index // 4), shape)
+    const_ref[2] = jnp.broadcast_to(column(head_ref[...], index // 4), shape)
 
 
 def local(
@@ -398,7 +463,6 @@
     cols = width // UP
     local_rows = fine // UP
     plane_count = DSP // disp_size
-    place = jnp.stack([lax.axis_index("pix"), lax.axis_index("disp")]).astype(jnp.int32)
     swap = [(d, d ^ 1) for d in range(disp_size)]
     pairs = involution([(i, i + 1) for i in range(0, pix_size - 1, 2)], pix_size, disp_size)
     others = involution([(i, i + 1) for i in range(1, pix_size - 1, 2)], pix_size, disp_size)
@@ -413,29 +477,42 @@
         far += [(a, b), (b, a)]
     far = sorted(far)
 
-    packed = jnp.concatenate(
-        [left_image.astype(bf16), right_image.astype(bf16), confidence.astype(bf16)], 0
-    )
+    vmem = pl.BlockSpec(memory_space=pltpu.VMEM)
+    packed = pl.pallas_call(
+        pack_kernel,
+        out_shape=jax.ShapeDtypeStruct((3 * fine, width), bf16),
+        in_specs=[vmem] * 3,
+        out_specs=vmem,
+        compiler_params=pltpu.CompilerParams(vmem_limit_bytes=2 * 2**20),
+        name="pack",
+    )(left_image, right_image, confidence)
     from_pair = lax.ppermute(packed, both, pairs)
     from_other = lax.ppermute(packed, both, others)
 
-    first = toeplitz(first_weight, "channel_last")
-    second = toeplitz(second_weight, "channel_first")
     groups = 6 * local_rows
-    spread = jnp.einsum(
-        "abc,gh->gcbha", feat_weight.reshape(UP, UP, CH), jnp.eye(groups, dtype=f32),
-        precision=lax.Precision.HIGHEST,
-    ).reshape(groups * CH, UP * groups * UP)
-    project = jnp.concatenate(split3_outside(spread), 0)
-    by_phase = mask_weight.reshape(CH, 9, UP, UP).transpose(1, 3, 2, 0).reshape(-1, CH)
-    mask3 = jnp.concatenate(split3_outside(by_phase), 0)
-    consts = jnp.stack(
-        [jnp.tile(first_bias, 4), jnp.repeat(second_bias, 4), jnp.repeat(head_weight, 4)]
-    )
-    consts = jnp.broadcast_to(consts[:, :, None], consts.shape + (cols,))
-
-    vmem = pl.BlockSpec(memory_space=pltpu.VMEM)
-    smem = pl.BlockSpec(memory_space=pltpu.SMEM)
+    kinds = mask_weight.shape[1]
+    project, first, second, consts, mask3 = pl.pallas_call(
+        prepare_kernel,
+        out_shape=(
+            jax.ShapeDtypeStruct((3 * groups * CH, groups * UP * UP), bf16),
+            jax.ShapeDtypeStruct((192, 256), bf16),
+            jax.ShapeDtypeStruct((192, 256), bf16),
+            jax.ShapeDtypeStruct((3, 64, cols), f32),
+            jax.ShapeDtypeStruct((3 * kinds, CH), bf16),
+        ),
+        in_specs=[vmem] * 7,
+        out_specs=(vmem,) * 5,
+        compiler_params=pltpu.CompilerParams(vmem_limit_bytes=8 * 2**20),
+        name="prepare",
+    )(
+        feat_weight,
+        first_weight,
+        first_bias,
+        second_weight,
+        second_bias,
+        head_weight,
+        mask_weight,
+    )
     total, left, conf = pl.pallas_call(
         functools.partial(score_kernel, pix_size=pix_size, disp_size=disp_size),
         out_shape=(
@@ -443,16 +520,16 @@
             jax.ShapeDtypeStruct((3 * local_rows * CH, cols), bf16),
             jax.ShapeDtypeStruct((3 * fine, width), f32),
         ),
-        in_specs=[smem] + [vmem] * 7,
+        in_specs=[vmem] * 7,
         out_specs=(vmem, vmem, vmem),
         scratch_shapes=[
             pltpu.VMEM((plane_count + 4, 3 * local_rows * CH, cols), bf16),
             pltpu.VMEM((plane_count + 2, (local_rows + 2) * CH, cols), bf16),
             pltpu.VMEM((plane_count // 2, 8, cols), f32),
         ],
-        compiler_params=pltpu.CompilerParams(vmem_limit_bytes=32 * 2**20),
+        compiler_params=pltpu.CompilerParams(vmem_limit_bytes=16 * 2**20),
         name="score",
-    )(place, packed, from_pair, from_other, project, first, second, consts)
+    )(packed, from_pair, from_other, project, first, second, consts)
 
     total = total[:4]
     summed = total + lax.ppermute(total, "disp", swap)
@@ -466,15 +543,17 @@
         out_shape=jax.ShapeDtypeStruct((3 * local_rows, mask_weight.shape[1], cols), f32),
         in_specs=[vmem, vmem],
         out_specs=vmem,
+        compiler_params=pltpu.CompilerParams(vmem_limit_bytes=4 * 2**20),
         name="mixing",
     )(left, mask3)
     refined = pl.pallas_call(
         functools.partial(refine_kernel, pix_size=pix_size),
         out_shape=jax.ShapeDtypeStruct((fine, width), f32),
-        in_specs=[smem] + [vmem] * 7,
+        in_specs=[vmem] * 7,
         out_specs=vmem,
+        compiler_params=pltpu.CompilerParams(vmem_limit_bytes=8 * 2**20),
         name="refine",
-    )(place, coarse, from_pair, from_other, far_rows, swapped, mix, conf)
+    )(coarse, from_pair, from_other, far_rows, swapped, mix, conf)
     return (coarse, refined)
 
 

time: 53.7 us -> 31.3 us (0.58)
  Pallas kernels: 31.3 us -> 15.6 us
  local copies, waits for them, and re-layouts: 8.33 us -> 3.22 us
  other arithmetic: 3.6 us -> 0.01 us
  waiting for transfers between devices: 0.53 us -> 2.14 us
  starting transfers between devices: 8.36 us -> 9.24 us
    pallas_call x1, Pallas kernels: 25.2 us -> 11.3 us  [local(): pl.pallas_call(functools.partial(score_kernel, pix_size=pix_size, disp_si...]
    another operation x11 -> x0, local copies, waits for them, and re-layouts: 3.83 us -> none  [the longest x6 2.86 us: toeplitz(): jnp.stack([jnp.pad(moved, ((0, 0), (0, 0), (do, 1 - do), (ro, 1 - ro), (0...]
    convert_element_type x5 -> x0, other arithmetic: 2.37 us -> none  [the longest x1 0.77 us: local(): confidence.astype(bf16)]
    pallas_call x1, Pallas kernels: 2.44 us -> 0.56 us  [local(): pl.pallas_call(mixing_kernel, out_shape=jax.ShapeDtypeStruct((3 * local_r...]
    pallas_call x0 -> x2, Pallas kernels: none -> 1.36 us  [the longest x1 1.35 us: local(): pl.pallas_call(prepare_kernel, out_shape=(jax.ShapeDtypeStruct((3 * group...]
    pallas_call x1, Pallas kernels: 3.66 us -> 2.38 us  [local(): pl.pallas_call(functools.partial(refine_kernel, pix_size=pix_size), out_s...]
    ppermute x1, starting transfers between devices: 3 us -> 4.02 us  [local(): from_pair = lax.ppermute(packed, both, pairs)]
    ppermute x1, waiting for transfers between devices: 0.01 us -> 0.98 us  [local(): from_pair = lax.ppermute(coarse, both, pairs)]
  transfers between devices with their start and end apart: 7 -> 7, of which waited for: 1 -> 2; matrix products, arithmetic and copies ran while one was open for 14% -> 0% of each run, Pallas kernels for 5% -> 6%
where the time goes in v2:
time: 31.3 us; the launch traced here: 31 us
  Pallas kernels  15.6 us (50%)
  starting transfers between devices  9.24 us (30%)
  local copies, waits for them, and re-layouts  3.22 us (10%)
  waiting for transfers between devices  2.14 us (7%)
  between operations  0.77 us (2%)
    pallas_call x1, Pallas kernels, local(): pl.pallas_call(functools.partial(score_kernel, pix_size=pix_size, disp_si...  11.3 us
    ppermute x1, starting transfers between devices, local(): from_pair = lax.ppermute(packed, both, pairs)  4.02 us
    unnamed x22, local copies, waits for them, and re-layouts  3.22 us
    ppermute x1, starting transfers between devices, local(): from_pair = lax.ppermute(coarse, both, pairs)  2.87 us
    pallas_call x1, Pallas kernels, local(): pl.pallas_call(functools.partial(refine_kernel, pix_size=pix_size), out_s...  2.38 us
    ppermute x1, starting transfers between devices, local(): far_rows = lax.ppermute(coarse, both, far)  1.54 us
    pallas_call x1, Pallas kernels, local(): pl.pallas_call(prepare_kernel, out_shape=(jax.ShapeDtypeStruct((3 * group...  1.35 us
    ppermute x1, waiting for transfers between devices, local(): summed = total + lax.ppermute(total, 'disp', swap)  1.15 us
  transfers between devices with their start and end apart: 7, of which 2 were waited for; matrix products, arithmetic and copies ran while one was open for 0% of the time, Pallas kernels for 6%

profile of v2, /device:TPU:0, one launch (start us, length us, event | category | flops | bytes accessed | tf_op | source)
XLA Modules:
  0.0 31.0 jit_solution(2811163206370169910)
XLA Ops:
  0.6 0.0 copy-start
  0.6 0.0 copy-start.2
  0.7 0.8 %copy-done.2 = s32[8,1024]{1,0:T(8,128)S(1)} copy-done((s32[8,1024]{1,0:T(8,128)S(1)}, s32[8,1024]{1,0:T(8,128)}, u32[]{:S(2)}) %copy-start.2) | copy-done | bytes 32792
  1.4 0.8 %copy-done.3 = s32[8,1024]{1,0:T(8,128)S(1)} copy-done((s32[8,1024]{1,0:T(8,128)S(1)}, s32[8,1024]{1,0:T(8,128)}, u32[]{:S(2)}) %copy-start.3) | copy-done | bytes 32792
  2.2 0.8 %copy-done.4 = f32[8,1024]{1,0:T(8,128)S(1)} copy-done((f32[8,1024]{1,0:T(8,128)S(1)}, f32[8,1024]{1,0:T(8,128)}, u32[]{:S(2)}) %copy-start.4) | copy-done | bytes 32792
  3.0 0.0 copy-start.10
  3.0 0.6 %collective-permute-start.1 = (bf16[24,1024]{1,0:T(8,128)(2,1)S(1)}, bf16[24,1024]{1,0:T(8,128)(2,1)S(1)}, u32[]{:S(2)}, u32[]{:S(2)}) collective-permute-start(bf16[24,1024]{1,0:T(8,128)(2,1)S(1)} %pack.1.own_ref), channel_id=1, source_target_pairs={{0,1},{1,0},{2,4},{3,5},{4,2},{5,3},{6,8},{7,9},{8,6},{9,7},{10,12... | collective-permute-start | bytes 147464 | tf_op jit(solution)/shard_map/ppermute | solution.py:490
  3.5 4.0 %collective-permute-start = (bf16[24,1024]{1,0:T(8,128)(2,1)S(1)}, bf16[24,1024]{1,0:T(8,128)(2,1)S(1)}, u32[]{:S(2)}, u32[]{:S(2)}) collective-permute-start(bf16[24,1024]{1,0:T(8,128)(2,1)S(1)} %pack.1.own_ref), channel_id=1, source_target_pairs={{0,2},{1,3},{2,0},{3,1},{4,6},{5,7},{6,4},{7,5},{8,10},{9,11},{10,... | collective-permute-start | bytes 147464 | tf_op jit(solution)/shard_map/ppermute | solution.py:489
  7.6 0.0 copy-done
  7.6 0.0 copy-done.5
  7.6 0.0 copy-done.7
  7.6 0.0 copy-done.8
  7.6 0.0 copy-start.1
  7.6 0.9 %copy-done.1 = bf16[3,3,3,16,16]{4,3,2,1,0:T(8,128)(2,1)S(1)} copy-done((bf16[3,3,3,16,16]{4,3,2,1,0:T(8,128)(2,1)S(1)}, bf16[3,3,3,16,16]{4,3,2,1,0:T(8,128)(2,1)}, u32[]{:S(2)}) %copy-start.1) | copy-done | bytes 13848
  8.5 1.3 %prepare.1 = (bf16[576,192]{1,0:T(8,128)(2,1)S(1)}, bf16[192,256]{1,0:T(8,128)(2,1)S(1)}, bf16[192,256]{1,0:T(8,128)(2,1)S(1)}, f32[3,64,256]{2,1,0:T(8,128)S(1)}, bf16[432,16]{1,0:T(8,128)(2,1)S(1)}) custom-call(f32[16,16]{1,0:T(8,128)S(1)} %copy-done.7, bf16[3,3,3,16,16]{4,3,2,1,0:T(8,128)(2,1)S(1)} %copy-done, f32[16]{0:T(128)S(1)} %copy-done.8, ...), custom_call_target="tpu_custom_call" | custom-call | tf_op jit(solution)/shard_map/prepare/pallas_call | solution.py:494
  9.9 0.0 collective-permute-done.1.other_ref
  9.9 0.0 collective-permute-done.pair_ref
  9.9 11.3 %score.1 = (f32[8,256]{1,0:T(8,128)S(1)}, bf16[96,256]{1,0:T(8,128)(2,1)S(1)}, f32[24,1024]{1,0:T(8,128)S(1)}) custom-call(bf16[24,1024]{1,0:T(8,128)(2,1)S(1)} %pack.1.own_ref, bf16[24,1024]{1,0:T(8,128)(2,1)S(1)} %collective-permute-done.pair_ref, bf16[24,1024]{1,0:T(8,128)(2,1)S(1)} %collective-permute-done.1.other_ref, ...), custom_call_target="tpu_custom_call" | custom-call | tf_op jit(solution)/shard_map/score/pallas_call | solution.py:516
  21.2 0.1 collective-permute-start.2
  21.3 1.2 %collective-permute-done.2 = f32[4,256]{1,0:T(4,128)S(1)} collective-permute-done((f32[4,256]{1,0:T(4,128)S(1)}, f32[4,256]{1,0:T(4,128)S(1)}, u32[]{:S(2)}, u32[]{:S(2)}) %collective-permute-start.2) | collective-permute-done | bytes 4128 | tf_op jit(solution)/shard_map/ppermute | solution.py:535
  22.4 0.0 copy-start.6
  22.5 1.5 %collective-permute-start.5 = (f32[2,256]{1,0:T(2,128)S(1)}, f32[2,256]{1,0:T(2,128)S(1)}, u32[]{:S(2)}, u32[]{:S(2)}) collective-permute-start(f32[2,256]{1,0:T(2,128)S(1)} %slice_divide_fusion.own_ref), channel_id=1, source_target_pairs={{0,5},{1,3},{2,7},{3,1},{4,9},{5,0},{6,11},{7,2},{8,13},{9,4},{10,... | collective-permute-start | bytes 6152 | tf_op jit(solution)/shard_map/ppermute | solution.py:537
  24.0 0.2 collective-permute-start.4
  24.2 2.9 %collective-permute-start.3 = (f32[2,256]{1,0:T(2,128)S(1)}, f32[2,256]{1,0:T(2,128)S(1)}, u32[]{:S(2)}, u32[]{:S(2)}) collective-permute-start(f32[2,256]{1,0:T(2,128)S(1)} %slice_divide_fusion.own_ref), channel_id=1, source_target_pairs={{0,2},{1,3},{2,0},{3,1},{4,6},{5,7},{6,4},{7,5},{8,10},{9,11},{10,... | collective-permute-start | bytes 6152 | tf_op jit(solution)/shard_map/ppermute | solution.py:538
  27.0 0.0 collective-permute-done.5.far_ref
  27.0 0.0 collective-permute-start.6
  27.0 0.6 %mixing.1.mix_ref = f32[6,144,256]{2,1,0:T(8,128)S(1)} custom-call(bf16[96,256]{1,0:T(8,128)(2,1)S(1)} %get-tuple-element.15.left_ref, bf16[432,16]{1,0:T(8,128)(2,1)S(1)} %get-tuple-element.16.mask_ref), custom_call_target="tpu_custom_call" | custom-call | tf_op jit(solution)/shard_map/mixing/pallas_call | solution.py:541
  27.6 0.0 collective-permute-done.4.other_ref
  27.6 1.0 %collective-permute-done.3.pair_ref = f32[2,256]{1,0:T(2,128)S(1)} collective-permute-done((f32[2,256]{1,0:T(2,128)S(1)}, f32[2,256]{1,0:T(2,128)S(1)}, u32[]{:S(2)}, u32[]{:S(2)}) %collective-permute-start.3) | collective-permute-done | bytes 2080 | tf_op jit(solution)/shard_map/ppermute | solution.py:538
  28.6 0.0 collective-permute-done.6.swapped_ref
  28.6 0.0 copy-done.6
  28.6 2.4 %refine.1 = f32[8,1024]{1,0:T(8,128)} custom-call(f32[2,256]{1,0:T(2,128)S(1)} %slice_divide_fusion.own_ref, f32[2,256]{1,0:T(2,128)S(1)} %collective-permute-done.3.pair_ref, f32[2,256]{1,0:T(2,128)S(1)} %collective-permute-done.4.other_ref, f32[2,256]{1,0:T(2,128)S(1)} %collective-permute-done.5.far_ref, f32[2,256]{1,0:T(2,128)S(1)} %collective-permute-done.6.swapped_ref, ...), custom_call_target="tpu_custom_call" | custom-call | tf_op jit(solution)/shard_map/refine/pallas_call | solution.py:549
  (12 shorter events, 0.0 us)
Async XLA Ops:
  0.6 6.9 %copy-start = (bf16[3,3,3,16,16]{4,3,2,1,0:T(8,128)(2,1)S(1)}, bf16[3,3,3,16,16]{4,3,2,1,0:T(8,128)(2,1)}, u32[]{:S(2)}) copy-start(bf16[3,3,3,16,16]{4,3,2,1,0:T(8,128)(2,1)} %first_weight_ref.1) | copy-start | bytes 41476
  0.6 0.8 %copy-start.2 = (s32[8,1024]{1,0:T(8,128)S(1)}, s32[8,1024]{1,0:T(8,128)}, u32[]{:S(2)}) copy-start(s32[8,1024]{1,0:T(8,128)} %left_ref.1) | copy-start | bytes 98308
  1.4 0.8 %copy-start.3 = (s32[8,1024]{1,0:T(8,128)S(1)}, s32[8,1024]{1,0:T(8,128)}, u32[]{:S(2)}) copy-start(s32[8,1024]{1,0:T(8,128)} %right_ref.1) | copy-start | bytes 98308
  2.2 0.8 %copy-start.4 = (f32[8,1024]{1,0:T(8,128)S(1)}, f32[8,1024]{1,0:T(8,128)}, u32[]{:S(2)}) copy-start(f32[8,1024]{1,0:T(8,128)} %conf_ref.1) | copy-start | bytes 98308
  3.0 4.6 %copy-start.5 = (f32[16,144]{1,0:T(8,128)S(1)}, f32[16,144]{1,0:T(8,128)}, u32[]{:S(2)}) copy-start(f32[16,144]{1,0:T(8,128)} %mask_weight_ref.1) | copy-start | bytes 27652
  3.0 4.6 %copy-start.7 = (f32[16,16]{1,0:T(8,128)S(1)}, f32[16,16]{1,0:T(8,128)}, u32[]{:S(2)}) copy-start(f32[16,16]{1,0:T(8,128)} %feat_ref.1) | copy-start | bytes 3076
  3.0 4.6 %copy-start.8 = (f32[16]{0:T(128)S(1)}, f32[16]{0:T(128)}, u32[]{:S(2)}) copy-start(f32[16]{0:T(128)} %first_bias_ref.1) | copy-start | bytes 196
  3.0 4.6 %copy-start.9 = (f32[16]{0:T(128)S(1)}, f32[16]{0:T(128)}, u32[]{:S(2)}) copy-start(f32[16]{0:T(128)} %second_bias_ref.1) | copy-start | bytes 196
  3.0 4.6 %copy-start.10 = (f32[16]{0:T(128)S(1)}, f32[16]{0:T(128)}, u32[]{:S(2)}) copy-start(f32[16]{0:T(128)} %head_ref.1) | copy-start | bytes 196
  3.0 6.9 %collective-permute-start.1 = (bf16[24,1024]{1,0:T(8,128)(2,1)S(1)}, bf16[24,1024]{1,0:T(8,128)(2,1)S(1)}, u32[]{:S(2)}, u32[]{:S(2)}) collective-permute-start(bf16[24,1024]{1,0:T(8,128)(2,1)S(1)} %pack.1.own_ref), channel_id=1, source_target_pairs={{0,1},{1,0},{2,4},{3,5},{4,2},{5,3},{6,8},{7,9},{8,6},{9,7},{10,12... | collective-permute-start | bytes 147464 | tf_op jit(solution)/shard_map/ppermute | solution.py:490
  3.5 6.3 %collective-permute-start = (bf16[24,1024]{1,0:T(8,128)(2,1)S(1)}, bf16[24,1024]{1,0:T(8,128)(2,1)S(1)}, u32[]{:S(2)}, u32[]{:S(2)}) collective-permute-start(bf16[24,1024]{1,0:T(8,128)(2,1)S(1)} %pack.1.own_ref), channel_id=1, source_target_pairs={{0,2},{1,3},{2,0},{3,1},{4,6},{5,7},{6,4},{7,5},{8,10},{9,11},{10,... | collective-permute-start | bytes 147464 | tf_op jit(solution)/shard_map/ppermute | solution.py:489
  7.6 0.9 %copy-start.1 = (bf16[3,3,3,16,16]{4,3,2,1,0:T(8,128)(2,1)S(1)}, bf16[3,3,3,16,16]{4,3,2,1,0:T(8,128)(2,1)}, u32[]{:S(2)}) copy-start(bf16[3,3,3,16,16]{4,3,2,1,0:T(8,128)(2,1)} %second_weight_ref.1) | copy-start | bytes 41476
  21.2 1.2 %collective-permute-start.2 = (f32[4,256]{1,0:T(4,128)S(1)}, f32[4,256]{1,0:T(4,128)S(1)}, u32[]{:S(2)}, u32[]{:S(2)}) collective-permute-start(f32[4,256]{1,0:T(4,128)S(1)} %slice.9), channel_id=1, source_target_pairs={{0,1},{1,0},{2,3},{3,2},{4,5},{5,4},{6,7},{7,6},{8,9},{9,8},{10,11... | collective-permute-start | bytes 12296 | tf_op jit(solution)/shard_map/ppermute | solution.py:535
  22.4 6.2 %copy-start.6 = (f32[2,256]{1,0:T(2,128)}, f32[2,256]{1,0:T(2,128)S(1)}, u32[]{:S(2)}) copy-start(f32[2,256]{1,0:T(2,128)S(1)} %slice_divide_fusion.own_ref) | copy-start | bytes 6148
  22.5 4.6 %collective-permute-start.5 = (f32[2,256]{1,0:T(2,128)S(1)}, f32[2,256]{1,0:T(2,128)S(1)}, u32[]{:S(2)}, u32[]{:S(2)}) collective-permute-start(f32[2,256]{1,0:T(2,128)S(1)} %slice_divide_fusion.own_ref), channel_id=1, source_target_pairs={{0,5},{1,3},{2,7},{3,1},{4,9},{5,0},{6,11},{7,2},{8,13},{9,4},{10,... | collective-permute-start | bytes 6152 | tf_op jit(solution)/shard_map/ppermute | solution.py:537
  24.0 3.6 %collective-permute-start.4 = (f32[2,256]{1,0:T(2,128)S(1)}, f32[2,256]{1,0:T(2,128)S(1)}, u32[]{:S(2)}, u32[]{:S(2)}) collective-permute-start(f32[2,256]{1,0:T(2,128)S(1)} %slice_divide_fusion.own_ref), channel_id=1, source_target_pairs={{0,1},{1,0},{2,4},{3,5},{4,2},{5,3},{6,8},{7,9},{8,6},{9,7},{10,12... | collective-permute-start | bytes 6152 | tf_op jit(solution)/shard_map/ppermute | solution.py:539
  24.2 4.4 %collective-permute-start.3 = (f32[2,256]{1,0:T(2,128)S(1)}, f32[2,256]{1,0:T(2,128)S(1)}, u32[]{:S(2)}, u32[]{:S(2)}) collective-permute-start(f32[2,256]{1,0:T(2,128)S(1)} %slice_divide_fusion.own_ref), channel_id=1, source_target_pairs={{0,2},{1,3},{2,0},{3,1},{4,6},{5,7},{6,4},{7,5},{8,10},{9,11},{10,... | collective-permute-start | bytes 6152 | tf_op jit(solution)/shard_map/ppermute | solution.py:538
  27.0 1.6 %collective-permute-start.6 = (f32[2,256]{1,0:T(2,128)S(1)}, f32[2,256]{1,0:T(2,128)S(1)}, u32[]{:S(2)}, u32[]{:S(2)}) collective-permute-start(f32[2,256]{1,0:T(2,128)S(1)} %collective-permute-done.5.far_ref), channel_id=1, source_target_pairs={{0,1},{1,0},{2,3},{3,2},{4,5},{5,4},{6,7},{7,6},{8,9},{9,8},{10,11... | collective-permute-start | bytes 6152 | tf_op jit(solution)/shard_map/ppermute | solution.py:540

commit v3 on v2

--- a/solution.py
+++ b/solution.py
@@ -21,17 +21,26 @@
 bf16 = jnp.bfloat16
 
 
-def involution(pairs, pix_size, disp_size):
-    perm = []
-    used = set()
-    for i, j in pairs:
-        used |= {i, j}
-        for d in range(disp_size):
-            perm += [(i * disp_size + d, j * disp_size + d), (j * disp_size + d, i * disp_size + d)]
+def mixed_exchange(pix_size, disp_size):
+    send = {}
     for i in range(pix_size):
-        if i not in used:
-            perm += [(i * disp_size + d, i * disp_size + (d ^ 1)) for d in range(disp_size)]
-    return sorted(perm)
+        send[i, 0] = (i ^ 1, 0)
+        j = i + 1 if i % 2 else i - 1
+        send[i, 1] = (j, 1) if 0 <= j < pix_size else (i, 0)
+    for end in (0, pix_size - 1):
+        send[end ^ 1, 0] = (end, 1)
+    order = sorted(send)
+    return [tuple(p * disp_size + d for p, d in (key, send[key])) for key in order]
+
+
+def sort_neighbours(received, swapped, pix, disp, pix_size):
+    at_end = (pix == 0) | (pix == pix_size - 1)
+    direct = (disp == 0) != at_end
+    even = pix % 2 == 0
+    first_is_below = direct == even
+    below = jnp.where(first_is_below, received, swapped)
+    above = jnp.where(first_is_below, swapped, received)
+    return above, below
 
 
 def split3(values):
@@ -115,15 +124,14 @@
 
 def join_taps(taps):
     size = taps.shape[0] // 3
-    return (
-        taps[size : 2 * size] + shift_right(taps[:size]) + shift_left(taps[2 * size :])
-    )
+    sides = shift_right(taps[:size].astype(bf16)) + shift_left(taps[2 * size :].astype(bf16))
+    return taps[size : 2 * size] + sides.astype(f32)
 
 
 def score_kernel(
     own_ref,
-    pair_ref,
-    other_ref,
+    received_ref,
+    exchanged_ref,
     project_ref,
     first_ref,
     second_ref,
@@ -133,7 +141,6 @@
     conf_ref,
     volume,
     hidden,
-    folded,
     *,
     pix_size,
     disp_size,
@@ -141,11 +148,9 @@
     pix = lax.axis_index("pix")
     disp = lax.axis_index("disp")
     plane_count = DSP // disp_size
-    even = pix % 2 == 0
-    pair = pair_ref[...].astype(f32)
-    other = other_ref[...].astype(f32)
-    above = jnp.where(even, other, pair)
-    below = jnp.where(even, pair, other)
+    above, below = sort_neighbours(
+        received_ref[...].astype(f32), exchanged_ref[...].astype(f32), pix, disp, pix_size
+    )
     gathered = jnp.concatenate([above, own_ref[...].astype(f32), below], 0).astype(bf16)
     phases = deinterleave(gathered)
     fine = own_ref.shape[0] // 3
@@ -177,89 +182,76 @@
     left = jnp.where(inside, feats[:half], 0.0).astype(bf16)
     right = feats[half:].astype(bf16).astype(f32)
     left_ref[...] = left
-    left_wide = left.astype(f32)
     lane = lax.broadcasted_iota(jnp.int32, right.shape, 1)
     start = disp * plane_count
 
     def shifted_by(amount):
-        return jnp.where(lane >= amount, pltpu.roll(right, amount, 1), 0.0)
-
-    @pl.when(disp == 0)
-    def _():
-        volume[0:2] = jnp.zeros(volume[0:2].shape, bf16)
-
-    @pl.when(disp > 0)
-    def _():
-        volume[0] = (left_wide * shifted_by(start - 2)).astype(bf16)
-        volume[1] = (left_wide * shifted_by(start - 1)).astype(bf16)
-
-    def fill(t, moved):
-        for k in range(6):
-            plane = moved if k == 0 else shift_right(moved, k)
-            volume[2 + 6 * t + k] = (left_wide * plane).astype(bf16)
-        return shift_right(moved, 6)
-
-    lax.fori_loop(0, (plane_count + 2) // 6, fill, shifted_by(start))
-
-    @pl.when(disp == disp_size - 1)
-    def _():
-        volume[plane_count + 2 :] = jnp.zeros((2,) + volume.shape[1:], bf16)
-
-    hid_rows = hidden.shape[1]
-    first = first_ref[...]
-    first_bias = const_ref[0]
-
-    def conv_first(t, carry):
-        for window in range(hid_rows // 32):
-            block = volume[pl.ds(2 * t, 4), 32 * window : 32 * window + 64, :]
-            block = block.reshape(256, block.shape[2])
-            taps = jnp.dot(first, block, preferred_element_type=f32)
-            made = jnp.maximum(join_taps(taps) + first_bias, 0.0).astype(bf16)
-            hidden[pl.ds(2 * t, 2), 32 * window : 32 * window + 32, :] = made.reshape(
-                2, 32, made.shape[1]
-            )
-        return carry
-
-    lax.fori_loop(0, plane_count // 2 + 1, conv_first, 0, unroll=3)
-
-    @pl.when(disp == 0)
-    def _():
-        hidden[0] = jnp.zeros(hidden.shape[1:], bf16)
-
-    @pl.when(disp == disp_size - 1)
-    def _():
-        hidden[plane_count + 1] = jnp.zeros(hidden.shape[1:], bf16)
-
-    @pl.when(pix == 0)
-    def _():
-        hidden[:, :CH] = jnp.zeros((hidden.shape[0], CH, hidden.shape[2]), bf16)
-
-    @pl.when(pix == pix_size - 1)
-    def _():
-        hidden[:, hid_rows - CH :] = jnp.zeros((hidden.shape[0], CH, hidden.shape[2]), bf16)
+        return jnp.where(lane >= amount, pltpu.roll(right, amount, 1), 0.0).astype(bf16)
+
+    hid_rows, cols = hidden.shape[1:]
+    windows = hid_rows // 32
+    pair_count = plane_count // 2 + 1
+    state = [shifted_by(start)]
+
+    def fill(t):
+        if t == 0:
+            planes = [shifted_by(jnp.maximum(start - 2 + k, 0)) for k in range(2)]
+            planes = [jnp.where(disp > 0, plane, jnp.zeros_like(plane)) for plane in planes]
+        else:
+            base = state[-1]
+            step = 2 * ((t - 1) % 3)
+            planes = [base if step + k == 0 else shift_right(base, step + k) for k in range(2)]
+            if step == 4:
+                state.append(shift_right(base, 6))
+            if t == pair_count:
+                exists = disp < disp_size - 1
+                planes = [jnp.where(exists, plane, jnp.zeros_like(plane)) for plane in planes]
+        for k in range(2):
+            volume[2 * t + k] = left * planes[k]
+
+    block_row = lax.broadcasted_iota(jnp.int32, (first_ref.shape[0], 1), 0) // CH
+    live = [block_row >= 0 for _ in range(windows)]
+    live[0] = (pix > 0) | (block_row % 2 == 1)
+    live[-1] = live[-1] & ((pix < pix_size - 1) | (block_row % 2 == 0))
+    first = [jnp.where(keep, first_ref[...].astype(f32), 0.0).astype(bf16) for keep in live]
+    first_bias = [jnp.where(keep[:64], const_ref[0], 0.0) for keep in live]
+
+    def conv_first(t):
+        for window in range(windows):
+            block = volume[2 * t : 2 * t + 4, 32 * window : 32 * window + 64, :]
+            taps = jnp.dot(first[window], block.reshape(256, cols), preferred_element_type=f32)
+            made = jnp.maximum(join_taps(taps) + first_bias[window], 0.0)
+            halves = [made[:32], made[32:]]
+            if t == 0:
+                halves[0] = jnp.where(disp > 0, halves[0], 0.0)
+            if t == pair_count - 1:
+                halves[1] = jnp.where(disp < disp_size - 1, halves[1], 0.0)
+            for k in range(2):
+                hidden[2 * t + k, 32 * window : 32 * window + 32, :] = halves[k].astype(bf16)
 
     second = second_ref[...]
     second_bias = const_ref[1]
     head = const_ref[2]
-
-    def conv_second(t, carry):
-        block = hidden[pl.ds(2 * t, 4)]
-        block = block.reshape(256, block.shape[2])
-        taps = jnp.dot(second, block, preferred_element_type=f32)
+    partial = []
+
+    def conv_second(t):
+        block = hidden[2 * t : 2 * t + 4]
+        taps = jnp.dot(second, block.reshape(256, cols), preferred_element_type=f32)
         made = jnp.maximum(join_taps(taps) + second_bias, 0.0) * head
-        folded[t] = jnp.sum(made.reshape(8, 8, made.shape[1]), 0)
-        return carry
-
-    lax.fori_loop(0, plane_count // 2, conv_second, 0, unroll=4)
-
-    score = folded[...]
-    cols = score.shape[2]
-    score = score.reshape(-1, cols)
+        partial.append(jnp.sum(made.reshape(8, 8, cols), 0))
+
+    for t in range(pair_count + 1):
+        fill(t)
+    for t in range(pair_count):
+        conv_first(t)
+    for t in range(pair_count - 1):
+        conv_second(t)
+
     row8 = lax.broadcasted_iota(jnp.int32, (8, cols), 0)
     weight = jnp.zeros((8, cols), f32)
     moment = jnp.zeros((8, cols), f32)
     for t in range(plane_count // 2):
-        part = score[8 * t : 8 * t + 8]
+        part = partial[t]
         raw = part + pltpu.roll(part, 4, 0)
         expo = jnp.exp(-cost_scale * jnp.tanh(raw))
         plane = (start + 2 * t + (row8 // 2) % 2).astype(f32) / DSP
@@ -284,8 +276,8 @@
 
 def refine_kernel(
     own_ref,
-    pair_ref,
-    other_ref,
+    received_ref,
+    exchanged_ref,
     far_ref,
     swapped_ref,
     mix_ref,
@@ -297,9 +289,7 @@
     pix = lax.axis_index("pix")
     disp = lax.axis_index("disp")
     local = own_ref.shape[0]
-    even = pix % 2 == 0
-    above = jnp.where(even, other_ref[...], pair_ref[...])
-    below = jnp.where(even, pair_ref[...], other_ref[...])
+    above, below = sort_neighbours(received_ref[...], exchanged_ref[...], pix, disp, pix_size)
     first_core = disp == 0
     far_below = jnp.where(first_core, far_ref[...], swapped_ref[...])
     far_above = jnp.where(first_core, swapped_ref[...], far_ref[...])
@@ -325,37 +315,50 @@
     lanes = target.shape[1]
     global_row = lax.broadcasted_iota(jnp.int32, target.shape, 0) + (pix - 1) * out_rows
     row_inside = (global_row >= 0) & (global_row < pix_size * out_rows - 1)
-    lane_id = lax.broadcasted_iota(jnp.int32, target.shape, 1)
-    last_col = lane_id == lanes - 1
+    target = target * (dual_step / tv_bound)
     anchor = primal_step * conf * target
     scale = 1.0 / (1.0 + primal_step * conf)
-    both_steps = primal_step * dual_step
-    gain_y = jnp.where(row_inside, both_steps, 0.0)
-    gain_x = jnp.where(last_col, 0.0, both_steps)
-    bound = primal_step * tv_bound
+    keep_y = jnp.where(row_inside, 1.0, 0.0)
+    last_lane = lax.broadcasted_iota(jnp.int32, (fine, cols), 1) == cols - 1
     primal = target
     extrap = target
-    dual_x = jnp.zeros_like(target)
-    dual_y = jnp.zeros_like(target)
+    dual_x = None
     for _ in range(TV_ITERS):
-        downward = pltpu.roll(extrap, fine - 1, 0)
-        ahead = jnp.concatenate([extrap[:, cols:], shift_left(extrap[:, :cols])], 1)
-        trial_x = dual_x + gain_x * (ahead - extrap)
-        trial_y = dual_y + gain_y * (downward - extrap)
-        shrink = jnp.minimum(1.0, bound * lax.rsqrt(trial_x * trial_x + trial_y * trial_y))
+        trial_y = keep_y * (pltpu.roll(extrap, fine - 1, 0) - extrap)
+        wrapped = jnp.where(last_lane, extrap[:, lanes - cols :], shift_left(extrap[:, :cols]))
+        trial_x = jnp.concatenate([extrap[:, cols:], wrapped], 1) - extrap
+        if dual_x is not None:
+            trial_x = dual_x + trial_x
+            trial_y = dual_y + trial_y
+        shrink = lax.rsqrt(jnp.maximum(1.0, trial_x * trial_x + trial_y * trial_y))
         dual_x = trial_x * shrink
         dual_y = trial_y * shrink
         upper = pltpu.roll(dual_y, 1, 0)
         behind = jnp.concatenate([shift_right(dual_x[:, lanes - cols :]), dual_x[:, : lanes - cols]], 1)
-        updated = (primal + (dual_x - behind + dual_y - upper) + anchor) * scale
+        divergence = dual_x - behind + dual_y - upper
+        updated = (primal + (primal_step * dual_step) * divergence + anchor) * scale
         extrap = 2.0 * updated - primal
         primal = updated
+    primal = primal * (tv_bound / dual_step)
     kept = primal[out_rows : 2 * out_rows]
     out_ref[...] = interleave([kept[:, b * cols : (b + 1) * cols] for b in range(UP)])
 
 
-def pack_kernel(left_ref, right_ref, conf_ref, out_ref):
-    parts = [left_ref[...].astype(f32), right_ref[...].astype(f32), conf_ref[...]]
+def in_hbm(values):
+    return pltpu.with_memory_space_constraint(values, pltpu.HBM)
+
+
+def pack_kernel(left_ref, right_ref, conf_ref, out_ref, images, conf, sems):
+    copies = [
+        pltpu.make_async_copy(left_ref, images.at[0], sems.at[0]),
+        pltpu.make_async_copy(right_ref, images.at[1], sems.at[1]),
+        pltpu.make_async_copy(conf_ref, conf, sems.at[2]),
+    ]
+    for copy in copies:
+        copy.start()
+    for copy in copies:
+        copy.wait()
+    parts = [images[0].astype(f32), images[1].astype(f32), conf[...]]
     out_ref[...] = jnp.concatenate(parts, 0).astype(bf16)
 
 
@@ -391,11 +394,49 @@
     second_ref,
     const_ref,
     mask_ref,
+    weights,
+    sems,
 ):
-    taps = first_weight_ref.shape[0] ** 3 * CH
-    flat = [
-        transposed(ref[...].reshape(taps, CH)) for ref in (first_weight_ref, second_weight_ref)
+    copies = [
+        pltpu.make_async_copy(ref, weights.at[n], sems.at[n])
+        for n, ref in enumerate((first_weight_ref, second_weight_ref))
     ]
+    for copy in copies:
+        copy.start()
+
+    size = project_ref.shape[1]
+    groups = size // (UP * UP)
+    pixel = lax.broadcasted_iota(jnp.int32, (UP * UP, size), 0)
+    spot = lax.broadcasted_iota(jnp.int32, (UP * UP, size), 1)
+    expand = jnp.where(pixel == UP * (spot % UP) + spot // (UP * groups), 1.0, 0.0).astype(bf16)
+    own_group = lax.broadcasted_iota(jnp.int32, (size, size), 0) // CH
+    keep = own_group == (lax.broadcasted_iota(jnp.int32, (size, size), 1) // UP) % groups
+    for n, part in enumerate(split3(feat_ref[...])):
+        wide = jnp.dot(transposed(part), expand, preferred_element_type=f32)
+        wide = jnp.concatenate([wide] * groups, 0)
+        project_ref[size * n : size * n + size, :] = jnp.where(keep, wide, 0.0).astype(bf16)
+
+    kinds = mask_weight_ref.shape[1]
+    new = lax.broadcasted_iota(jnp.int32, (kinds, kinds), 0)
+    old = lax.broadcasted_iota(jnp.int32, (kinds, kinds), 1)
+    swapped = (new // (UP * UP)) * (UP * UP) + (new % UP) * UP + (new // UP) % UP
+    swapped = jnp.where(old == swapped, 1.0, 0.0).astype(bf16)
+    for n, part in enumerate(split3(mask_weight_ref[...])):
+        moved = lax.dot_general(
+            swapped, part, (((1,), (1,)), ((), ())), preferred_element_type=f32
+        )
+        mask_ref[kinds * n : kinds * n + kinds, :] = moved.astype(bf16)
+
+    index = lax.broadcasted_iota(jnp.int32, (64, 1), 0)
+    shape = const_ref.shape[1:]
+    const_ref[0] = jnp.broadcast_to(column(first_bias_ref[...], index % CH), shape)
+    const_ref[1] = jnp.broadcast_to(column(second_bias_ref[...], index // 4), shape)
+    const_ref[2] = jnp.broadcast_to(column(head_ref[...], index // 4), shape)
+
+    for copy in copies:
+        copy.wait()
+    taps = weights.shape[1] ** 3 * CH
+    flat = [transposed(weights[n].reshape(taps, CH)) for n in range(2)]
     flat = jnp.concatenate(flat, 0)
     source = lax.broadcasted_iota(jnp.int32, (taps, 256), 0)
     lane = lax.broadcasted_iota(jnp.int32, (1, 256), 1)
@@ -412,35 +453,6 @@
         first_ref[64 * tap : 64 * tap + 64, :] = blocks[0].astype(bf16)
         mixed = jnp.dot(regroup, blocks[1].astype(bf16), preferred_element_type=f32)
         second_ref[64 * tap : 64 * tap + 64, :] = mixed.astype(bf16)
-
-    size = project_ref.shape[1]
-    groups = size // (UP * UP)
-    pixel = lax.broadcasted_iota(jnp.int32, (UP * UP, size), 0)
-    spot = lax.broadcasted_iota(jnp.int32, (UP * UP, size), 1)
-    expand = jnp.where(pixel == UP * (spot % UP) + spot // (UP * groups), 1.0, 0.0).astype(bf16)
-    own_group = lax.broadcasted_iota(jnp.int32, (size, size), 0) // CH
-    keep = own_group == (lax.broadcasted_iota(jnp.int32, (size, size), 1) // UP) % groups
-    for n, part in enumerate(split3(feat_ref[...])):
-        wide = jnp.dot(transposed(part), expand, preferred_element_type=f32)
-        wide = jnp.concatenate([wide] * groups, 0)
-        project_ref[size * n : size * n + size, :] = jnp.where(keep, wide, 0.0).astype(bf16)
-
-    kinds = mask_weight_ref.shape[1]
-    new = lax.broadcasted_iota(jnp.int32, (kinds, kinds), 0)
-    old = lax.broadcasted_iota(jnp.int32, (kinds, kinds), 1)
-    swapped = (new // (UP * UP)) * (UP * UP) + (new % UP) * UP + (new // UP) % UP
-    swapped = jnp.where(old == swapped, 1.0, 0.0).astype(bf16)
-    for n, part in enumerate(split3(mask_weight_ref[...])):
-        moved = lax.dot_general(
-            swapped, part, (((1,), (1,)), ((), ())), preferred_element_type=f32
-        )
-        mask_ref[kinds * n : kinds * n + kinds, :] = moved.astype(bf16)
-
-    index = lax.broadcasted_iota(jnp.int32, (64, 1), 0)
-    shape = const_ref.shape[1:]
-    const_ref[0] = jnp.broadcast_to(column(first_bias_ref[...], index % CH), shape)
-    const_ref[1] = jnp.broadcast_to(column(second_bias_ref[...], index // 4), shape)
-    const_ref[2] = jnp.broadcast_to(column(head_ref[...], index // 4), shape)
 
 
 def local(
@@ -464,8 +476,7 @@
     local_rows = fine // UP
     plane_count = DSP // disp_size
     swap = [(d, d ^ 1) for d in range(disp_size)]
-    pairs = involution([(i, i + 1) for i in range(0, pix_size - 1, 2)], pix_size, disp_size)
-    others = involution([(i, i + 1) for i in range(1, pix_size - 1, 2)], pix_size, disp_size)
+    neighbours = mixed_exchange(pix_size, disp_size)
     far = []
     taken = set()
     for i in range(pix_size - 2):
@@ -478,16 +489,21 @@
     far = sorted(far)
 
     vmem = pl.BlockSpec(memory_space=pltpu.VMEM)
+    hbm = pl.BlockSpec(memory_space=pltpu.HBM)
     packed = pl.pallas_call(
         pack_kernel,
         out_shape=jax.ShapeDtypeStruct((3 * fine, width), bf16),
-        in_specs=[vmem] * 3,
+        in_specs=[hbm] * 3,
         out_specs=vmem,
+        scratch_shapes=[
+            pltpu.VMEM((2, fine, width), left_image.dtype),
+            pltpu.VMEM((fine, width), f32),
+            pltpu.SemaphoreType.DMA((3,)),
+        ],
         compiler_params=pltpu.CompilerParams(vmem_limit_bytes=2 * 2**20),
         name="pack",
-    )(left_image, right_image, confidence)
-    from_pair = lax.ppermute(packed, both, pairs)
-    from_other = lax.ppermute(packed, both, others)
+    )(in_hbm(left_image), in_hbm(right_image), in_hbm(confidence))
+    received = lax.ppermute(packed, both, neighbours)
 
     groups = 6 * local_rows
     kinds = mask_weight.shape[1]
@@ -500,19 +516,27 @@
             jax.ShapeDtypeStruct((3, 64, cols), f32),
             jax.ShapeDtypeStruct((3 * kinds, CH), bf16),
         ),
-        in_specs=[vmem] * 7,
+        in_specs=[vmem, hbm, vmem, hbm, vmem, vmem, vmem],
         out_specs=(vmem,) * 5,
+        scratch_shapes=[
+            pltpu.VMEM((2,) + first_weight.shape, bf16),
+            pltpu.SemaphoreType.DMA((2,)),
+        ],
         compiler_params=pltpu.CompilerParams(vmem_limit_bytes=8 * 2**20),
         name="prepare",
     )(
         feat_weight,
-        first_weight,
+        in_hbm(first_weight),
         first_bias,
-        second_weight,
+        in_hbm(second_weight),
         second_bias,
         head_weight,
         mask_weight,
     )
+    received, project, first, second, consts, mask3 = lax.optimization_barrier(
+        (received, project, first, second, consts, mask3)
+    )
+    exchanged = lax.ppermute(received, "disp", swap)
     total, left, conf = pl.pallas_call(
         functools.partial(score_kernel, pix_size=pix_size, disp_size=disp_size),
         out_shape=(
@@ -525,18 +549,17 @@
         scratch_shapes=[
             pltpu.VMEM((plane_count + 4, 3 * local_rows * CH, cols), bf16),
             pltpu.VMEM((plane_count + 2, (local_rows + 2) * CH, cols), bf16),
-            pltpu.VMEM((plane_count // 2, 8, cols), f32),
         ],
         compiler_params=pltpu.CompilerParams(vmem_limit_bytes=16 * 2**20),
         name="score",
-    )(packed, from_pair, from_other, project, first, second, consts)
+    )(packed, received, exchanged, project, first, second, consts)
 
     total = total[:4]
     summed = total + lax.ppermute(total, "disp", swap)
     coarse = summed[local_rows:] / summed[:local_rows]
+    received = lax.ppermute(coarse, both, neighbours)
     far_rows = lax.ppermute(coarse, both, far)
-    from_pair = lax.ppermute(coarse, both, pairs)
-    from_other = lax.ppermute(coarse, both, others)
+    exchanged = lax.ppermute(received, "disp", swap)
     swapped = lax.ppermute(far_rows, "disp", swap)
     mix = pl.pallas_call(
         mixing_kernel,
@@ -553,7 +576,7 @@
         out_specs=vmem,
         compiler_params=pltpu.CompilerParams(vmem_limit_bytes=8 * 2**20),
         name="refine",
-    )(coarse, from_pair, from_other, far_rows, swapped, mix, conf)
+    )(coarse, received, exchanged, far_rows, swapped, mix, conf)
     return (coarse, refined)
 
 

time: 31.3 us -> 22.3 us (0.71)
  Pallas kernels: 15.6 us -> 9.85 us
  local copies, waits for them, and re-layouts: 3.22 us -> 0.03 us
  waiting for transfers between devices: 2.14 us -> 4.79 us
  starting transfers between devices: 9.24 us -> 6.66 us
    pallas_call x1, Pallas kernels: 11.3 us -> 4.02 us  [local(): pl.pallas_call(functools.partial(score_kernel, pix_size=pix_size, disp_si...]
    unnamed x22 -> x12, local copies, waits for them, and re-layouts: 3.22 us -> 0.03 us
    ppermute x4, starting transfers between devices: 7.62 us -> 5.48 us  [the longest x1 3.05 us: local(): received = lax.ppermute(packed, both, neighbours)]
    ppermute x1, waiting for transfers between devices: 0.01 us -> 1.62 us  [local(): far_rows = lax.ppermute(coarse, both, far)]
    pallas_call x1, Pallas kernels: 0.01 us -> 0.85 us  [local(): pl.pallas_call(pack_kernel, out_shape=jax.ShapeDtypeStruct((3 * fine, wid...]
    pallas_call x1, Pallas kernels: 1.35 us -> 2.04 us  [local(): pl.pallas_call(prepare_kernel, out_shape=(jax.ShapeDtypeStruct((3 * group...]
    ppermute x4, waiting for transfers between devices: 0.98 us -> 1.58 us  [the longest x2 1.22 us: local(): exchanged = lax.ppermute(received, 'disp', swap)]
    ppermute x1, starting transfers between devices: 1.54 us -> 0.95 us  [local(): far_rows = lax.ppermute(coarse, both, far)]
  transfers between devices with their start and end apart: 7 -> 7, of which waited for: 2 -> 5; matrix products, arithmetic and copies ran while one was open for 0% -> 0% of each run, Pallas kernels for 6% -> 12%
where the time goes in v3:
time: 22.3 us; the launch traced here: 22.1 us
  Pallas kernels  9.85 us (44%)
  starting transfers between devices  6.66 us (30%)
  waiting for transfers between devices  4.79 us (21%)
  between operations  0.76 us (3%)
    pallas_call x1, Pallas kernels, local(): pl.pallas_call(functools.partial(score_kernel, pix_size=pix_size, disp_si...  4.02 us
    ppermute x1, starting transfers between devices, local(): received = lax.ppermute(packed, both, neighbours)  3.05 us
    pallas_call x1, Pallas kernels, local(): pl.pallas_call(functools.partial(refine_kernel, pix_size=pix_size), out_s...  2.38 us
    ppermute x1, starting transfers between devices, local(): received = lax.ppermute(coarse, both, neighbours)  2.29 us
    pallas_call x1, Pallas kernels, local(): pl.pallas_call(prepare_kernel, out_shape=(jax.ShapeDtypeStruct((3 * group...  2.04 us
    ppermute x1, waiting for transfers between devices, local(): far_rows = lax.ppermute(coarse, both, far)  1.62 us
    ppermute x2, waiting for transfers between devices, local(): exchanged = lax.ppermute(received, 'disp', swap)  1.22 us
    ppermute x1, waiting for transfers between devices, local(): summed = total + lax.ppermute(total, 'disp', swap)  1.01 us
  transfers between devices with their start and end apart: 7, of which 5 were waited for; matrix products, arithmetic and copies ran while one was open for 0% of the time, Pallas kernels for 12%

profile of v3, /device:TPU:0, one launch (start us, length us, event | category | flops | bytes accessed | tf_op | source)
XLA Modules:
  0.0 22.1 jit_solution(4133013992728486609)
XLA Ops:
  0.6 0.0 copy-start.2
  0.6 0.0 copy-start.3
  0.7 0.0 copy-start.4
  0.7 0.0 copy-start.5
  0.7 0.0 copy-start
  0.7 0.9 %pack.1.own_ref = bf16[24,1024]{1,0:T(8,128)(2,1)S(1)} custom-call(s32[8,1024]{1,0:T(8,128)} %left_ref.1, s32[8,1024]{1,0:T(8,128)} %right_ref.1, f32[8,1024]{1,0:T(8,128)} %conf_ref.1), custom_call_target="tpu_custom_call" | custom-call | tf_op jit(solution)/shard_map/pack/pallas_call | solution.py:493
  1.5 3.0 %collective-permute-start = (bf16[24,1024]{1,0:T(8,128)(2,1)S(1)}, bf16[24,1024]{1,0:T(8,128)(2,1)S(1)}, u32[]{:S(2)}, u32[]{:S(2)}) collective-permute-start(bf16[24,1024]{1,0:T(8,128)(2,1)S(1)} %pack.1.own_ref), channel_id=1, source_target_pairs={{0,2},{1,0},{2,1},{3,5},{4,6},{5,3},{6,4},{7,9},{8,10},{9,7},{10,8... | collective-permute-start | bytes 147464 | tf_op jit(solution)/shard_map/ppermute | solution.py:506
  4.6 0.0 copy-done.2
  4.6 0.0 copy-done.3
  4.6 0.0 copy-done.4
  4.6 0.0 copy-done.5
  4.6 0.0 copy-done
  4.6 2.0 %prepare.1 = (bf16[576,192]{1,0:T(8,128)(2,1)S(1)}, bf16[192,256]{1,0:T(8,128)(2,1)S(1)}, bf16[192,256]{1,0:T(8,128)(2,1)S(1)}, f32[3,64,256]{2,1,0:T(8,128)S(1)}, bf16[432,16]{1,0:T(8,128)(2,1)S(1)}) custom-call(f32[16,16]{1,0:T(8,128)S(1)} %copy-done.2, bf16[3,3,3,16,16]{4,3,2,1,0:T(8,128)(2,1)} %first_weight_ref.1, f32[16]{0:T(128)S(1)} %copy-done.3, ...), custom_call_target="tpu_custom_call" | custom-call | tf_op jit(solution)/shard_map/prepare/pallas_call | solution.py:510
  6.7 0.0 collective-permute-done.received_ref
  6.7 0.1 collective-permute-start.1
  6.8 1.2 %collective-permute-done.1.exchanged_ref = bf16[24,1024]{1,0:T(8,128)(2,1)S(1)} collective-permute-done((bf16[24,1024]{1,0:T(8,128)(2,1)S(1)}, bf16[24,1024]{1,0:T(8,128)(2,1)S(1)}, u32[]{:S(2)}, u32[]{:S(2)}) %collective-permute-start.1) | collective-permute-done | bytes 49184 | tf_op jit(solution)/shard_map/ppermute | solution.py:539
  8.0 4.0 %score.1 = (f32[8,256]{1,0:T(8,128)S(1)}, bf16[96,256]{1,0:T(8,128)(2,1)S(1)}, f32[24,1024]{1,0:T(8,128)S(1)}) custom-call(bf16[24,1024]{1,0:T(8,128)(2,1)S(1)} %pack.1.own_ref, bf16[24,1024]{1,0:T(8,128)(2,1)S(1)} %collective-permute-done.received_ref, bf16[24,1024]{1,0:T(8,128)(2,1)S(1)} %collective-permute-done.1.exchanged_ref, ...), custom_call_target="tpu_custom_call" | custom-call | tf_op jit(solution)/shard_map/score/pallas_call | solution.py:540
  12.0 0.2 %collective-permute-start.2 = (f32[4,256]{1,0:T(4,128)S(1)}, f32[4,256]{1,0:T(4,128)S(1)}, u32[]{:S(2)}, u32[]{:S(2)}) collective-permute-start(f32[4,256]{1,0:T(4,128)S(1)} %slice.9), channel_id=1, source_target_pairs={{0,1},{1,0},{2,3},{3,2},{4,5},{5,4},{6,7},{7,6},{8,9},{9,8},{10,11... | collective-permute-start | bytes 12296 | tf_op jit(solution)/shard_map/ppermute | solution.py:558
  12.2 1.0 %collective-permute-done.2 = f32[4,256]{1,0:T(4,128)S(1)} collective-permute-done((f32[4,256]{1,0:T(4,128)S(1)}, f32[4,256]{1,0:T(4,128)S(1)}, u32[]{:S(2)}, u32[]{:S(2)}) %collective-permute-start.2) | collective-permute-done | bytes 4128 | tf_op jit(solution)/shard_map/ppermute | solution.py:558
  13.2 0.0 copy-start.1
  13.3 2.3 %collective-permute-start.3 = (f32[2,256]{1,0:T(2,128)S(1)}, f32[2,256]{1,0:T(2,128)S(1)}, u32[]{:S(2)}, u32[]{:S(2)}) collective-permute-start(f32[2,256]{1,0:T(2,128)S(1)} %slice_divide_fusion.own_ref), channel_id=1, source_target_pairs={{0,2},{1,0},{2,1},{3,5},{4,6},{5,3},{6,4},{7,9},{8,10},{9,7},{10,8... | collective-permute-start | bytes 6152 | tf_op jit(solution)/shard_map/ppermute | solution.py:560
  15.5 1.0 %collective-permute-start.5 = (f32[2,256]{1,0:T(2,128)S(1)}, f32[2,256]{1,0:T(2,128)S(1)}, u32[]{:S(2)}, u32[]{:S(2)}) collective-permute-start(f32[2,256]{1,0:T(2,128)S(1)} %slice_divide_fusion.own_ref), channel_id=1, source_target_pairs={{0,5},{1,3},{2,7},{3,1},{4,9},{5,0},{6,11},{7,2},{8,13},{9,4},{10,... | collective-permute-start | bytes 6152 | tf_op jit(solution)/shard_map/ppermute | solution.py:561
  16.5 0.4 %collective-permute-done.3.received_ref = f32[2,256]{1,0:T(2,128)S(1)} collective-permute-done((f32[2,256]{1,0:T(2,128)S(1)}, f32[2,256]{1,0:T(2,128)S(1)}, u32[]{:S(2)}, u32[]{:S(2)}) %collective-permute-start.3) | collective-permute-done | bytes 2080 | tf_op jit(solution)/shard_map/ppermute | solution.py:560
  16.9 0.1 collective-permute-start.4
  16.9 1.6 %collective-permute-done.5.far_ref = f32[2,256]{1,0:T(2,128)S(1)} collective-permute-done((f32[2,256]{1,0:T(2,128)S(1)}, f32[2,256]{1,0:T(2,128)S(1)}, u32[]{:S(2)}, u32[]{:S(2)}) %collective-permute-start.5) | collective-permute-done | bytes 2080 | tf_op jit(solution)/shard_map/ppermute | solution.py:561
  18.6 0.0 collective-permute-start.6
  18.6 0.6 %mixing.1.mix_ref = f32[6,144,256]{2,1,0:T(8,128)S(1)} custom-call(bf16[96,256]{1,0:T(8,128)(2,1)S(1)} %get-tuple-element.27.left_ref, bf16[432,16]{1,0:T(8,128)(2,1)S(1)} %get-tuple-element.28.mask_ref), custom_call_target="tpu_custom_call" | custom-call | tf_op jit(solution)/shard_map/mixing/pallas_call | solution.py:564
  19.1 0.0 collective-permute-done.4.exchanged_ref
  19.1 0.6 %collective-permute-done.6.swapped_ref = f32[2,256]{1,0:T(2,128)S(1)} collective-permute-done((f32[2,256]{1,0:T(2,128)S(1)}, f32[2,256]{1,0:T(2,128)S(1)}, u32[]{:S(2)}, u32[]{:S(2)}) %collective-permute-start.6) | collective-permute-done | bytes 2080 | tf_op jit(solution)/shard_map/ppermute | solution.py:563
  19.7 0.0 copy-done.1
  19.7 2.4 %refine.1 = f32[8,1024]{1,0:T(8,128)} custom-call(f32[2,256]{1,0:T(2,128)S(1)} %slice_divide_fusion.own_ref, f32[2,256]{1,0:T(2,128)S(1)} %collective-permute-done.3.received_ref, f32[2,256]{1,0:T(2,128)S(1)} %collective-permute-done.4.exchanged_ref, f32[2,256]{1,0:T(2,128)S(1)} %collective-permute-done.5.far_ref, ...), custom_call_target="tpu_custom_call" | custom-call | tf_op jit(solution)/shard_map/refine/pallas_call | solution.py:572
  (3 shorter events, 0.0 us)
Async XLA Ops:
  0.6 4.0 %copy-start.2 = (f32[16,16]{1,0:T(8,128)S(1)}, f32[16,16]{1,0:T(8,128)}, u32[]{:S(2)}) copy-start(f32[16,16]{1,0:T(8,128)} %feat_ref.1) | copy-start | bytes 3076
  0.6 4.0 %copy-start.3 = (f32[16]{0:T(128)S(1)}, f32[16]{0:T(128)}, u32[]{:S(2)}) copy-start(f32[16]{0:T(128)} %first_bias_ref.1) | copy-start | bytes 196
  0.7 3.9 %copy-start.4 = (f32[16]{0:T(128)S(1)}, f32[16]{0:T(128)}, u32[]{:S(2)}) copy-start(f32[16]{0:T(128)} %second_bias_ref.1) | copy-start | bytes 196
  0.7 3.9 %copy-start.5 = (f32[16]{0:T(128)S(1)}, f32[16]{0:T(128)}, u32[]{:S(2)}) copy-start(f32[16]{0:T(128)} %head_ref.1) | copy-start | bytes 196
  0.7 3.9 %copy-start = (f32[16,144]{1,0:T(8,128)S(1)}, f32[16,144]{1,0:T(8,128)}, u32[]{:S(2)}) copy-start(f32[16,144]{1,0:T(8,128)} %mask_weight_ref.1) | copy-start | bytes 27652
  1.5 5.1 %collective-permute-start = (bf16[24,1024]{1,0:T(8,128)(2,1)S(1)}, bf16[24,1024]{1,0:T(8,128)(2,1)S(1)}, u32[]{:S(2)}, u32[]{:S(2)}) collective-permute-start(bf16[24,1024]{1,0:T(8,128)(2,1)S(1)} %pack.1.own_ref), channel_id=1, source_target_pairs={{0,2},{1,0},{2,1},{3,5},{4,6},{5,3},{6,4},{7,9},{8,10},{9,7},{10,8... | collective-permute-start | bytes 147464 | tf_op jit(solution)/shard_map/ppermute | solution.py:506
  6.7 1.3 %collective-permute-start.1 = (bf16[24,1024]{1,0:T(8,128)(2,1)S(1)}, bf16[24,1024]{1,0:T(8,128)(2,1)S(1)}, u32[]{:S(2)}, u32[]{:S(2)}) collective-permute-start(bf16[24,1024]{1,0:T(8,128)(2,1)S(1)} %collective-permute-done.received_ref), channel_id=1, source_target_pairs={{0,1},{1,0},{2,3},{3,2},{4,5},{5,4},{6,7},{7,6},{8,9},{9,8},{10,11... | collective-permute-start | bytes 147464 | tf_op jit(solution)/shard_map/ppermute | solution.py:539
  12.0 1.2 %collective-permute-start.2 = (f32[4,256]{1,0:T(4,128)S(1)}, f32[4,256]{1,0:T(4,128)S(1)}, u32[]{:S(2)}, u32[]{:S(2)}) collective-permute-start(f32[4,256]{1,0:T(4,128)S(1)} %slice.9), channel_id=1, source_target_pairs={{0,1},{1,0},{2,3},{3,2},{4,5},{5,4},{6,7},{7,6},{8,9},{9,8},{10,11... | collective-permute-start | bytes 12296 | tf_op jit(solution)/shard_map/ppermute | solution.py:558
  13.2 6.5 %copy-start.1 = (f32[2,256]{1,0:T(2,128)}, f32[2,256]{1,0:T(2,128)S(1)}, u32[]{:S(2)}) copy-start(f32[2,256]{1,0:T(2,128)S(1)} %slice_divide_fusion.own_ref) | copy-start | bytes 6148
  13.3 3.6 %collective-permute-start.3 = (f32[2,256]{1,0:T(2,128)S(1)}, f32[2,256]{1,0:T(2,128)S(1)}, u32[]{:S(2)}, u32[]{:S(2)}) collective-permute-start(f32[2,256]{1,0:T(2,128)S(1)} %slice_divide_fusion.own_ref), channel_id=1, source_target_pairs={{0,2},{1,0},{2,1},{3,5},{4,6},{5,3},{6,4},{7,9},{8,10},{9,7},{10,8... | collective-permute-start | bytes 6152 | tf_op jit(solution)/shard_map/ppermute | solution.py:560
  15.5 3.0 %collective-permute-start.5 = (f32[2,256]{1,0:T(2,128)S(1)}, f32[2,256]{1,0:T(2,128)S(1)}, u32[]{:S(2)}, u32[]{:S(2)}) collective-permute-start(f32[2,256]{1,0:T(2,128)S(1)} %slice_divide_fusion.own_ref), channel_id=1, source_target_pairs={{0,5},{1,3},{2,7},{3,1},{4,9},{5,0},{6,11},{7,2},{8,13},{9,4},{10,... | collective-permute-start | bytes 6152 | tf_op jit(solution)/shard_map/ppermute | solution.py:561
  16.9 2.3 %collective-permute-start.4 = (f32[2,256]{1,0:T(2,128)S(1)}, f32[2,256]{1,0:T(2,128)S(1)}, u32[]{:S(2)}, u32[]{:S(2)}) collective-permute-start(f32[2,256]{1,0:T(2,128)S(1)} %collective-permute-done.3.received_ref), channel_id=1, source_target_pairs={{0,1},{1,0},{2,3},{3,2},{4,5},{5,4},{6,7},{7,6},{8,9},{9,8},{10,11... | collective-permute-start | bytes 6152 | tf_op jit(solution)/shard_map/ppermute | solution.py:562
  18.6 1.2 %collective-permute-start.6 = (f32[2,256]{1,0:T(2,128)S(1)}, f32[2,256]{1,0:T(2,128)S(1)}, u32[]{:S(2)}, u32[]{:S(2)}) collective-permute-start(f32[2,256]{1,0:T(2,128)S(1)} %collective-permute-done.5.far_ref), channel_id=1, source_target_pairs={{0,1},{1,0},{2,3},{3,2},{4,5},{5,4},{6,7},{7,6},{8,9},{9,8},{10,11... | collective-permute-start | bytes 6152 | tf_op jit(solution)/shard_map/ppermute | solution.py:563

commit v4 on v3

--- a/solution.py
+++ b/solution.py
@@ -19,6 +19,19 @@
 mask_scale = 3.0
 f32 = jnp.float32
 bf16 = jnp.bfloat16
+
+
+def involution(pairs, pix_size, disp_size):
+    perm = []
+    used = set()
+    for i, j in pairs:
+        used |= {i, j}
+        for d in range(disp_size):
+            perm += [(i * disp_size + d, j * disp_size + d), (j * disp_size + d, i * disp_size + d)]
+    for i in range(pix_size):
+        if i not in used:
+            perm += [(i * disp_size + d, i * disp_size + (d ^ 1)) for d in range(disp_size)]
+    return sorted(perm)
 
 
 def mixed_exchange(pix_size, disp_size):
@@ -56,7 +69,7 @@
     cols = lax.broadcasted_iota(jnp.int32, (256, 256), 1)
     if transposed:
         rows, cols = cols, rows
-    return jnp.where(rows == UP * (cols % 64) + cols // 64, 1.0, 0.0).astype(bf16)
+    return jnp.where(rows == UP * (cols & 63) + (cols >> 6), 1.0, 0.0).astype(bf16)
 
 
 def deinterleave(values):
@@ -83,25 +96,20 @@
 
 
 def interleave(phases):
-    perm = phase_matrix(True)
     rows = phases[0].shape[0]
     lane = lax.broadcasted_iota(jnp.int32, (rows, 128), 1)
-    outs = []
+    chunks = []
     for t in range(phases[0].shape[1] // 128):
         tiles = [phase[:, 128 * t : 128 * t + 128] for phase in phases]
         rolled = [pltpu.roll(tile, 64, 1) for tile in tiles]
-        for half in range(2):
-            if half == 0:
-                packed = [jnp.where(lane < 64, tiles[b], rolled[b + 1]) for b in (0, 2)]
-            else:
-                packed = [jnp.where(lane < 64, rolled[b], tiles[b + 1]) for b in (0, 2)]
-            packed = jnp.concatenate(packed, 1)
-            total = None
-            for part in split3(packed)[::-1]:
-                moved = jnp.dot(part, perm, preferred_element_type=f32)
-                total = moved if total is None else total + moved
-            outs.append(total)
-    return jnp.concatenate(outs, 1)
+        chunks.append([jnp.where(lane < 64, tiles[b], rolled[b + 1]) for b in (0, 2)])
+        chunks.append([jnp.where(lane < 64, rolled[b], tiles[b + 1]) for b in (0, 2)])
+    packed = jnp.concatenate([jnp.concatenate(chunk, 1) for chunk in chunks], 0)
+    size = packed.shape[0]
+    parts = jnp.concatenate(split3(packed), 0)
+    moved = jnp.dot(parts, phase_matrix(True), preferred_element_type=f32)
+    moved = (moved[2 * size :] + moved[size : 2 * size]) + moved[:size]
+    return jnp.concatenate([moved[rows * j : rows * j + rows] for j in range(len(chunks))], 1)
 
 
 def shift_right(values, amount=1):
@@ -148,9 +156,10 @@
     pix = lax.axis_index("pix")
     disp = lax.axis_index("disp")
     plane_count = DSP // disp_size
-    above, below = sort_neighbours(
-        received_ref[...].astype(f32), exchanged_ref[...].astype(f32), pix, disp, pix_size
-    )
+    even = pix % 2 == 0
+    pair, other = (received_ref[...].astype(f32), exchanged_ref[...].astype(f32))
+    above = jnp.where(even, other, pair)
+    below = jnp.where(even, pair, other)
     gathered = jnp.concatenate([above, own_ref[...].astype(f32), below], 0).astype(bf16)
     phases = deinterleave(gathered)
     fine = own_ref.shape[0] // 3
@@ -211,8 +220,8 @@
 
     block_row = lax.broadcasted_iota(jnp.int32, (first_ref.shape[0], 1), 0) // CH
     live = [block_row >= 0 for _ in range(windows)]
-    live[0] = (pix > 0) | (block_row % 2 == 1)
-    live[-1] = live[-1] & ((pix < pix_size - 1) | (block_row % 2 == 0))
+    live[0] = (pix > 0) | ((block_row & 1) == 1)
+    live[-1] = live[-1] & ((pix < pix_size - 1) | ((block_row & 1) == 0))
     first = [jnp.where(keep, first_ref[...].astype(f32), 0.0).astype(bf16) for keep in live]
     first_bias = [jnp.where(keep[:64], const_ref[0], 0.0) for keep in live]
 
@@ -250,25 +259,39 @@
     row8 = lax.broadcasted_iota(jnp.int32, (8, cols), 0)
     weight = jnp.zeros((8, cols), f32)
     moment = jnp.zeros((8, cols), f32)
-    for t in range(plane_count // 2):
-        part = partial[t]
-        raw = part + pltpu.roll(part, 4, 0)
+    upper = row8 < 4
+    for t in range(0, plane_count // 2, 2):
+        kept = jnp.where(upper, partial[t], partial[t + 1])
+        other = jnp.where(upper, partial[t + 1], partial[t])
+        raw = kept + pltpu.roll(other, 4, 0)
         expo = jnp.exp(-cost_scale * jnp.tanh(raw))
-        plane = (start + 2 * t + (row8 // 2) % 2).astype(f32) / DSP
+        plane = (start + 2 * t + (row8 >> 1)).astype(f32) / DSP
         weight = weight + expo
         moment = moment + expo * plane
-    weight = weight + pltpu.roll(weight, 2, 0)
-    moment = moment + pltpu.roll(moment, 2, 0)
-    total_ref[...] = jnp.where(row8 % 4 < 2, weight, moment)
-
-
-def mixing_kernel(left_ref, mask_ref, mix_ref):
+    for turn in (4, 2):
+        weight = weight + pltpu.roll(weight, turn, 0)
+        moment = moment + pltpu.roll(moment, turn, 0)
+    total_ref[...] = jnp.where((row8 & 3) < 2, weight, moment)
+
+
+def mixing_kernel(left_ref, mask_weight_ref, mix_ref):
     cols = left_ref.shape[1]
-    kinds = mask_ref.shape[0] // 3
+    kinds = mask_weight_ref.shape[1]
+    new = lax.broadcasted_iota(jnp.int32, (kinds, kinds), 0)
+    old = lax.broadcasted_iota(jnp.int32, (kinds, kinds), 1)
+    swapped = (new & ~15) + (new & 3) * UP + ((new >> 2) & 3)
+    swapped = jnp.where(old == swapped, 1.0, 0.0).astype(bf16)
+    mask = jnp.concatenate(
+        [
+            lax.dot_general(
+                swapped, part, (((1,), (1,)), ((), ())), preferred_element_type=f32
+            ).astype(bf16)
+            for part in split3(mask_weight_ref[...])
+        ],
+        0,
+    )
     for r in range(mix_ref.shape[0]):
-        logits3 = jnp.dot(
-            mask_ref[...], left_ref[CH * r : CH * r + CH, :], preferred_element_type=f32
-        )
+        logits3 = jnp.dot(mask, left_ref[CH * r : CH * r + CH, :], preferred_element_type=f32)
         logits = (logits3[2 * kinds :] + logits3[kinds : 2 * kinds]) + logits3[:kinds]
         expo = jnp.exp(mask_scale * jnp.tanh(logits)).reshape(9, UP * UP, cols)
         mix_ref[r] = (expo / jnp.sum(expo, 0)).reshape(kinds, cols)
@@ -388,12 +411,10 @@
     second_weight_ref,
     second_bias_ref,
     head_ref,
-    mask_weight_ref,
     project_ref,
     first_ref,
     second_ref,
     const_ref,
-    mask_ref,
     weights,
     sems,
 ):
@@ -416,17 +437,6 @@
         wide = jnp.concatenate([wide] * groups, 0)
         project_ref[size * n : size * n + size, :] = jnp.where(keep, wide, 0.0).astype(bf16)
 
-    kinds = mask_weight_ref.shape[1]
-    new = lax.broadcasted_iota(jnp.int32, (kinds, kinds), 0)
-    old = lax.broadcasted_iota(jnp.int32, (kinds, kinds), 1)
-    swapped = (new // (UP * UP)) * (UP * UP) + (new % UP) * UP + (new // UP) % UP
-    swapped = jnp.where(old == swapped, 1.0, 0.0).astype(bf16)
-    for n, part in enumerate(split3(mask_weight_ref[...])):
-        moved = lax.dot_general(
-            swapped, part, (((1,), (1,)), ((), ())), preferred_element_type=f32
-        )
-        mask_ref[kinds * n : kinds * n + kinds, :] = moved.astype(bf16)
-
     index = lax.broadcasted_iota(jnp.int32, (64, 1), 0)
     shape = const_ref.shape[1:]
     const_ref[0] = jnp.broadcast_to(column(first_bias_ref[...], index % CH), shape)
@@ -440,10 +450,10 @@
     flat = jnp.concatenate(flat, 0)
     source = lax.broadcasted_iota(jnp.int32, (taps, 256), 0)
     lane = lax.broadcasted_iota(jnp.int32, (1, 256), 1)
-    plane, row, chan = (lane // 64, (lane // CH) % 4, lane % CH)
+    plane, row, chan = (lane >> 6, (lane >> 4) & 3, lane & 15)
     out_row = lax.broadcasted_iota(jnp.int32, (64, 64), 0)
     out_col = lax.broadcasted_iota(jnp.int32, (64, 64), 1)
-    regroup = jnp.where(out_col == (out_row % 4) * CH + out_row // 4, 1.0, 0.0).astype(bf16)
+    regroup = jnp.where(out_col == (out_row & 3) * CH + (out_row >> 2), 1.0, 0.0).astype(bf16)
     for tap in range(3):
         wanted = jnp.where((plane < 3) & (row < 3), ((plane * 3 + row) * 3 + tap) * CH + chan, -1)
         select = jnp.where(source == wanted, 1.0, 0.0).astype(bf16)
@@ -477,6 +487,8 @@
     plane_count = DSP // disp_size
     swap = [(d, d ^ 1) for d in range(disp_size)]
     neighbours = mixed_exchange(pix_size, disp_size)
+    pairs = involution([(i, i + 1) for i in range(0, pix_size - 1, 2)], pix_size, disp_size)
+    others = involution([(i, i + 1) for i in range(1, pix_size - 1, 2)], pix_size, disp_size)
     far = []
     taken = set()
     for i in range(pix_size - 2):
@@ -503,21 +515,20 @@
         compiler_params=pltpu.CompilerParams(vmem_limit_bytes=2 * 2**20),
         name="pack",
     )(in_hbm(left_image), in_hbm(right_image), in_hbm(confidence))
-    received = lax.ppermute(packed, both, neighbours)
+    from_pair = lax.ppermute(packed, both, pairs)
+    from_other = lax.ppermute(packed, both, others)
 
     groups = 6 * local_rows
-    kinds = mask_weight.shape[1]
-    project, first, second, consts, mask3 = pl.pallas_call(
+    project, first, second, consts = pl.pallas_call(
         prepare_kernel,
         out_shape=(
             jax.ShapeDtypeStruct((3 * groups * CH, groups * UP * UP), bf16),
             jax.ShapeDtypeStruct((192, 256), bf16),
             jax.ShapeDtypeStruct((192, 256), bf16),
             jax.ShapeDtypeStruct((3, 64, cols), f32),
-            jax.ShapeDtypeStruct((3 * kinds, CH), bf16),
         ),
-        in_specs=[vmem, hbm, vmem, hbm, vmem, vmem, vmem],
-        out_specs=(vmem,) * 5,
+        in_specs=[vmem, hbm, vmem, hbm, vmem, vmem],
+        out_specs=(vmem,) * 4,
         scratch_shapes=[
             pltpu.VMEM((2,) + first_weight.shape, bf16),
             pltpu.SemaphoreType.DMA((2,)),
@@ -531,12 +542,7 @@
         in_hbm(second_weight),
         second_bias,
         head_weight,
-        mask_weight,
-    )
-    received, project, first, second, consts, mask3 = lax.optimization_barrier(
-        (received, project, first, second, consts, mask3)
-    )
-    exchanged = lax.ppermute(received, "disp", swap)
+    )
     total, left, conf = pl.pallas_call(
         functools.partial(score_kernel, pix_size=pix_size, disp_size=disp_size),
         out_shape=(
@@ -552,7 +558,7 @@
         ],
         compiler_params=pltpu.CompilerParams(vmem_limit_bytes=16 * 2**20),
         name="score",
-    )(packed, received, exchanged, project, first, second, consts)
+    )(packed, from_pair, from_other, project, first, second, consts)
 
     total = total[:4]
     summed = total + lax.ppermute(total, "disp", swap)
@@ -568,7 +574,7 @@
         out_specs=vmem,
         compiler_params=pltpu.CompilerParams(vmem_limit_bytes=4 * 2**20),
         name="mixing",
-    )(left, mask3)
+    )(left, mask_weight)
     refined = pl.pallas_call(
         functools.partial(refine_kernel, pix_size=pix_size),
         out_shape=jax.ShapeDtypeStruct((fine, width), f32),

time: 22.3 us -> 21.8 us (0.978)
  waiting for transfers between devices: 4.79 us -> 2.68 us
  starting transfers between devices: 6.66 us -> 8.33 us
    ppermute x1, waiting for transfers between devices: 1.62 us -> 0.01 us  [local(): far_rows = lax.ppermute(coarse, both, far)]
    ppermute x1 -> x2, starting transfers between devices: 3.05 us -> 4.58 us  [the longest x1 4.02 us: local(): from_pair = lax.ppermute(packed, both, pairs)]
    ppermute x2 -> x1, waiting for transfers between devices: 1.22 us -> 0.2 us  [local(): exchanged = lax.ppermute(received, 'disp', swap)]
    ppermute x1, waiting for transfers between devices: 0.36 us -> 1.3 us  [local(): received = lax.ppermute(coarse, both, neighbours)]
    ppermute x1, starting transfers between devices: 0.95 us -> 1.82 us  [local(): far_rows = lax.ppermute(coarse, both, far)]
    ppermute x1, starting transfers between devices: 2.29 us -> 1.62 us  [local(): received = lax.ppermute(coarse, both, neighbours)]
    ppermute x1, waiting for transfers between devices: 0.58 us -> 0.01 us  [local(): swapped = lax.ppermute(far_rows, 'disp', swap)]
  transfers between devices with their start and end apart: 7 -> 7, of which waited for: 5 -> 3; matrix products, arithmetic and copies ran while one was open for 0% -> 0% of each run, Pallas kernels for 12% -> 13%
where the time goes in v4:
time: 21.8 us; the launch traced here: 21.6 us
  Pallas kernels  9.77 us (45%)
  starting transfers between devices  8.33 us (38%)
  waiting for transfers between devices  2.68 us (12%)
  between operations  0.75 us (3%)
    ppermute x1, starting transfers between devices, local(): from_pair = lax.ppermute(packed, both, pairs)  4.02 us
    pallas_call x1, Pallas kernels, local(): pl.pallas_call(functools.partial(score_kernel, pix_size=pix_size, disp_si...  3.99 us
    pallas_call x1, Pallas kernels, local(): pl.pallas_call(functools.partial(refine_kernel, pix_size=pix_size), out_s...  2.22 us
    pallas_call x1, Pallas kernels, local(): pl.pallas_call(prepare_kernel, out_shape=(jax.ShapeDtypeStruct((3 * group...  2.02 us
    ppermute x1, starting transfers between devices, local(): far_rows = lax.ppermute(coarse, both, far)  1.82 us
    ppermute x1, starting transfers between devices, local(): received = lax.ppermute(coarse, both, neighbours)  1.62 us
    ppermute x1, waiting for transfers between devices, local(): received = lax.ppermute(coarse, both, neighbours)  1.3 us
    ppermute x1, waiting for transfers between devices, local(): summed = total + lax.ppermute(total, 'disp', swap)  1.15 us
  transfers between devices with their start and end apart: 7, of which 3 were waited for; matrix products, arithmetic and copies ran while one was open for 0% of the time, Pallas kernels for 13%

profile of v4, /device:TPU:0, one launch (start us, length us, event | category | flops | bytes accessed | tf_op | source)
XLA Modules:
  0.0 21.6 jit_solution(17364215897172463915)
XLA Ops:
  0.6 0.0 copy-start.5
  0.6 0.0 copy-start.4
  0.7 0.0 copy-start.3
  0.7 0.0 copy-start.2
  0.7 0.8 %pack.1.own_ref = bf16[24,1024]{1,0:T(8,128)(2,1)S(1)} custom-call(s32[8,1024]{1,0:T(8,128)} %left_ref.1, s32[8,1024]{1,0:T(8,128)} %right_ref.1, f32[8,1024]{1,0:T(8,128)} %conf_ref.1), custom_call_target="tpu_custom_call" | custom-call | tf_op jit(solution)/shard_map/pack/pallas_call | solution.py:505
  1.5 0.6 %collective-permute-start.1 = (bf16[24,1024]{1,0:T(8,128)(2,1)S(1)}, bf16[24,1024]{1,0:T(8,128)(2,1)S(1)}, u32[]{:S(2)}, u32[]{:S(2)}) collective-permute-start(bf16[24,1024]{1,0:T(8,128)(2,1)S(1)} %pack.1.own_ref), channel_id=1, source_target_pairs={{0,1},{1,0},{2,4},{3,5},{4,2},{5,3},{6,8},{7,9},{8,6},{9,7},{10,12... | collective-permute-start | bytes 147464 | tf_op jit(solution)/shard_map/ppermute | solution.py:519
  2.1 4.0 %collective-permute-start = (bf16[24,1024]{1,0:T(8,128)(2,1)S(1)}, bf16[24,1024]{1,0:T(8,128)(2,1)S(1)}, u32[]{:S(2)}, u32[]{:S(2)}) collective-permute-start(bf16[24,1024]{1,0:T(8,128)(2,1)S(1)} %pack.1.own_ref), channel_id=1, source_target_pairs={{0,2},{1,3},{2,0},{3,1},{4,6},{5,7},{6,4},{7,5},{8,10},{9,11},{10,... | collective-permute-start | bytes 147464 | tf_op jit(solution)/shard_map/ppermute | solution.py:518
  6.1 0.0 copy-done.5
  6.1 0.0 copy-done.4
  6.1 0.0 copy-done.3
  6.1 0.0 copy-done.2
  6.1 2.0 %prepare.1 = (bf16[576,192]{1,0:T(8,128)(2,1)S(1)}, bf16[192,256]{1,0:T(8,128)(2,1)S(1)}, bf16[192,256]{1,0:T(8,128)(2,1)S(1)}, f32[3,64,256]{2,1,0:T(8,128)S(1)}) custom-call(f32[16,16]{1,0:T(8,128)S(1)} %copy-done.2, bf16[3,3,3,16,16]{4,3,2,1,0:T(8,128)(2,1)} %first_weight_ref.1, f32[16]{0:T(128)S(1)} %copy-done.3, ...), custom_call_target="tpu_custom_call" | custom-call | tf_op jit(solution)/shard_map/prepare/pallas_call | solution.py:522
  8.1 0.0 collective-permute-done.1.exchanged_ref
  8.2 0.0 collective-permute-done.received_ref
  8.2 4.0 %score.1 = (f32[8,256]{1,0:T(8,128)S(1)}, bf16[96,256]{1,0:T(8,128)(2,1)S(1)}, f32[24,1024]{1,0:T(8,128)S(1)}) custom-call(bf16[24,1024]{1,0:T(8,128)(2,1)S(1)} %pack.1.own_ref, bf16[24,1024]{1,0:T(8,128)(2,1)S(1)} %collective-permute-done.received_ref, bf16[24,1024]{1,0:T(8,128)(2,1)S(1)} %collective-permute-done.1.exchanged_ref, ...), custom_call_target="tpu_custom_call" | custom-call | tf_op jit(solution)/shard_map/score/pallas_call | solution.py:546
  12.2 0.0 copy-start
  12.2 0.1 collective-permute-start.2
  12.3 1.2 %collective-permute-done.2 = f32[4,256]{1,0:T(4,128)S(1)} collective-permute-done((f32[4,256]{1,0:T(4,128)S(1)}, f32[4,256]{1,0:T(4,128)S(1)}, u32[]{:S(2)}, u32[]{:S(2)}) %collective-permute-start.2) | collective-permute-done | bytes 4128 | tf_op jit(solution)/shard_map/ppermute | solution.py:564
  13.4 0.0 copy-start.1
  13.4 1.8 %collective-permute-start.5 = (f32[2,256]{1,0:T(2,128)S(1)}, f32[2,256]{1,0:T(2,128)S(1)}, u32[]{:S(2)}, u32[]{:S(2)}) collective-permute-start(f32[2,256]{1,0:T(2,128)S(1)} %slice_divide_fusion.own_ref), channel_id=1, source_target_pairs={{0,5},{1,3},{2,7},{3,1},{4,9},{5,0},{6,11},{7,2},{8,13},{9,4},{10,... | collective-permute-start | bytes 6152 | tf_op jit(solution)/shard_map/ppermute | solution.py:567
  15.3 1.6 %collective-permute-start.3 = (f32[2,256]{1,0:T(2,128)S(1)}, f32[2,256]{1,0:T(2,128)S(1)}, u32[]{:S(2)}, u32[]{:S(2)}) collective-permute-start(f32[2,256]{1,0:T(2,128)S(1)} %slice_divide_fusion.own_ref), channel_id=1, source_target_pairs={{0,2},{1,0},{2,1},{3,5},{4,6},{5,3},{6,4},{7,9},{8,10},{9,7},{10,8... | collective-permute-start | bytes 6152 | tf_op jit(solution)/shard_map/ppermute | solution.py:566
  16.9 0.0 collective-permute-done.5.far_ref
  16.9 0.0 collective-permute-start.6
  16.9 1.3 %collective-permute-done.3.received_ref = f32[2,256]{1,0:T(2,128)S(1)} collective-permute-done((f32[2,256]{1,0:T(2,128)S(1)}, f32[2,256]{1,0:T(2,128)S(1)}, u32[]{:S(2)}, u32[]{:S(2)}) %collective-permute-start.3) | collective-permute-done | bytes 2080 | tf_op jit(solution)/shard_map/ppermute | solution.py:566
  18.2 0.2 %collective-permute-start.4 = (f32[2,256]{1,0:T(2,128)S(1)}, f32[2,256]{1,0:T(2,128)S(1)}, u32[]{:S(2)}, u32[]{:S(2)}) collective-permute-start(f32[2,256]{1,0:T(2,128)S(1)} %collective-permute-done.3.received_ref), channel_id=1, source_target_pairs={{0,1},{1,0},{2,3},{3,2},{4,5},{5,4},{6,7},{7,6},{8,9},{9,8},{10,11... | collective-permute-start | bytes 6152 | tf_op jit(solution)/shard_map/ppermute | solution.py:568
  18.4 0.0 copy-done
  18.4 0.7 %mixing.1.mix_ref = f32[6,144,256]{2,1,0:T(8,128)S(1)} custom-call(bf16[96,256]{1,0:T(8,128)(2,1)S(1)} %get-tuple-element.14.left_ref, f32[16,144]{1,0:T(8,128)S(1)} %copy-done), custom_call_target="tpu_custom_call" | custom-call | tf_op jit(solution)/shard_map/mixing/pallas_call | solution.py:570
  19.1 0.0 collective-permute-done.6.swapped_ref
  19.2 0.2 collective-permute-done.4.exchanged_ref
  19.4 0.0 copy-done.1
  19.4 2.2 %refine.1 = f32[8,1024]{1,0:T(8,128)} custom-call(f32[2,256]{1,0:T(2,128)S(1)} %slice_divide_fusion.own_ref, f32[2,256]{1,0:T(2,128)S(1)} %collective-permute-done.3.received_ref, f32[2,256]{1,0:T(2,128)S(1)} %collective-permute-done.4.exchanged_ref, f32[2,256]{1,0:T(2,128)S(1)} %collective-permute-done.5.far_ref, ...), custom_call_target="tpu_custom_call" | custom-call | tf_op jit(solution)/shard_map/refine/pallas_call | solution.py:578
  (3 shorter events, 0.0 us)
Async XLA Ops:
  0.6 5.5 %copy-start.5 = (f32[16]{0:T(128)S(1)}, f32[16]{0:T(128)}, u32[]{:S(2)}) copy-start(f32[16]{0:T(128)} %head_ref.1) | copy-start | bytes 196
  0.6 5.5 %copy-start.4 = (f32[16]{0:T(128)S(1)}, f32[16]{0:T(128)}, u32[]{:S(2)}) copy-start(f32[16]{0:T(128)} %second_bias_ref.1) | copy-start | bytes 196
  0.7 5.5 %copy-start.3 = (f32[16]{0:T(128)S(1)}, f32[16]{0:T(128)}, u32[]{:S(2)}) copy-start(f32[16]{0:T(128)} %first_bias_ref.1) | copy-start | bytes 196
  0.7 5.5 %copy-start.2 = (f32[16,16]{1,0:T(8,128)S(1)}, f32[16,16]{1,0:T(8,128)}, u32[]{:S(2)}) copy-start(f32[16,16]{1,0:T(8,128)} %feat_ref.1) | copy-start | bytes 3076
  1.5 6.6 %collective-permute-start.1 = (bf16[24,1024]{1,0:T(8,128)(2,1)S(1)}, bf16[24,1024]{1,0:T(8,128)(2,1)S(1)}, u32[]{:S(2)}, u32[]{:S(2)}) collective-permute-start(bf16[24,1024]{1,0:T(8,128)(2,1)S(1)} %pack.1.own_ref), channel_id=1, source_target_pairs={{0,1},{1,0},{2,4},{3,5},{4,2},{5,3},{6,8},{7,9},{8,6},{9,7},{10,12... | collective-permute-start | bytes 147464 | tf_op jit(solution)/shard_map/ppermute | solution.py:519
  2.1 6.1 %collective-permute-start = (bf16[24,1024]{1,0:T(8,128)(2,1)S(1)}, bf16[24,1024]{1,0:T(8,128)(2,1)S(1)}, u32[]{:S(2)}, u32[]{:S(2)}) collective-permute-start(bf16[24,1024]{1,0:T(8,128)(2,1)S(1)} %pack.1.own_ref), channel_id=1, source_target_pairs={{0,2},{1,3},{2,0},{3,1},{4,6},{5,7},{6,4},{7,5},{8,10},{9,11},{10,... | collective-permute-start | bytes 147464 | tf_op jit(solution)/shard_map/ppermute | solution.py:518
  12.2 6.3 %copy-start = (f32[16,144]{1,0:T(8,128)S(1)}, f32[16,144]{1,0:T(8,128)}, u32[]{:S(2)}) copy-start(f32[16,144]{1,0:T(8,128)} %mask_weight_ref.1) | copy-start | bytes 27652
  12.2 1.2 %collective-permute-start.2 = (f32[4,256]{1,0:T(4,128)S(1)}, f32[4,256]{1,0:T(4,128)S(1)}, u32[]{:S(2)}, u32[]{:S(2)}) collective-permute-start(f32[4,256]{1,0:T(4,128)S(1)} %slice.9), channel_id=1, source_target_pairs={{0,1},{1,0},{2,3},{3,2},{4,5},{5,4},{6,7},{7,6},{8,9},{9,8},{10,11... | collective-permute-start | bytes 12296 | tf_op jit(solution)/shard_map/ppermute | solution.py:564
  13.4 5.9 %copy-start.1 = (f32[2,256]{1,0:T(2,128)}, f32[2,256]{1,0:T(2,128)S(1)}, u32[]{:S(2)}) copy-start(f32[2,256]{1,0:T(2,128)S(1)} %slice_divide_fusion.own_ref) | copy-start | bytes 6148
  13.4 3.4 %collective-permute-start.5 = (f32[2,256]{1,0:T(2,128)S(1)}, f32[2,256]{1,0:T(2,128)S(1)}, u32[]{:S(2)}, u32[]{:S(2)}) collective-permute-start(f32[2,256]{1,0:T(2,128)S(1)} %slice_divide_fusion.own_ref), channel_id=1, source_target_pairs={{0,5},{1,3},{2,7},{3,1},{4,9},{5,0},{6,11},{7,2},{8,13},{9,4},{10,... | collective-permute-start | bytes 6152 | tf_op jit(solution)/shard_map/ppermute | solution.py:567
  15.3 2.9 %collective-permute-start.3 = (f32[2,256]{1,0:T(2,128)S(1)}, f32[2,256]{1,0:T(2,128)S(1)}, u32[]{:S(2)}, u32[]{:S(2)}) collective-permute-start(f32[2,256]{1,0:T(2,128)S(1)} %slice_divide_fusion.own_ref), channel_id=1, source_target_pairs={{0,2},{1,0},{2,1},{3,5},{4,6},{5,3},{6,4},{7,9},{8,10},{9,7},{10,8... | collective-permute-start | bytes 6152 | tf_op jit(solution)/shard_map/ppermute | solution.py:566
  16.9 2.3 %collective-permute-start.6 = (f32[2,256]{1,0:T(2,128)S(1)}, f32[2,256]{1,0:T(2,128)S(1)}, u32[]{:S(2)}, u32[]{:S(2)}) collective-permute-start(f32[2,256]{1,0:T(2,128)S(1)} %collective-permute-done.5.far_ref), channel_id=1, source_target_pairs={{0,1},{1,0},{2,3},{3,2},{4,5},{5,4},{6,7},{7,6},{8,9},{9,8},{10,11... | collective-permute-start | bytes 6152 | tf_op jit(solution)/shard_map/ppermute | solution.py:569
  18.2 1.2 %collective-permute-start.4 = (f32[2,256]{1,0:T(2,128)S(1)}, f32[2,256]{1,0:T(2,128)S(1)}, u32[]{:S(2)}, u32[]{:S(2)}) collective-permute-start(f32[2,256]{1,0:T(2,128)S(1)} %collective-permute-done.3.received_ref), channel_id=1, source_target_pairs={{0,1},{1,0},{2,3},{3,2},{4,5},{5,4},{6,7},{7,6},{8,9},{9,8},{10,11... | collective-permute-start | bytes 6152 | tf_op jit(solution)/shard_map/ppermute | solution.py:568

commit v5 on v4

--- a/solution.py
+++ b/solution.py
@@ -132,8 +132,9 @@
 
 def join_taps(taps):
     size = taps.shape[0] // 3
-    sides = shift_right(taps[:size].astype(bf16)) + shift_left(taps[2 * size :].astype(bf16))
-    return taps[size : 2 * size] + sides.astype(f32)
+    before = shift_right(taps[:size].astype(bf16)).astype(f32)
+    after = shift_left(taps[2 * size :].astype(bf16)).astype(f32)
+    return taps[size : 2 * size] + (before + after)
 
 
 def score_kernel(

time: 21.8 us -> 22 us (level)
  Pallas kernels: 9.77 us -> 10 us
    pallas_call x1, Pallas kernels: 3.99 us -> 4.23 us  [local(): pl.pallas_call(functools.partial(score_kernel, pix_size=pix_size, disp_si...]
  transfers between devices with their start and end apart: 7 -> 7, of which waited for: 3 -> 3; matrix products, arithmetic and copies ran while one was open for 0% -> 0% of each run, Pallas kernels for 13% -> 12%
where the time goes in v5:
time: 22 us; the launch traced here: 21.8 us
  Pallas kernels  10 us (45%)
  starting transfers between devices  8.33 us (38%)
  waiting for transfers between devices  2.68 us (12%)
  between operations  0.76 us (3%)
    pallas_call x1, Pallas kernels, local(): pl.pallas_call(functools.partial(score_kernel, pix_size=pix_size, disp_si...  4.23 us
    ppermute x1, starting transfers between devices, local(): from_pair = lax.ppermute(packed, both, pairs)  4.02 us
    pallas_call x1, Pallas kernels, local(): pl.pallas_call(functools.partial(refine_kernel, pix_size=pix_size), out_s...  2.22 us
    pallas_call x1, Pallas kernels, local(): pl.pallas_call(prepare_kernel, out_shape=(jax.ShapeDtypeStruct((3 * group...  2.02 us
    ppermute x1, starting transfers between devices, local(): far_rows = lax.ppermute(coarse, both, far)  1.82 us
    ppermute x1, starting transfers between devices, local(): received = lax.ppermute(coarse, both, neighbours)  1.61 us
    ppermute x1, waiting for transfers between devices, local(): received = lax.ppermute(coarse, both, neighbours)  1.3 us
    ppermute x1, waiting for transfers between devices, local(): summed = total + lax.ppermute(total, 'disp', swap)  1.15 us
  transfers between devices with their start and end apart: 7, of which 3 were waited for; matrix products, arithmetic and copies ran while one was open for 0% of the time, Pallas kernels for 12%

profile of v5, /device:TPU:0, one launch (start us, length us, event | category | flops | bytes accessed | tf_op | source)
XLA Modules:
  0.0 21.8 jit_solution(3422759877472001933)
XLA Ops:
  0.6 0.0 copy-start.5
  0.6 0.0 copy-start.4
  0.7 0.0 copy-start.3
  0.7 0.0 copy-start.2
  0.7 0.8 %pack.1.own_ref = bf16[24,1024]{1,0:T(8,128)(2,1)S(1)} custom-call(s32[8,1024]{1,0:T(8,128)} %left_ref.1, s32[8,1024]{1,0:T(8,128)} %right_ref.1, f32[8,1024]{1,0:T(8,128)} %conf_ref.1), custom_call_target="tpu_custom_call" | custom-call | tf_op jit(solution)/shard_map/pack/pallas_call | solution.py:506
  1.5 0.6 %collective-permute-start.1 = (bf16[24,1024]{1,0:T(8,128)(2,1)S(1)}, bf16[24,1024]{1,0:T(8,128)(2,1)S(1)}, u32[]{:S(2)}, u32[]{:S(2)}) collective-permute-start(bf16[24,1024]{1,0:T(8,128)(2,1)S(1)} %pack.1.own_ref), channel_id=1, source_target_pairs={{0,1},{1,0},{2,4},{3,5},{4,2},{5,3},{6,8},{7,9},{8,6},{9,7},{10,12... | collective-permute-start | bytes 147464 | tf_op jit(solution)/shard_map/ppermute | solution.py:520
  2.1 4.0 %collective-permute-start = (bf16[24,1024]{1,0:T(8,128)(2,1)S(1)}, bf16[24,1024]{1,0:T(8,128)(2,1)S(1)}, u32[]{:S(2)}, u32[]{:S(2)}) collective-permute-start(bf16[24,1024]{1,0:T(8,128)(2,1)S(1)} %pack.1.own_ref), channel_id=1, source_target_pairs={{0,2},{1,3},{2,0},{3,1},{4,6},{5,7},{6,4},{7,5},{8,10},{9,11},{10,... | collective-permute-start | bytes 147464 | tf_op jit(solution)/shard_map/ppermute | solution.py:519
  6.1 0.0 copy-done.5
  6.1 0.0 copy-done.4
  6.1 0.0 copy-done.3
  6.1 0.0 copy-done.2
  6.1 2.0 %prepare.1 = (bf16[576,192]{1,0:T(8,128)(2,1)S(1)}, bf16[192,256]{1,0:T(8,128)(2,1)S(1)}, bf16[192,256]{1,0:T(8,128)(2,1)S(1)}, f32[3,64,256]{2,1,0:T(8,128)S(1)}) custom-call(f32[16,16]{1,0:T(8,128)S(1)} %copy-done.2, bf16[3,3,3,16,16]{4,3,2,1,0:T(8,128)(2,1)} %first_weight_ref.1, f32[16]{0:T(128)S(1)} %copy-done.3, ...), custom_call_target="tpu_custom_call" | custom-call | tf_op jit(solution)/shard_map/prepare/pallas_call | solution.py:523
  8.1 0.0 collective-permute-done.1.exchanged_ref
  8.2 0.0 collective-permute-done.received_ref
  8.2 4.2 %score.1 = (f32[8,256]{1,0:T(8,128)S(1)}, bf16[96,256]{1,0:T(8,128)(2,1)S(1)}, f32[24,1024]{1,0:T(8,128)S(1)}) custom-call(bf16[24,1024]{1,0:T(8,128)(2,1)S(1)} %pack.1.own_ref, bf16[24,1024]{1,0:T(8,128)(2,1)S(1)} %collective-permute-done.received_ref, bf16[24,1024]{1,0:T(8,128)(2,1)S(1)} %collective-permute-done.1.exchanged_ref, ...), custom_call_target="tpu_custom_call" | custom-call | tf_op jit(solution)/shard_map/score/pallas_call | solution.py:547
  12.4 0.0 copy-start
  12.4 0.1 collective-permute-start.2
  12.5 1.2 %collective-permute-done.2 = f32[4,256]{1,0:T(4,128)S(1)} collective-permute-done((f32[4,256]{1,0:T(4,128)S(1)}, f32[4,256]{1,0:T(4,128)S(1)}, u32[]{:S(2)}, u32[]{:S(2)}) %collective-permute-start.2) | collective-permute-done | bytes 4128 | tf_op jit(solution)/shard_map/ppermute | solution.py:565
  13.7 0.0 copy-start.1
  13.7 1.8 %collective-permute-start.5 = (f32[2,256]{1,0:T(2,128)S(1)}, f32[2,256]{1,0:T(2,128)S(1)}, u32[]{:S(2)}, u32[]{:S(2)}) collective-permute-start(f32[2,256]{1,0:T(2,128)S(1)} %slice_divide_fusion.own_ref), channel_id=1, source_target_pairs={{0,5},{1,3},{2,7},{3,1},{4,9},{5,0},{6,11},{7,2},{8,13},{9,4},{10,... | collective-permute-start | bytes 6152 | tf_op jit(solution)/shard_map/ppermute | solution.py:568
  15.5 1.6 %collective-permute-start.3 = (f32[2,256]{1,0:T(2,128)S(1)}, f32[2,256]{1,0:T(2,128)S(1)}, u32[]{:S(2)}, u32[]{:S(2)}) collective-permute-start(f32[2,256]{1,0:T(2,128)S(1)} %slice_divide_fusion.own_ref), channel_id=1, source_target_pairs={{0,2},{1,0},{2,1},{3,5},{4,6},{5,3},{6,4},{7,9},{8,10},{9,7},{10,8... | collective-permute-start | bytes 6152 | tf_op jit(solution)/shard_map/ppermute | solution.py:567
  17.1 0.0 collective-permute-done.5.far_ref
  17.1 0.0 collective-permute-start.6
  17.1 1.3 %collective-permute-done.3.received_ref = f32[2,256]{1,0:T(2,128)S(1)} collective-permute-done((f32[2,256]{1,0:T(2,128)S(1)}, f32[2,256]{1,0:T(2,128)S(1)}, u32[]{:S(2)}, u32[]{:S(2)}) %collective-permute-start.3) | collective-permute-done | bytes 2080 | tf_op jit(solution)/shard_map/ppermute | solution.py:567
  18.4 0.2 %collective-permute-start.4 = (f32[2,256]{1,0:T(2,128)S(1)}, f32[2,256]{1,0:T(2,128)S(1)}, u32[]{:S(2)}, u32[]{:S(2)}) collective-permute-start(f32[2,256]{1,0:T(2,128)S(1)} %collective-permute-done.3.received_ref), channel_id=1, source_target_pairs={{0,1},{1,0},{2,3},{3,2},{4,5},{5,4},{6,7},{7,6},{8,9},{9,8},{10,11... | collective-permute-start | bytes 6152 | tf_op jit(solution)/shard_map/ppermute | solution.py:569
  18.7 0.0 copy-done
  18.7 0.7 %mixing.1.mix_ref = f32[6,144,256]{2,1,0:T(8,128)S(1)} custom-call(bf16[96,256]{1,0:T(8,128)(2,1)S(1)} %get-tuple-element.14.left_ref, f32[16,144]{1,0:T(8,128)S(1)} %copy-done), custom_call_target="tpu_custom_call" | custom-call | tf_op jit(solution)/shard_map/mixing/pallas_call | solution.py:571
  19.4 0.0 collective-permute-done.6.swapped_ref
  19.4 0.2 collective-permute-done.4.exchanged_ref
  19.6 0.0 copy-done.1
  19.6 2.2 %refine.1 = f32[8,1024]{1,0:T(8,128)} custom-call(f32[2,256]{1,0:T(2,128)S(1)} %slice_divide_fusion.own_ref, f32[2,256]{1,0:T(2,128)S(1)} %collective-permute-done.3.received_ref, f32[2,256]{1,0:T(2,128)S(1)} %collective-permute-done.4.exchanged_ref, f32[2,256]{1,0:T(2,128)S(1)} %collective-permute-done.5.far_ref, ...), custom_call_target="tpu_custom_call" | custom-call | tf_op jit(solution)/shard_map/refine/pallas_call | solution.py:579
  (3 shorter events, 0.0 us)
Async XLA Ops:
  0.6 5.5 %copy-start.5 = (f32[16]{0:T(128)S(1)}, f32[16]{0:T(128)}, u32[]{:S(2)}) copy-start(f32[16]{0:T(128)} %head_ref.1) | copy-start | bytes 196
  0.6 5.5 %copy-start.4 = (f32[16]{0:T(128)S(1)}, f32[16]{0:T(128)}, u32[]{:S(2)}) copy-start(f32[16]{0:T(128)} %second_bias_ref.1) | copy-start | bytes 196
  0.7 5.5 %copy-start.3 = (f32[16]{0:T(128)S(1)}, f32[16]{0:T(128)}, u32[]{:S(2)}) copy-start(f32[16]{0:T(128)} %first_bias_ref.1) | copy-start | bytes 196
  0.7 5.5 %copy-start.2 = (f32[16,16]{1,0:T(8,128)S(1)}, f32[16,16]{1,0:T(8,128)}, u32[]{:S(2)}) copy-start(f32[16,16]{1,0:T(8,128)} %feat_ref.1) | copy-start | bytes 3076
  1.5 6.6 %collective-permute-start.1 = (bf16[24,1024]{1,0:T(8,128)(2,1)S(1)}, bf16[24,1024]{1,0:T(8,128)(2,1)S(1)}, u32[]{:S(2)}, u32[]{:S(2)}) collective-permute-start(bf16[24,1024]{1,0:T(8,128)(2,1)S(1)} %pack.1.own_ref), channel_id=1, source_target_pairs={{0,1},{1,0},{2,4},{3,5},{4,2},{5,3},{6,8},{7,9},{8,6},{9,7},{10,12... | collective-permute-start | bytes 147464 | tf_op jit(solution)/shard_map/ppermute | solution.py:520
  2.1 6.1 %collective-permute-start = (bf16[24,1024]{1,0:T(8,128)(2,1)S(1)}, bf16[24,1024]{1,0:T(8,128)(2,1)S(1)}, u32[]{:S(2)}, u32[]{:S(2)}) collective-permute-start(bf16[24,1024]{1,0:T(8,128)(2,1)S(1)} %pack.1.own_ref), channel_id=1, source_target_pairs={{0,2},{1,3},{2,0},{3,1},{4,6},{5,7},{6,4},{7,5},{8,10},{9,11},{10,... | collective-permute-start | bytes 147464 | tf_op jit(solution)/shard_map/ppermute | solution.py:519
  12.4 6.3 %copy-start = (f32[16,144]{1,0:T(8,128)S(1)}, f32[16,144]{1,0:T(8,128)}, u32[]{:S(2)}) copy-start(f32[16,144]{1,0:T(8,128)} %mask_weight_ref.1) | copy-start | bytes 27652
  12.4 1.2 %collective-permute-start.2 = (f32[4,256]{1,0:T(4,128)S(1)}, f32[4,256]{1,0:T(4,128)S(1)}, u32[]{:S(2)}, u32[]{:S(2)}) collective-permute-start(f32[4,256]{1,0:T(4,128)S(1)} %slice.9), channel_id=1, source_target_pairs={{0,1},{1,0},{2,3},{3,2},{4,5},{5,4},{6,7},{7,6},{8,9},{9,8},{10,11... | collective-permute-start | bytes 12296 | tf_op jit(solution)/shard_map/ppermute | solution.py:565
  13.7 5.9 %copy-start.1 = (f32[2,256]{1,0:T(2,128)}, f32[2,256]{1,0:T(2,128)S(1)}, u32[]{:S(2)}) copy-start(f32[2,256]{1,0:T(2,128)S(1)} %slice_divide_fusion.own_ref) | copy-start | bytes 6148
  13.7 3.4 %collective-permute-start.5 = (f32[2,256]{1,0:T(2,128)S(1)}, f32[2,256]{1,0:T(2,128)S(1)}, u32[]{:S(2)}, u32[]{:S(2)}) collective-permute-start(f32[2,256]{1,0:T(2,128)S(1)} %slice_divide_fusion.own_ref), channel_id=1, source_target_pairs={{0,5},{1,3},{2,7},{3,1},{4,9},{5,0},{6,11},{7,2},{8,13},{9,4},{10,... | collective-permute-start | bytes 6152 | tf_op jit(solution)/shard_map/ppermute | solution.py:568
  15.5 2.9 %collective-permute-start.3 = (f32[2,256]{1,0:T(2,128)S(1)}, f32[2,256]{1,0:T(2,128)S(1)}, u32[]{:S(2)}, u32[]{:S(2)}) collective-permute-start(f32[2,256]{1,0:T(2,128)S(1)} %slice_divide_fusion.own_ref), channel_id=1, source_target_pairs={{0,2},{1,0},{2,1},{3,5},{4,6},{5,3},{6,4},{7,9},{8,10},{9,7},{10,8... | collective-permute-start | bytes 6152 | tf_op jit(solution)/shard_map/ppermute | solution.py:567
  17.1 2.3 %collective-permute-start.6 = (f32[2,256]{1,0:T(2,128)S(1)}, f32[2,256]{1,0:T(2,128)S(1)}, u32[]{:S(2)}, u32[]{:S(2)}) collective-permute-start(f32[2,256]{1,0:T(2,128)S(1)} %collective-permute-done.5.far_ref), channel_id=1, source_target_pairs={{0,1},{1,0},{2,3},{3,2},{4,5},{5,4},{6,7},{7,6},{8,9},{9,8},{10,11... | collective-permute-start | bytes 6152 | tf_op jit(solution)/shard_map/ppermute | solution.py:570
  18.4 1.2 %collective-permute-start.4 = (f32[2,256]{1,0:T(2,128)S(1)}, f32[2,256]{1,0:T(2,128)S(1)}, u32[]{:S(2)}, u32[]{:S(2)}) collective-permute-start(f32[2,256]{1,0:T(2,128)S(1)} %collective-permute-done.3.received_ref), channel_id=1, source_target_pairs={{0,1},{1,0},{2,3},{3,2},{4,5},{5,4},{6,7},{7,6},{8,9},{9,8},{10,11... | collective-permute-start | bytes 6152 | tf_op jit(solution)/shard_map/ppermute | solution.py:569

commit v6 on v5

--- a/solution.py
+++ b/solution.py
@@ -421,7 +421,7 @@
 ):
     copies = [
         pltpu.make_async_copy(ref, weights.at[n], sems.at[n])
-        for n, ref in enumerate((first_weight_ref, second_weight_ref))
+        for n, ref in enumerate((second_weight_ref,))
     ]
     for copy in copies:
         copy.start()
@@ -444,10 +444,10 @@
     const_ref[1] = jnp.broadcast_to(column(second_bias_ref[...], index // 4), shape)
     const_ref[2] = jnp.broadcast_to(column(head_ref[...], index // 4), shape)
 
-    for copy in copies:
-        copy.wait()
     taps = weights.shape[1] ** 3 * CH
-    flat = [transposed(weights[n].reshape(taps, CH)) for n in range(2)]
+    flat = [transposed(first_weight_ref[...].reshape(taps, CH))]
+    copies[0].wait()
+    flat.append(transposed(weights[0].reshape(taps, CH)))
     flat = jnp.concatenate(flat, 0)
     source = lax.broadcasted_iota(jnp.int32, (taps, 256), 0)
     lane = lax.broadcasted_iota(jnp.int32, (1, 256), 1)
@@ -528,17 +528,17 @@
             jax.ShapeDtypeStruct((192, 256), bf16),
             jax.ShapeDtypeStruct((3, 64, cols), f32),
         ),
-        in_specs=[vmem, hbm, vmem, hbm, vmem, vmem],
+        in_specs=[vmem, vmem, vmem, hbm, vmem, vmem],
         out_specs=(vmem,) * 4,
         scratch_shapes=[
-            pltpu.VMEM((2,) + first_weight.shape, bf16),
-            pltpu.SemaphoreType.DMA((2,)),
+            pltpu.VMEM((1,) + first_weight.shape, bf16),
+            pltpu.SemaphoreType.DMA((1,)),
         ],
         compiler_params=pltpu.CompilerParams(vmem_limit_bytes=8 * 2**20),
         name="prepare",
     )(
         feat_weight,
-        in_hbm(first_weight),
+        first_weight,
         first_bias,
         in_hbm(second_weight),
         second_bias,

time: 22 us -> 22 us (level)
  transfers between devices with their start and end apart: 7 -> 7, of which waited for: 3 -> 4; matrix products, arithmetic and copies ran while one was open for 0% -> 0% of each run, Pallas kernels for 12% -> 12%
where the time goes in v6:
time: 22 us; the launch traced here: 21.9 us
  Pallas kernels  9.93 us (45%)
  starting transfers between devices  8.33 us (38%)
  waiting for transfers between devices  2.78 us (13%)
  between operations  0.77 us (4%)
    pallas_call x1, Pallas kernels, local(): pl.pallas_call(functools.partial(score_kernel, pix_size=pix_size, disp_si...  4.23 us
    ppermute x1, starting transfers between devices, local(): from_pair = lax.ppermute(packed, both, pairs)  4.02 us
    pallas_call x1, Pallas kernels, local(): pl.pallas_call(functools.partial(refine_kernel, pix_size=pix_size), out_s...  2.22 us
    pallas_call x1, Pallas kernels, local(): pl.pallas_call(prepare_kernel, out_shape=(jax.ShapeDtypeStruct((3 * group...  1.91 us
    ppermute x1, starting transfers between devices, local(): far_rows = lax.ppermute(coarse, both, far)  1.82 us
    ppermute x1, starting transfers between devices, local(): received = lax.ppermute(coarse, both, neighbours)  1.61 us
    ppermute x1, waiting for transfers between devices, local(): received = lax.ppermute(coarse, both, neighbours)  1.3 us
    ppermute x1, waiting for transfers between devices, local(): summed = total + lax.ppermute(total, 'disp', swap)  1.15 us
  transfers between devices with their start and end apart: 7, of which 4 were waited for; matrix products, arithmetic and copies ran while one was open for 0% of the time, Pallas kernels for 12%

profile of v6, /device:TPU:0, one launch (start us, length us, event | category | flops | bytes accessed | tf_op | source)
XLA Modules:
  0.0 21.9 jit_solution(17941604427693896623)
XLA Ops:
  0.6 0.0 copy-start.6
  0.6 0.0 copy-start.5
  0.7 0.0 copy-start.4
  0.7 0.0 copy-start
  0.7 0.0 copy-start.3
  0.7 0.9 %pack.1.own_ref = bf16[24,1024]{1,0:T(8,128)(2,1)S(1)} custom-call(s32[8,1024]{1,0:T(8,128)} %left_ref.1, s32[8,1024]{1,0:T(8,128)} %right_ref.1, f32[8,1024]{1,0:T(8,128)} %conf_ref.1), custom_call_target="tpu_custom_call" | custom-call | tf_op jit(solution)/shard_map/pack/pallas_call | solution.py:506
  1.6 0.6 %collective-permute-start.1 = (bf16[24,1024]{1,0:T(8,128)(2,1)S(1)}, bf16[24,1024]{1,0:T(8,128)(2,1)S(1)}, u32[]{:S(2)}, u32[]{:S(2)}) collective-permute-start(bf16[24,1024]{1,0:T(8,128)(2,1)S(1)} %pack.1.own_ref), channel_id=1, source_target_pairs={{0,1},{1,0},{2,4},{3,5},{4,2},{5,3},{6,8},{7,9},{8,6},{9,7},{10,12... | collective-permute-start | bytes 147464 | tf_op jit(solution)/shard_map/ppermute | solution.py:520
  2.1 4.0 %collective-permute-start = (bf16[24,1024]{1,0:T(8,128)(2,1)S(1)}, bf16[24,1024]{1,0:T(8,128)(2,1)S(1)}, u32[]{:S(2)}, u32[]{:S(2)}) collective-permute-start(bf16[24,1024]{1,0:T(8,128)(2,1)S(1)} %pack.1.own_ref), channel_id=1, source_target_pairs={{0,2},{1,3},{2,0},{3,1},{4,6},{5,7},{6,4},{7,5},{8,10},{9,11},{10,... | collective-permute-start | bytes 147464 | tf_op jit(solution)/shard_map/ppermute | solution.py:519
  6.1 0.0 copy-done.6
  6.1 0.0 copy-done.5
  6.1 0.0 copy-done.4
  6.1 0.0 copy-done
  6.2 0.0 copy-done.3
  6.2 1.9 %prepare.1 = (bf16[576,192]{1,0:T(8,128)(2,1)S(1)}, bf16[192,256]{1,0:T(8,128)(2,1)S(1)}, bf16[192,256]{1,0:T(8,128)(2,1)S(1)}, f32[3,64,256]{2,1,0:T(8,128)S(1)}) custom-call(f32[16,16]{1,0:T(8,128)S(1)} %copy-done.3, bf16[3,3,3,16,16]{4,3,2,1,0:T(8,128)(2,1)S(1)} %copy-done, f32[16]{0:T(128)S(1)} %copy-done.4, ...), custom_call_target="tpu_custom_call" | custom-call | tf_op jit(solution)/shard_map/prepare/pallas_call | solution.py:523
  8.1 0.0 collective-permute-done.1.exchanged_ref
  8.1 0.1 collective-permute-done.received_ref
  8.2 4.2 %score.1 = (f32[8,256]{1,0:T(8,128)S(1)}, bf16[96,256]{1,0:T(8,128)(2,1)S(1)}, f32[24,1024]{1,0:T(8,128)S(1)}) custom-call(bf16[24,1024]{1,0:T(8,128)(2,1)S(1)} %pack.1.own_ref, bf16[24,1024]{1,0:T(8,128)(2,1)S(1)} %collective-permute-done.received_ref, bf16[24,1024]{1,0:T(8,128)(2,1)S(1)} %collective-permute-done.1.exchanged_ref, ...), custom_call_target="tpu_custom_call" | custom-call | tf_op jit(solution)/shard_map/score/pallas_call | solution.py:547
  12.4 0.0 copy-start.1
  12.5 0.1 collective-permute-start.2
  12.5 1.2 %collective-permute-done.2 = f32[4,256]{1,0:T(4,128)S(1)} collective-permute-done((f32[4,256]{1,0:T(4,128)S(1)}, f32[4,256]{1,0:T(4,128)S(1)}, u32[]{:S(2)}, u32[]{:S(2)}) %collective-permute-start.2) | collective-permute-done | bytes 4128 | tf_op jit(solution)/shard_map/ppermute | solution.py:565
  13.7 0.0 copy-start.2
  13.7 1.8 %collective-permute-start.5 = (f32[2,256]{1,0:T(2,128)S(1)}, f32[2,256]{1,0:T(2,128)S(1)}, u32[]{:S(2)}, u32[]{:S(2)}) collective-permute-start(f32[2,256]{1,0:T(2,128)S(1)} %slice_divide_fusion.own_ref), channel_id=1, source_target_pairs={{0,5},{1,3},{2,7},{3,1},{4,9},{5,0},{6,11},{7,2},{8,13},{9,4},{10,... | collective-permute-start | bytes 6152 | tf_op jit(solution)/shard_map/ppermute | solution.py:568
  15.5 1.6 %collective-permute-start.3 = (f32[2,256]{1,0:T(2,128)S(1)}, f32[2,256]{1,0:T(2,128)S(1)}, u32[]{:S(2)}, u32[]{:S(2)}) collective-permute-start(f32[2,256]{1,0:T(2,128)S(1)} %slice_divide_fusion.own_ref), channel_id=1, source_target_pairs={{0,2},{1,0},{2,1},{3,5},{4,6},{5,3},{6,4},{7,9},{8,10},{9,7},{10,8... | collective-permute-start | bytes 6152 | tf_op jit(solution)/shard_map/ppermute | solution.py:567
  17.2 0.0 collective-permute-done.5.far_ref
  17.2 0.0 collective-permute-start.6
  17.2 1.3 %collective-permute-done.3.received_ref = f32[2,256]{1,0:T(2,128)S(1)} collective-permute-done((f32[2,256]{1,0:T(2,128)S(1)}, f32[2,256]{1,0:T(2,128)S(1)}, u32[]{:S(2)}, u32[]{:S(2)}) %collective-permute-start.3) | collective-permute-done | bytes 2080 | tf_op jit(solution)/shard_map/ppermute | solution.py:567
  18.5 0.2 %collective-permute-start.4 = (f32[2,256]{1,0:T(2,128)S(1)}, f32[2,256]{1,0:T(2,128)S(1)}, u32[]{:S(2)}, u32[]{:S(2)}) collective-permute-start(f32[2,256]{1,0:T(2,128)S(1)} %collective-permute-done.3.received_ref), channel_id=1, source_target_pairs={{0,1},{1,0},{2,3},{3,2},{4,5},{5,4},{6,7},{7,6},{8,9},{9,8},{10,11... | collective-permute-start | bytes 6152 | tf_op jit(solution)/shard_map/ppermute | solution.py:569
  18.7 0.0 copy-done.1
  18.7 0.7 %mixing.1.mix_ref = f32[6,144,256]{2,1,0:T(8,128)S(1)} custom-call(bf16[96,256]{1,0:T(8,128)(2,1)S(1)} %get-tuple-element.14.left_ref, f32[16,144]{1,0:T(8,128)S(1)} %copy-done.1), custom_call_target="tpu_custom_call" | custom-call | tf_op jit(solution)/shard_map/mixing/pallas_call | solution.py:571
  19.4 0.0 collective-permute-done.6.swapped_ref
  19.4 0.2 collective-permute-done.4.exchanged_ref
  19.6 2.2 %refine.1 = f32[8,1024]{1,0:T(8,128)} custom-call(f32[2,256]{1,0:T(2,128)S(1)} %slice_divide_fusion.own_ref, f32[2,256]{1,0:T(2,128)S(1)} %collective-permute-done.3.received_ref, f32[2,256]{1,0:T(2,128)S(1)} %collective-permute-done.4.exchanged_ref, f32[2,256]{1,0:T(2,128)S(1)} %collective-permute-done.5.far_ref, ...), custom_call_target="tpu_custom_call" | custom-call | tf_op jit(solution)/shard_map/refine/pallas_call | solution.py:579
  (4 shorter events, 0.0 us)
Async XLA Ops:
  0.6 5.5 %copy-start.6 = (f32[16]{0:T(128)S(1)}, f32[16]{0:T(128)}, u32[]{:S(2)}) copy-start(f32[16]{0:T(128)} %head_ref.1) | copy-start | bytes 196
  0.6 5.5 %copy-start.5 = (f32[16]{0:T(128)S(1)}, f32[16]{0:T(128)}, u32[]{:S(2)}) copy-start(f32[16]{0:T(128)} %second_bias_ref.1) | copy-start | bytes 196
  0.7 5.5 %copy-start.4 = (f32[16]{0:T(128)S(1)}, f32[16]{0:T(128)}, u32[]{:S(2)}) copy-start(f32[16]{0:T(128)} %first_bias_ref.1) | copy-start | bytes 196
  0.7 5.5 %copy-start = (bf16[3,3,3,16,16]{4,3,2,1,0:T(8,128)(2,1)S(1)}, bf16[3,3,3,16,16]{4,3,2,1,0:T(8,128)(2,1)}, u32[]{:S(2)}) copy-start(bf16[3,3,3,16,16]{4,3,2,1,0:T(8,128)(2,1)} %first_weight_ref.1) | copy-start | bytes 41476
  0.7 5.5 %copy-start.3 = (f32[16,16]{1,0:T(8,128)S(1)}, f32[16,16]{1,0:T(8,128)}, u32[]{:S(2)}) copy-start(f32[16,16]{1,0:T(8,128)} %feat_ref.1) | copy-start | bytes 3076
  1.6 6.5 %collective-permute-start.1 = (bf16[24,1024]{1,0:T(8,128)(2,1)S(1)}, bf16[24,1024]{1,0:T(8,128)(2,1)S(1)}, u32[]{:S(2)}, u32[]{:S(2)}) collective-permute-start(bf16[24,1024]{1,0:T(8,128)(2,1)S(1)} %pack.1.own_ref), channel_id=1, source_target_pairs={{0,1},{1,0},{2,4},{3,5},{4,2},{5,3},{6,8},{7,9},{8,6},{9,7},{10,12... | collective-permute-start | bytes 147464 | tf_op jit(solution)/shard_map/ppermute | solution.py:520
  2.1 6.1 %collective-permute-start = (bf16[24,1024]{1,0:T(8,128)(2,1)S(1)}, bf16[24,1024]{1,0:T(8,128)(2,1)S(1)}, u32[]{:S(2)}, u32[]{:S(2)}) collective-permute-start(bf16[24,1024]{1,0:T(8,128)(2,1)S(1)} %pack.1.own_ref), channel_id=1, source_target_pairs={{0,2},{1,3},{2,0},{3,1},{4,6},{5,7},{6,4},{7,5},{8,10},{9,11},{10,... | collective-permute-start | bytes 147464 | tf_op jit(solution)/shard_map/ppermute | solution.py:519
  12.4 6.3 %copy-start.1 = (f32[16,144]{1,0:T(8,128)S(1)}, f32[16,144]{1,0:T(8,128)}, u32[]{:S(2)}) copy-start(f32[16,144]{1,0:T(8,128)} %mask_weight_ref.1) | copy-start | bytes 27652
  12.5 1.2 %collective-permute-start.2 = (f32[4,256]{1,0:T(4,128)S(1)}, f32[4,256]{1,0:T(4,128)S(1)}, u32[]{:S(2)}, u32[]{:S(2)}) collective-permute-start(f32[4,256]{1,0:T(4,128)S(1)} %slice.9), channel_id=1, source_target_pairs={{0,1},{1,0},{2,3},{3,2},{4,5},{5,4},{6,7},{7,6},{8,9},{9,8},{10,11... | collective-permute-start | bytes 12296 | tf_op jit(solution)/shard_map/ppermute | solution.py:565
  13.7 5.9 %copy-start.2 = (f32[2,256]{1,0:T(2,128)}, f32[2,256]{1,0:T(2,128)S(1)}, u32[]{:S(2)}) copy-start(f32[2,256]{1,0:T(2,128)S(1)} %slice_divide_fusion.own_ref) | copy-start | bytes 6148
  13.7 3.4 %collective-permute-start.5 = (f32[2,256]{1,0:T(2,128)S(1)}, f32[2,256]{1,0:T(2,128)S(1)}, u32[]{:S(2)}, u32[]{:S(2)}) collective-permute-start(f32[2,256]{1,0:T(2,128)S(1)} %slice_divide_fusion.own_ref), channel_id=1, source_target_pairs={{0,5},{1,3},{2,7},{3,1},{4,9},{5,0},{6,11},{7,2},{8,13},{9,4},{10,... | collective-permute-start | bytes 6152 | tf_op jit(solution)/shard_map/ppermute | solution.py:568
  15.5 2.9 %collective-permute-start.3 = (f32[2,256]{1,0:T(2,128)S(1)}, f32[2,256]{1,0:T(2,128)S(1)}, u32[]{:S(2)}, u32[]{:S(2)}) collective-permute-start(f32[2,256]{1,0:T(2,128)S(1)} %slice_divide_fusion.own_ref), channel_id=1, source_target_pairs={{0,2},{1,0},{2,1},{3,5},{4,6},{5,3},{6,4},{7,9},{8,10},{9,7},{10,8... | collective-permute-start | bytes 6152 | tf_op jit(solution)/shard_map/ppermute | solution.py:567
  17.2 2.3 %collective-permute-start.6 = (f32[2,256]{1,0:T(2,128)S(1)}, f32[2,256]{1,0:T(2,128)S(1)}, u32[]{:S(2)}, u32[]{:S(2)}) collective-permute-start(f32[2,256]{1,0:T(2,128)S(1)} %collective-permute-done.5.far_ref), channel_id=1, source_target_pairs={{0,1},{1,0},{2,3},{3,2},{4,5},{5,4},{6,7},{7,6},{8,9},{9,8},{10,11... | collective-permute-start | bytes 6152 | tf_op jit(solution)/shard_map/ppermute | solution.py:570
  18.5 1.2 %collective-permute-start.4 = (f32[2,256]{1,0:T(2,128)S(1)}, f32[2,256]{1,0:T(2,128)S(1)}, u32[]{:S(2)}, u32[]{:S(2)}) collective-permute-start(f32[2,256]{1,0:T(2,128)S(1)} %collective-permute-done.3.received_ref), channel_id=1, source_target_pairs={{0,1},{1,0},{2,3},{3,2},{4,5},{5,4},{6,7},{7,6},{8,9},{9,8},{10,11... | collective-permute-start | bytes 6152 | tf_op jit(solution)/shard_map/ppermute | solution.py:569
